TPU v7x, 32 devices: a whole 2x2x4 slice. The times are simulated.
32 devices in a mesh: rep: 2 (over y), lat: 16 (over z, x, core).
Axes of the slice: x: 2, y: 2, z: 4, core: 2. Of those that a mesh axis runs over, the one named last changes fastest.
Arguments:
- block_input: bfloat16 [32, 180, 768], P(('rep', 'lat')), parts along dimension 0, may hold values from -6 to 6
- cotangent: bfloat16 [32, 180, 768], P(('rep', 'lat')), parts along dimension 0, may hold values from -8 to 8
- first_gain: float32 [768], replicated, may hold values from 0.5 to 1.5
- first_shift: float32 [768], replicated, may hold values from -1.25 to 1.25
- inner_weight: float32 [2, 768, 96], replicated, may hold values from -0.4375 to 0.4375
- inner_bias: float32 [2, 768], replicated, may hold values from -3 to 3
- outer_weight: float32 [2, 768, 96], replicated, may hold values from -0.4375 to 0.4375
- outer_bias: float32 [2, 768], replicated, may hold values from -0.125 to 0.125
- second_gain: float32 [768], replicated, may hold values from 0.5 to 1.5
- second_shift: float32 [768], replicated, may hold values from -1.25 to 1.25
- up_weight: bfloat16 [3072, 768], replicated, may hold values from -0.21875 to 0.21875
- up_bias: float32 [3072], replicated, may hold values from -3 to 3
- down_weight: bfloat16 [768, 3072], replicated, may hold values from -0.109375 to 0.109375
- down_bias: float32 [768], replicated, may hold values from -1.75 to 1.75
Outputs:
- block_output: bfloat16 [32, 180, 768], P(('rep', 'lat')), parts along dimension 0
- input_grad: bfloat16 [32, 180, 768], P(('rep', 'lat')), parts along dimension 0
- up_grad: float32 [6144, 768], P(('rep', 'lat')), parts along dimension 0
- down_grad: float32 [1536, 3072], P(('rep', 'lat')), parts along dimension 0
- inner_grad: float32 [4, 768, 96], P('rep', 'lat'), parts along dimension 0
- outer_grad: float32 [4, 768, 96], P('rep', 'lat'), parts along dimension 0
There are 2 independent parts, one for each index of `rep`. A program takes and returns all parts, laid end to end along the dimension named above; an argument that names none is the same for every part. Nothing has to cross between parts.
All inputs are finite; a program needn't handle non-finite values.
Results may differ from a plain program's by a relative error of at most 0.017.
Values may be sent and summed in bfloat16 or wider, within the bound.
No kernel may reach another device: no remote copies, remote signals or barrier semaphores. Data moves between devices by JAX's collectives and lax.ppermute only.
A program may use at most 128 MiB of HBM per device.

v0:
```python
from functools import partial
import math

import jax
import jax.numpy as jnp
from jax import lax
from jax.sharding import PartitionSpec as P

EPS = 1e-05
SHRINK = 0.01
FULL_ACCURACY = lax.Precision.HIGHEST


def layer_norm(values, scaling, offset):
    average = jnp.mean(values, axis=-1, keepdims=True)
    centered = values - average
    variance = jnp.mean(centered * centered, axis=-1, keepdims=True)
    return centered * lax.rsqrt(variance + EPS) * scaling + offset


def gelu_exact(values):
    return jax.nn.gelu(values, approximate=False)


def block_mix(real_part, imag_part, weight, offset):
    leading = real_part.shape[:-1]
    features = weight.shape[1]
    block_size = weight.shape[2]
    blocks = features // block_size
    weight_re = weight[0].reshape(blocks, block_size, block_size)
    weight_im = weight[1].reshape(blocks, block_size, block_size)
    real_blocks = real_part.reshape(leading + (blocks, block_size))
    imag_blocks = imag_part.reshape(leading + (blocks, block_size))
    mixing = partial(jnp.einsum, "...bi,bio->...bo", precision=FULL_ACCURACY)
    out_real = mixing(real_blocks, weight_re) - mixing(imag_blocks, weight_im)
    out_imag = mixing(imag_blocks, weight_re) + mixing(real_blocks, weight_im)
    return (
        out_real.reshape(leading + (features,)) + offset[0],
        out_imag.reshape(leading + (features,)) + offset[1],
    )


def soft_threshold(values):
    return values - SHRINK * jnp.tanh(values / SHRINK)


def spectral_mlp(real_part, imag_part, inner_weight, inner_bias, outer_weight, outer_bias):
    hidden_re, hidden_im = block_mix(real_part, imag_part, inner_weight, inner_bias)
    hidden_re = gelu_exact(hidden_re)
    hidden_im = gelu_exact(hidden_im)
    out_re, out_im = block_mix(hidden_re, hidden_im, outer_weight, outer_bias)
    return (soft_threshold(out_re), soft_threshold(out_im))


def lon_tables(length, padded, weighted):
    frequency = jnp.arange(padded, dtype=jnp.int32)[:, None]
    position = jnp.arange(length, dtype=jnp.int32)[None, :]
    angles = 2.0 * math.pi / length * (frequency * position % length).astype(jnp.float32)
    retained = (frequency < length // 2 + 1).astype(jnp.float32)
    if weighted:
        retained = retained * jnp.where((frequency == 0) | (frequency == length // 2), 1.0, 2.0)
    factor = retained / math.sqrt(length)
    return (jnp.cos(angles) * factor, -jnp.sin(angles) * factor)


def lat_tables(latitudes):
    frequency = jnp.arange(latitudes, dtype=jnp.int32)[:, None]
    position = jnp.arange(latitudes, dtype=jnp.int32)[None, :]
    angles = 2.0 * math.pi / latitudes * (frequency * position % latitudes).astype(jnp.float32)
    factor = 1.0 / math.sqrt(latitudes)
    return (jnp.cos(angles) * factor, -jnp.sin(angles) * factor)


def lon_section(field, cosine, sine):
    real_part = jnp.einsum("kw,awd->akd", cosine, field, precision=FULL_ACCURACY)
    imag_part = jnp.einsum("kw,awd->akd", sine, field, precision=FULL_ACCURACY)
    return jnp.stack((real_part, imag_part), axis=2)


def lon_restore(spectrum, cosine, sine):
    first_term = jnp.einsum("kw,akd->awd", cosine, spectrum[:, :, 0], precision=FULL_ACCURACY)
    return first_term + jnp.einsum("kw,akd->awd", sine, spectrum[:, :, 1], precision=FULL_ACCURACY)


def lat_transform(spectrum, cosine, sine, conjugate):
    orient = -1.0 if conjugate else 1.0
    contract_product = partial(jnp.einsum, "pq,qej->pej", precision=FULL_ACCURACY)
    real_part = spectrum[:, :, 0]
    imag_part = spectrum[:, :, 1]
    out_real = contract_product(cosine, real_part) - orient * contract_product(sine, imag_part)
    out_imag = contract_product(cosine, imag_part) + orient * contract_product(sine, real_part)
    return jnp.stack((out_real, out_imag), axis=2)


def to_modes(outgoing):
    return lax.all_to_all(outgoing, "lat", split_axis=1, concat_axis=0, tiled=True)


def to_latitude(outgoing):
    return lax.all_to_all(outgoing, "lat", split_axis=0, concat_axis=1, tiled=True)


def shards(
    block_input,
    cotangent,
    first_gain,
    first_shift,
    inner_weight,
    inner_bias,
    outer_weight,
    outer_bias,
    second_gain,
    second_shift,
    up_weight,
    up_bias,
    down_weight,
    down_bias,
):
    bands, length, channels = block_input.shape
    devices = lax.axis_size("lat")
    latitudes = bands * devices
    padded = -(-(length // 2 + 1) // devices) * devices
    fwd_cos, fwd_sin = lon_tables(length, padded, False)
    inv_cos, inv_sin = lon_tables(length, padded, True)
    lat_cos, lat_sin = lat_tables(latitudes)
    input_f32 = block_input.astype(jnp.float32)
    normed_one, first_vjp = jax.vjp(
        lambda values: layer_norm(values, first_gain, first_shift), input_f32
    )
    outgoing = lon_section(normed_one, fwd_cos, fwd_sin).astype(jnp.bfloat16)
    spectrum = lat_transform(to_modes(outgoing).astype(jnp.float32), lat_cos, lat_sin, False)

    def filter_mlp(real_part, imag_part, weight_a, weight_b):
        return spectral_mlp(real_part, imag_part, weight_a, inner_bias, weight_b, outer_bias)

    mixed_pair, mlp_vjp = jax.vjp(
        filter_mlp, spectrum[:, :, 0], spectrum[:, :, 1], inner_weight, outer_weight
    )
    mixed = jnp.stack(mixed_pair, axis=2)
    returning = lat_transform(mixed, lat_cos, lat_sin, True).astype(jnp.bfloat16)
    filtered = (
        lon_restore(to_latitude(returning).astype(jnp.float32), inv_cos, inv_sin) + normed_one
    )
    residual = (input_f32 + filtered).astype(jnp.bfloat16)
    residual_f32 = residual.astype(jnp.float32)
    normed_two, second_vjp = jax.vjp(
        lambda values: layer_norm(values, second_gain, second_shift), residual_f32
    )
    flat_normed = normed_two.astype(jnp.bfloat16).reshape(bands * length, channels)
    pre_act = (
        jnp.einsum("td,fd->tf", flat_normed, up_weight, preferred_element_type=jnp.float32)
        + up_bias
    )
    hidden_f32, gelu_vjp = jax.vjp(gelu_exact, pre_act)
    hidden = hidden_f32.astype(jnp.bfloat16)
    outcome = (
        jnp.einsum("tf,df->td", hidden, down_weight, preferred_element_type=jnp.float32) + down_bias
    )
    block_output = (
        (residual_f32.reshape(bands * length, channels) + outcome)
        .astype(jnp.bfloat16)
        .reshape(bands, length, channels)
    )
    grad_flat = cotangent.reshape(bands * length, channels)
    grad_hidden = jnp.einsum(
        "td,df->tf", grad_flat, down_weight, preferred_element_type=jnp.float32
    )
    grad_pre = gelu_vjp(grad_hidden)[0].astype(jnp.bfloat16)
    grad_second = jnp.einsum(
        "tf,fd->td", grad_pre, up_weight, preferred_element_type=jnp.float32
    ).reshape(bands, length, channels)
    grad_resid = cotangent.astype(jnp.float32) + second_vjp(grad_second)[0]
    down_grad = lax.psum_scatter(
        jnp.einsum("tc,tf->cf", grad_flat, hidden, preferred_element_type=jnp.float32),
        "lat",
        scatter_dimension=0,
        tiled=True,
    )
    up_grad = lax.psum_scatter(
        jnp.einsum("tc,td->cd", grad_pre, flat_normed, preferred_element_type=jnp.float32),
        "lat",
        scatter_dimension=0,
        tiled=True,
    )
    grad_out = lon_section(grad_resid, inv_cos, inv_sin).astype(jnp.bfloat16)
    grad_spectrum = lat_transform(to_modes(grad_out).astype(jnp.float32), lat_cos, lat_sin, False)
    grad_real, grad_imag, grad_inner, grad_outer = mlp_vjp(
        (grad_spectrum[:, :, 0], grad_spectrum[:, :, 1])
    )
    gradient_longitude = lat_transform(
        jnp.stack((grad_real, grad_imag), axis=2), lat_cos, lat_sin, True
    ).astype(jnp.bfloat16)
    grad_first = (
        lon_restore(to_latitude(gradient_longitude).astype(jnp.float32), fwd_cos, fwd_sin)
        + grad_resid
    )
    input_grad = (grad_resid + first_vjp(grad_first)[0]).astype(jnp.bfloat16)
    inner_grad, outer_grad = (
        lax.psum_scatter(grad_inner, "lat", scatter_dimension=1, tiled=True),
        lax.psum_scatter(grad_outer, "lat", scatter_dimension=1, tiled=True),
    )
    return (block_output, input_grad, up_grad, down_grad, inner_grad, outer_grad)


def solution(mesh):
    placed = (
        P(("rep", "lat"), None, None),
        P(("rep", "lat"), None, None),
        P(),
        P(),
        P(),
        P(),
        P(),
        P(),
        P(),
        P(),
        P(),
        P(),
        P(),
        P(),
    )
    return jax.shard_map(
        shards,
        mesh=mesh,
        in_specs=placed,
        out_specs=(
            P(("rep", "lat"), None, None),
            P(("rep", "lat"), None, None),
            P(("rep", "lat"), None),
            P(("rep", "lat"), None),
            P("rep", "lat", None),
            P("rep", "lat", None),
        ),
        check_vma=False,
    )
```

profile of v0, /device:TPU:0, one launch (start us, length us, event | category | flops | bytes accessed | tf_op | source)
XLA Modules:
  0.0 468.0 jit_solution(15180506890431727519)
XLA Ops:
  7.2 1.1 convert_reduce_fusion
  8.3 1.2 fusion.49
  9.5 2.0 fusion.38
  11.6 2.0 fusion.37
  13.6 1.0 copy.98
  14.6 7.8 %all-to-all-start = ((bf16[1,96,2,768]{3,2,0,1:T(2,128)(2,1)}), bf16[1,96,2,768]{3,2,0,1:T(2,128)(2,1)S(1)}, u32[]{:S(2)}, u32[]{:S(2)}) async-start(bf16[1,96,2,768]{3,2,0,1:T(2,128)(2,1)} %copy.98), calls=%async_computation | async-start | bytes 589824 | tf_op jit(solution)/shard_map/all_to_all | solution.py:96
  23.5 9.5 %all-to-all-done = bf16[1,96,2,768]{3,2,0,1:T(2,128)(2,1)S(1)} async-done(((bf16[1,96,2,768]{3,2,0,1:T(2,128)(2,1)}), bf16[1,96,2,768]{3,2,0,1:T(2,128)(2,1)S(1)}, u32[]{:S(2)}, u32[]{:S(2)}) %all-to-all-start) | async-done | bytes 294944 | tf_op jit(solution)/shard_map/all_to_all | solution.py:96
  34.1 1.0 convolution_subtract_fusion.3
  35.7 1.3 reshape_squeeze_stack.6
  38.1 2.1 fusion.62
  40.2 2.1 fusion.60
  47.2 1.0 copy.111
  48.2 3.7 all-to-all-start.1
  52.1 10.3 %all-to-all-done.1 = bf16[16,6,2,768]{3,2,1,0:T(2,128)(2,1)S(1)} async-done(((bf16[16,6,2,768]{3,2,1,0:T(2,128)(2,1)}), bf16[16,6,2,768]{3,2,1,0:T(2,128)(2,1)S(1)}, u32[]{:S(2)}, u32[]{:S(2)}) %all-to-all-start.1) | async-done | bytes 294944 | tf_op jit(solution)/shard_map/all_to_all | solution.py:100
  63.7 1.0 fusion.412
  65.0 9.3 %multiply_convert_fusion = (bf16[180,3072]{1,0:T(8,128)(2,1)}, f32[180,3072]{1,0:T(8,128)S(1)}, f32[180,3072]{1,0:T(8,128)S(1)}) fusion(f32[3072]{0:T(1024)S(1)} %copy-done.34, bf16[3072,768]{1,0:T(8,128)(2,1)} %param.24, f32[1,180,768]{2,1,0:T(8,128)S(1)} %get-tuple-element.55, f32[768]{0:T(1024)S(1)} %copy-done.32, f32[768]{0:T(1024)S(1)} %copy-done.29, ...), kind=kOutput, calls=%fused_computation.5 | convolution fusion | flops 886533120 | bytes 10821024 | tf_op jit(solution)/shard_map/td,fd->tf/dot_general | solution.py:151
  74.4 1.9 add_convert_fusion
  76.3 1.2 fusion.58
  77.8 1.0 fusion.40
  78.8 1.0 fusion.39
  80.2 13.7 %all_to_all.48 = bf16[1,96,2,768]{3,2,0,1:T(2,128)(2,1)S(1)} all-to-all(bf16[1,96,2,768]{3,2,0,1:T(2,128)(2,1)S(1)} %copy.112), channel_id=1, replica_groups=mesh['rep'=2,'lat'=16] {'lat'}, dimensions={1} | all-to-all | bytes 589824 | tf_op jit(solution)/shard_map/all_to_all | solution.py:96
  95.3 1.0 fusion.227
  96.4 1.1 multiply_add_fusion
  97.4 1.9 reshape.355
  99.3 2.8 convolution_bitcast_fusion.1
  102.1 2.6 convolution_bitcast_fusion.3
  104.7 1.1 multiply_add_fusion.1
  105.8 1.1 reshape.354
  107.0 1.7 fusion.85
  108.7 1.7 fusion.87
  112.0 1.0 pad_add_fusion
  113.5 3.1 fusion.70
  116.6 1.6 fusion.66
  122.5 6.5 %fusion.401 = f32[3072,768]{1,0:T(8,128)} fusion(bf16[180,3072]{1,0:T(8,128)(2,1)} %copy-done.11, f32[1,180,768]{2,1,0:T(8,128)S(1)} %get-tuple-element.55, f32[768]{0:T(1024)S(1)} %copy-done.32, f32[768]{0:T(1024)S(1)} %copy-done.29, f32[180]{0:T(256)S(1)} %fusion.286, f32[180]{0:T(256)S(1)} %broadcast_multiply_fusion), kind=kOutput, calls=%fused_computation.494 | convolution fusion | flops 850037760 | bytes 11103648 | tf_op jit(solution)/shard_map/tc,td->cd/dot_general | solution.py:180
  129.3 6.4 %convolution_bitcast_fusion = f32[768,3072]{0,1:T(8,128)} fusion(bf16[180,3072]{1,0:T(8,128)(2,1)} %get-tuple-element.36, bf16[1,180,768]{2,1,0:T(8,128)(2,1)S(1)} %copy-done.1), kind=kOutput, calls=%fused_computation | convolution fusion | flops 849346560 | bytes 10819584 | tf_op jit(solution)/shard_map/tc,tf->cf/dot_general | solution.py:174
  135.7 9.6 %copy.138 = f32[768,3072]{1,0:T(8,128)} copy(f32[768,3072]{0,1:T(8,128)} %convolution_bitcast_fusion) | data formatting | bytes 18874368
  145.3 1.0 copy-done.17
  148.1 1.0 copy.118
  149.0 1.9 reshape.356
  155.0 1.0 copy.120
  156.0 3.5 all-to-all-start.3
  159.6 4.8 %fusion.32 = bf16[1,180,768]{2,1,0:T(8,128)(2,1)} fusion(bf16[180,3072]{1,0:T(8,128)(2,1)S(1)} %copy-done.20, bf16[768,3072]{1,0:T(8,128)(2,1)} %param.26, f32[1,180,768]{2,1,0:T(8,128)S(1)} %get-tuple-element.55, f32[768]{0:T(1024)S(1)} %copy-done.36), kind=kOutput, calls=%fused_computation.73 | convolution fusion | flops 849761280 | bytes 6657024 | tf_op jit(solution)/shard_map/tf,df->td/dot_general | solution.py:157
  164.4 6.2 %all-to-all-done.3 = bf16[16,6,2,768]{3,2,1,0:T(2,128)(2,1)S(1)} async-done(((bf16[16,6,2,768]{3,2,1,0:T(2,128)(2,1)}), bf16[16,6,2,768]{3,2,1,0:T(2,128)(2,1)S(1)}, u32[]{:S(2)}, u32[]{:S(2)}) %all-to-all-start.3) | async-done | bytes 294944 | tf_op jit(solution)/shard_map/all_to_all | solution.py:100
  171.8 1.1 fusion.55
  173.2 1.0 add_convert_fusion.1
  174.3 55.7 %reduce-scatter.9.cloned.1.call-done = f32[2,48,96]{2,1,0:T(8,128)} async-done(((f32[2,768,96]{2,1,0:T(8,128)}), f32[2,48,96]{2,1,0:T(8,128)}) %reduce-scatter.9.cloned.1.call-update) | async-done | bytes 36880 | tf_op jit(solution)/shard_map/reduce_scatter | solution.py:199
  230.0 115.1 %reduce-scatter.7.cloned.1.call-done = f32[192,768]{1,0:T(8,128)} async-done(((f32[3072,768]{1,0:T(8,128)}), f32[192,768]{1,0:T(8,128)}) %reduce-scatter.7.cloned.1.call-update) | async-done | bytes 589840 | tf_op jit(solution)/shard_map/reduce_scatter | solution.py:179
  345.1 116.2 %reduce-scatter.13.cloned.1.call-done = f32[48,3072]{1,0:T(8,128)} async-done(((f32[768,3072]{1,0:T(8,128)}), f32[48,3072]{1,0:T(8,128)}) %reduce-scatter.13.cloned.1.call-update) | async-done | bytes 589840
  (164 shorter events, 26.2 us)
Async XLA Ops:
  7.2 15.3 %copy-start.30 = (f32[2,768]{1,0:T(2,128)S(1)}, f32[2,768]{1,0:T(2,128)}, u32[]{:S(2)}) copy-start(f32[2,768]{1,0:T(2,128)} %param.19) | copy-start | bytes 18436
  7.2 15.5 %copy-start.26 = (f32[2,768,96]{1,2,0:T(8,128)S(1)}, f32[2,768,96]{1,2,0:T(8,128)}, u32[]{:S(2)}) copy-start(f32[2,768,96]{1,2,0:T(8,128)} %param.18) | copy-start | bytes 1769476
  13.6 9.5 %copy-start.27 = (f32[2,768,96]{1,2,0:T(8,128)S(1)}, f32[2,768,96]{1,2,0:T(8,128)}, u32[]{:S(2)}) copy-start(f32[2,768,96]{1,2,0:T(8,128)} %param.20) | copy-start | bytes 1769476
  14.6 18.4 %all-to-all-start = ((bf16[1,96,2,768]{3,2,0,1:T(2,128)(2,1)}), bf16[1,96,2,768]{3,2,0,1:T(2,128)(2,1)S(1)}, u32[]{:S(2)}, u32[]{:S(2)}) async-start(bf16[1,96,2,768]{3,2,0,1:T(2,128)(2,1)} %copy.98), calls=%async_computation | async-start | bytes 589824 | tf_op jit(solution)/shard_map/all_to_all | solution.py:96
  22.7 0.8 copy-start.31
  22.9 17.3 %copy-start.16 = (f32[1,768,96]{2,1,0:T(8,128)}, f32[1,768,96]{2,1,0:T(8,128)S(1)}, u32[]{:S(2)}) copy-start(f32[1,768,96]{2,1,0:T(8,128)S(1)} %copy.103) | copy-start | bytes 884740
  35.7 4.5 copy-start.2
  37.0 3.2 copy-start.4
  40.2 4.1 copy-start.6
  42.3 1.9 copy-start.9
  44.3 2.3 copy-start.12
  45.3 17.5 %copy-start.14 = (f32[16,6,768]{2,0,1:T(8,128)}, f32[16,6,768]{2,0,1:T(8,128)S(1)}, u32[]{:S(2)}) copy-start(f32[16,6,768]{2,0,1:T(8,128)S(1)} %reshape.345) | copy-start | bytes 884740
  46.7 17.0 %copy-start = (bf16[1,180,768]{2,1,0:T(8,128)(2,1)S(1)}, bf16[1,180,768]{2,1,0:T(8,128)(2,1)}, u32[]{:S(2)}) copy-start(bf16[1,180,768]{2,1,0:T(8,128)(2,1)} %param.14) | copy-start | bytes 829444
  46.7 17.0 %copy-start.33 = (f32[768]{0:T(1024)S(1)}, f32[768]{0:T(1024)}, u32[]{:S(2)}) copy-start(f32[768]{0:T(1024)} %param.16) | copy-start | bytes 9220
  46.7 17.0 %copy-start.35 = (f32[768]{0:T(1024)S(1)}, f32[768]{0:T(1024)}, u32[]{:S(2)}) copy-start(f32[768]{0:T(1024)} %param.17) | copy-start | bytes 9220
  48.2 16.8 %copy-start.29 = (f32[768]{0:T(1024)S(1)}, f32[768]{0:T(1024)}, u32[]{:S(2)}) copy-start(f32[768]{0:T(1024)} %param.22) | copy-start | bytes 9220
  48.2 16.8 %copy-start.32 = (f32[768]{0:T(1024)S(1)}, f32[768]{0:T(1024)}, u32[]{:S(2)}) copy-start(f32[768]{0:T(1024)} %param.23) | copy-start | bytes 9220
  48.2 16.8 %copy-start.34 = (f32[3072]{0:T(1024)S(1)}, f32[3072]{0:T(1024)}, u32[]{:S(2)}) copy-start(f32[3072]{0:T(1024)} %param.25) | copy-start | bytes 36868
  48.2 14.2 %all-to-all-start.1 = ((bf16[16,6,2,768]{3,2,1,0:T(2,128)(2,1)}), bf16[16,6,2,768]{3,2,1,0:T(2,128)(2,1)S(1)}, u32[]{:S(2)}, u32[]{:S(2)}) async-start(bf16[16,6,2,768]{3,2,1,0:T(2,128)(2,1)} %copy.111), calls=%async_computation.1 | async-start | bytes 589824 | tf_op jit(solution)/shard_map/all_to_all | solution.py:100
  51.9 122.4 %reduce-scatter.11.cloned.1.call-start = ((), (), s32[]{:S(2)}) async-start(), calls=%async_computation.10 | async-start | bytes 835584 | tf_op jit(solution)/shard_map/reduce_scatter | solution.py:200
  63.7 10.7 %slice-start.2 = ((s8[4718592]{0:T(1024)(128)(4,1)}), s8[4194304]{0:T(1024)(128)(4,1)S(1)}, s32[]{:S(2)}) async-start(s8[4718592]{0:T(1024)(128)(4,1)} %bitcast.593), calls=%async_computation.14 | async-start | bytes 8388608
  63.7 12.6 %slice-start = ((s8[4718592]{0:T(1024)(128)(4,1)}), s8[4194304]{0:T(1024)(128)(4,1)S(1)}, s32[]{:S(2)}) async-start(s8[4718592]{0:T(1024)(128)(4,1)} %bitcast.579), calls=%async_computation.12 | async-start | bytes 8388608
  65.0 9.3 %copy-start.1 = (bf16[1,180,768]{2,1,0:T(8,128)(2,1)S(1)}, bf16[1,180,768]{2,1,0:T(8,128)(2,1)}, u32[]{:S(2)}) copy-start(bf16[1,180,768]{2,1,0:T(8,128)(2,1)} %param.15) | copy-start | bytes 829444
  65.0 9.3 %slice-start.3 = ((s8[4718592]{0:T(1024)(128)(4,1)}), s8[524288]{0:T(1024)(128)(4,1)S(1)}, s32[]{:S(2)}) async-start(s8[4718592]{0:T(1024)(128)(4,1)} %bitcast.593), calls=%async_computation.15 | async-start | bytes 1048576
  65.0 11.2 %slice-start.1 = ((s8[4718592]{0:T(1024)(128)(4,1)}), s8[524288]{0:T(1024)(128)(4,1)S(1)}, s32[]{:S(2)}) async-start(s8[4718592]{0:T(1024)(128)(4,1)} %bitcast.579), calls=%async_computation.13 | async-start | bytes 1048576
  76.3 1.2 copy-start.11
  78.8 17.5 %copy-start.15 = (f32[16,6,768]{2,0,1:T(8,128)S(1)}, f32[16,6,768]{2,0,1:T(8,128)}, u32[]{:S(2)}) copy-start(f32[16,6,768]{2,0,1:T(8,128)} %copy-done.14) | copy-start | bytes 884740
  93.9 8.2 %copy-start.7 = (f32[16,6,8,96]{3,0,1,2:T(8,128)S(1)}, f32[16,6,8,96]{3,0,1,2:T(8,128)}, u32[]{:S(2)}) copy-start(f32[16,6,8,96]{3,0,1,2:T(8,128)} %copy-done.6) | copy-start | bytes 884740
  99.3 5.3 %copy-start.13 = (f32[16,6,768]{2,0,1:T(8,128)S(1)}, f32[16,6,768]{2,0,1:T(8,128)}, u32[]{:S(2)}) copy-start(f32[16,6,768]{2,0,1:T(8,128)} %copy-done.12) | copy-start | bytes 884740
  99.3 5.3 %copy-start.24 = (bf16[16,6,1,768]{3,2,1,0:T(2,128)(2,1)S(1)}, bf16[16,6,1,768]{3,2,1,0:T(2,128)(2,1)}, u32[]{:S(2)}) copy-start(bf16[16,6,1,768]{3,2,1,0:T(2,128)(2,1)} %copy-done.23) | copy-start | bytes 442372
  99.3 5.3 %copy-start.25 = (f32[16,6,768]{2,0,1:T(8,128)S(1)}, f32[16,6,768]{2,0,1:T(8,128)}, u32[]{:S(2)}) copy-start(f32[16,6,768]{2,0,1:T(8,128)} %fusion.227) | copy-start | bytes 884740
  106.9 3.4 copy-start.8
  106.9 3.4 copy-start.22
  106.9 4.2 copy-start.10
  107.0 4.2 copy-start.21
  113.0 117.0 %reduce-scatter.9.cloned.1.call-start = ((), (), s32[]{:S(2)}) async-start(), calls=%async_computation.9 | async-start | bytes 835584 | tf_op jit(solution)/shard_map/reduce_scatter | solution.py:199
  113.4 3.1 copy-start.18
  113.5 3.1 copy-start.28
  113.5 3.1 copy-start.37
  116.6 1.6 copy-start.3
  116.6 2.5 copy-start.5
  122.5 222.6 %reduce-scatter.7.cloned.1.call-start = ((), (), s32[]{:S(2)}) async-start(), calls=%async_computation.8 | async-start | bytes 10027008 | tf_op jit(solution)/shard_map/reduce_scatter | solution.py:179
  129.1 332.2 %reduce-scatter.13.cloned.1.call-start = ((), (), s32[]{:S(2)}) async-start(), calls=%async_computation.11 | async-start | bytes 10027008
  145.3 1.0 copy-start.17
  151.8 1.8 copy-start.19
  153.1 6.5 %copy-start.20 = (bf16[180,3072]{1,0:T(8,128)(2,1)S(1)}, bf16[180,3072]{1,0:T(8,128)(2,1)}, u32[]{:S(2)}) copy-start(bf16[180,3072]{1,0:T(8,128)(2,1)} %get-tuple-element.36) | copy-start | bytes 3317764
  153.1 6.5 %copy-start.36 = (f32[768]{0:T(1024)S(1)}, f32[768]{0:T(1024)}, u32[]{:S(2)}) copy-start(f32[768]{0:T(1024)} %param.27) | copy-start | bytes 9220
  156.0 14.6 %all-to-all-start.3 = ((bf16[16,6,2,768]{3,2,1,0:T(2,128)(2,1)}), bf16[16,6,2,768]{3,2,1,0:T(2,128)(2,1)S(1)}, u32[]{:S(2)}, u32[]{:S(2)}) async-start(bf16[16,6,2,768]{3,2,1,0:T(2,128)(2,1)} %copy.120), calls=%async_computation.3 | async-start | bytes 589824 | tf_op jit(solution)/shard_map/all_to_all | solution.py:100
  (1 other events, 0.7 us)
Sparse Core Ops, SparseCore 0:
  113.1 56.5 reduce-scatter.10
  174.3 55.6 reduce-scatter.8
  234.7 110.3 reduce-scatter.6
  350.1 111.1 reduce-scatter.12
where the time goes:
time: 472 us; the launch traced here: 468 us
  waiting for transfers between devices  313 us (66%)
  matrix products  78.1 us (17%)
  local copies, waits for them, and re-layouts  26 us (6%)
  starting transfers between devices  15.9 us (3%)
  between operations  14.9 us (3%)
  blocking collectives  13.7 us (3%)
  other arithmetic  6.24 us (1%)
    unnamed x5, waiting for transfers between devices  116 us
    reduce_scatter x1, waiting for transfers between devices, shards(): lax.psum_scatter(jnp.einsum('tc,td->cd', grad_pre, flat_normed, preferred...  115 us
    reduce_scatter x1, waiting for transfers between devices, shards(): lax.psum_scatter(grad_inner, 'lat', scatter_dimension=1, tiled=True)  55.7 us
    dot_general x12, matrix products, block_mix(): out_real = mixing(real_blocks, weight_re) - mixing(imag_blocks, weight_im)  17.1 us
    all_to_all x2, waiting for transfers between devices, to_latitude(): lax.all_to_all(outgoing, 'lat', split_axis=0, concat_axis=1, tiled=True)  16.5 us
    all_to_all x1, blocking collectives, to_modes(): lax.all_to_all(outgoing, 'lat', split_axis=1, concat_axis=0, tiled=True)  13.7 us
    dot_general x12, matrix products, block_mix(): out_imag = mixing(imag_blocks, weight_re) + mixing(real_blocks, weight_im)  12.1 us
    unnamed x85, local copies, waits for them, and re-layouts  11.5 us
  transfers between devices with their start and end apart: 7, of which 6 were waited for; matrix products, arithmetic and copies ran while one was open for 11% of the time, Pallas kernels for 0%

commit v1 on v0

v1 whole, which is shorter than its diff:
```python
from functools import partial
import math

import jax
import jax.numpy as jnp
import ml_dtypes
import numpy as np
from jax import lax
from jax.experimental import pallas as pl
from jax.experimental.pallas import tpu as pltpu
from jax.sharding import PartitionSpec as P

EPS = 1e-05
SHRINK = 0.01
LANES = 128
BF16 = jnp.bfloat16
F32 = jnp.float32


def dot(a, b, dims=((1,), (0,))):
    return lax.dot_general(a, b, (dims, ((), ())), preferred_element_type=F32)


def split(values):
    high = values.astype(BF16)
    return high, (values - high.astype(F32)).astype(BF16)


def dot3(a, b):
    return dot(a[0], b[0]) + (dot(a[0], b[1]) + dot(a[1], b[0]))


def host_split(table):
    high = table.astype(np.float32).astype(ml_dtypes.bfloat16)
    low = (table - high.astype(np.float64)).astype(np.float32).astype(ml_dtypes.bfloat16)
    return jnp.asarray(np.stack((high, low)))


def lon_table(length, members, per_member, weighted):
    count = length // 2 + 1
    mode = np.arange(members * per_member).reshape(members, 1, per_member, 1)
    angle = 2.0 * np.pi / length * ((mode * np.arange(length)) % length)
    weight = (mode < count) / math.sqrt(length)
    edge = (mode == 0) | (2 * mode == length)
    if weighted:
        weight = weight * np.where(edge, 1.0, 2.0)
    sine = np.where(edge, 0.0, -np.sin(angle))
    table = np.concatenate((np.cos(angle) * weight, sine * weight), axis=1)
    return table.reshape(members * 2 * per_member, length)


def moments(values):
    average = jnp.mean(values, axis=-1, keepdims=True)
    centered = values - average
    variance = jnp.mean(centered * centered, axis=-1, keepdims=True)
    scale = lax.rsqrt(variance + EPS)
    return centered * scale, scale


def norm_grad(unit, scale, grad_unit):
    mean_grad = jnp.mean(grad_unit, axis=-1, keepdims=True)
    mean_dot = jnp.mean(grad_unit * unit, axis=-1, keepdims=True)
    return scale * (grad_unit - mean_grad - unit * mean_dot)


def gelu_and_slope(values):
    magnitude = jnp.abs(values) * math.sqrt(0.5)
    t = 1.0 / (1.0 + 0.3275911 * magnitude)
    bell = jnp.exp(-0.5 * values * values)
    tail = t * (0.127414796 + t * (-0.142248368 + t * (0.7107068705 + t * (-0.7265760135 + t * 0.5307027145))))
    tail = tail * bell
    phi = jnp.where(values < 0.0, tail, 1.0 - tail)
    return values * phi, phi + values * (bell * (1.0 / math.sqrt(2.0 * math.pi)))


def fft(pairs, sign):
    n = len(pairs)
    if n == 1:
        return pairs
    assert n % 2 == 0
    even, odd = fft(pairs[0::2], sign), fft(pairs[1::2], sign)
    low, high = [], []
    for k in range(n // 2):
        (er, ei), (xr, xi) = even[k], odd[k]
        if k == 0:
            tr, ti = xr, xi
        elif 4 * k == n:
            tr, ti = (-xi, xr) if sign > 0 else (xi, -xr)
        else:
            c, s = math.cos(2.0 * math.pi * k / n), sign * math.sin(2.0 * math.pi * k / n)
            tr, ti = xr * c - xi * s, xr * s + xi * c
        low.append((er + tr, ei + ti))
        high.append((er - tr, ei - ti))
    return low + high


def spread(values, block):
    zeros = jnp.zeros((values.shape[0], LANES - block), values.dtype)
    pieces = []
    for b in range(values.shape[1] // block):
        pieces += [jnp.concatenate((values[:, b * block:(b + 1) * block], zeros), axis=1)]
    return jnp.concatenate(pieces, axis=1)


def compact(values, block, blocks):
    return jnp.concatenate([values[:, b * LANES:b * LANES + block] for b in range(blocks)], axis=1)


def lane_mask(shape, low, high):
    lane = lax.broadcasted_iota(jnp.int32, shape, 1)
    return (lane >= low) & (lane < high)


def pack(values, block):
    rows = values.shape[0]
    free = LANES - block
    kept = rows * block // LANES
    spare = rows - kept
    out = []
    for k in range(kept // spare):
        moved = pltpu.roll(values[kept:], block - k * free, 1)
        own = values[k * spare:(k + 1) * spare]
        out.append(jnp.where(lane_mask(own.shape, 0, block), own, moved))
    return jnp.concatenate(out, axis=0)


def unpack(values, block):
    kept = values.shape[0]
    free = LANES - block
    spare = kept * free // block
    last = jnp.zeros((spare, LANES), values.dtype)
    for k in range(kept // spare):
        moved = pltpu.roll(values[k * spare:(k + 1) * spare], LANES - block + k * free, 1)
        last = jnp.where(lane_mask(moved.shape, k * free, (k + 1) * free), moved, last)
    first = jnp.where(lane_mask(values.shape, 0, block), values, 0.0)
    return jnp.concatenate((first, last), axis=0)


def gather_blocks(ref, members, block, out_ref):
    devices = ref.shape[0]
    rows = out_ref.shape[0] // members
    for d in range(devices):
        b, r = d // members, d % members
        out_ref[r * rows:(r + 1) * rows, b * LANES:(b + 1) * LANES] = unpack(ref[d].astype(F32), block).astype(BF16)
    return out_ref[...]


def scatter_blocks(values, members, block, ref):
    rows = values.shape[0] // members
    for d in range(ref.shape[0]):
        b, r = d // members, d % members
        piece = values[r * rows:(r + 1) * rows, b * LANES:(b + 1) * LANES]
        ref[d] = pack(piece, block).astype(BF16)


def pad_rows(values, rows):
    return jnp.concatenate((values, jnp.zeros((rows - values.shape[0], values.shape[1]), values.dtype)), axis=0)


def fetch(pairs, sems):
    copies = [pltpu.make_async_copy(src, dst, sems.at[i]) for i, (src, dst) in enumerate(pairs)]
    for copy in copies:
        copy.start()
    return copies


def first_kernel(members, block, x_hbm, gain_ref, shift_ref, table_hbm, out_ref, x_ref, table_ref, sems):
    x_copy, table_copy = fetch(((x_hbm, x_ref), (table_hbm, table_ref)), sems)
    x_copy.wait()
    unit, _ = moments(x_ref[...].astype(F32))
    first = unit * gain_ref[...][None] + shift_ref[...][None]
    wide = split(spread(pad_rows(first, table_ref.shape[2]), block))
    table_copy.wait()
    scatter_blocks(dot3((table_ref[0], table_ref[1]), wide), members, block, out_ref)


def load_transform(ref, block, sign, wide_ref, rows_ref):
    devices, rows, _ = rows_ref.shape
    half = rows // 2
    factor = 1.0 / math.sqrt(devices)
    for h in range(devices):
        rows_ref[h] = unpack(ref[h].astype(F32) * factor, block)
    for row in range(0, half, 8):
        pairs = [(rows_ref[h, row:row + 8], rows_ref[h, half + row:half + row + 8]) for h in range(devices)]
        for h, (re, im) in enumerate(fft(pairs, sign)):
            wide_ref[h * half + row:h * half + row + 8, :LANES] = re
            wide_ref[h * half + row:h * half + row + 8, LANES:] = im


def store_transform(wide_ref, block, sign, ref, rows_ref):
    devices, rows, _ = rows_ref.shape
    half = rows // 2
    factor = 1.0 / math.sqrt(devices)
    for row in range(0, half, 8):
        pairs = [
            (wide_ref[h * half + row:h * half + row + 8, :LANES], wide_ref[h * half + row:h * half + row + 8, LANES:])
            for h in range(devices)
        ]
        for h, (re, im) in enumerate(fft(pairs, sign)):
            rows_ref[h, row:row + 8] = re
            rows_ref[h, half + row:half + row + 8] = im
    for h in range(devices):
        ref[h] = (pack(rows_ref[h], block) * factor).astype(BF16)


def filter_kernel(block, in_ref, w1h_ref, w1l_ref, b1_ref, w2h_ref, w2l_ref, b2_ref,
                  out_ref, spec_ref, hid_ref, slope_ref, shrink_ref, wide_ref, rows_ref):
    load_transform(in_ref, block, -1.0, wide_ref, rows_ref)
    spectrum = split(wide_ref[...])
    spec_ref[...] = spectrum[0]
    pre = dot3(spectrum, (w1h_ref[...], w1l_ref[...])) + b1_ref[...]
    inner, slope = gelu_and_slope(pre)
    slope_ref[...] = slope.astype(BF16)
    inner = split(inner)
    hid_ref[...] = inner[0]
    outer = dot3(inner, (w2h_ref[...], w2l_ref[...])) + b2_ref[...]
    bend = jnp.tanh(outer / SHRINK)
    shrink_ref[...] = (bend * bend).astype(BF16)
    wide_ref[...] = outer - SHRINK * bend
    store_transform(wide_ref, block, 1.0, out_ref, rows_ref)


def complex_grad(grad, block):
    a, b = slice(0, block), slice(LANES, LANES + block)
    return grad[a, a] + grad[b, b], grad[a, b] - grad[b, a]


def filter_grad_kernel(block, in_ref, w1_ref, w2_ref, spec_ref, hid_ref, slope_ref, shrink_ref,
                       out_ref, grads_ref, wide_ref, rows_ref):
    load_transform(in_ref, block, -1.0, wide_ref, rows_ref)
    grad_outer = (wide_ref[...] * shrink_ref[...].astype(F32)).astype(BF16)
    grad_inner = dot(grad_outer, w2_ref[...], ((1,), (1,)))
    grad_pre = (grad_inner * slope_ref[...].astype(F32)).astype(BF16)
    wide_ref[...] = dot(grad_pre, w1_ref[...], ((1,), (1,)))
    store_transform(wide_ref, block, 1.0, out_ref, rows_ref)
    re, im = complex_grad(dot(spec_ref[...], grad_pre, ((0,), (0,))), block)
    grads_ref[0, 0] = re
    grads_ref[0, 1] = im
    re, im = complex_grad(dot(hid_ref[...], grad_outer, ((0,), (0,))), block)
    grads_ref[1, 0] = re
    grads_ref[1, 1] = im


def second_kernel(members, block, blocks, in_ref, x_ref, gain1_ref, shift1_ref, gain2_ref, shift2_ref, table_hbm,
                  resid_ref, second_ref, rows_ref, table_ref, sems):
    (table_copy,) = fetch(((table_hbm, table_ref),), sems)
    back = gather_blocks(in_ref, members, block, rows_ref)
    x = x_ref[...].astype(F32)
    unit, _ = moments(x)
    x = pad_rows(x + (unit * gain1_ref[...][None] + shift1_ref[...][None]), resid_ref.shape[0])
    table_copy.wait()
    filtered = compact(dot(table_ref[0], back) + dot(table_ref[1], back), block, blocks)
    residual = (x + filtered).astype(BF16)
    resid_ref[...] = residual
    unit, _ = moments(residual.astype(F32))
    second = unit * gain2_ref[...][None] + shift2_ref[...][None]
    second_ref[...] = pad_rows(second[:x_ref.shape[0]], resid_ref.shape[0]).astype(BF16)


def mlp_kernel(members, block, chunk, second_ref, cot_ref, resid_ref, gain_ref, up_ref, upb_ref, ghid_ref, table_hbm,
               hid_ref, gres_ref, out_ref, acc_ref, table_ref, sems):
    (table_copy,) = fetch(((table_hbm, table_ref),), sems)
    for start in range(0, up_ref.shape[0], chunk):
        part = slice(start, start + chunk)
        pre = dot(second_ref[...], up_ref[part], ((1,), (1,))) + upb_ref[:, part]
        hidden, slope = gelu_and_slope(pre)
        hid_ref[:, part] = hidden.astype(BF16)
        grad_pre = (ghid_ref[:, part] * slope).astype(BF16)
        term = dot(grad_pre, up_ref[part])
        if start == 0:
            acc_ref[...] = term
        else:
            acc_ref[...] += term
    unit, scale = moments(resid_ref[...].astype(F32))
    grad = cot_ref[...].astype(F32) + norm_grad(unit, scale, acc_ref[...] * gain_ref[...][None])
    gres_ref[...] = grad
    wide = split(spread(grad, block))
    table_copy.wait()
    scatter_blocks(dot3((table_ref[0], table_ref[1]), wide), members, block, out_ref)


def last_kernel(members, block, blocks, in_ref, x_ref, gain_ref, gres_ref, table_hbm, out_ref, rows_ref, table_ref,
                sems):
    (table_copy,) = fetch(((table_hbm, table_ref),), sems)
    back = gather_blocks(in_ref, members, block, rows_ref)
    unit, scale = moments(x_ref[...].astype(F32))
    length = unit.shape[0]
    gres = gres_ref[:length]
    table_copy.wait()
    grad = compact(dot(table_ref[0], back) + dot(table_ref[1], back), block, blocks)[:length]
    out_ref[...] = (gres + norm_grad(unit, scale, (grad + gres) * gain_ref[...][None])).astype(BF16)


def down_part_kernel(second_ref, cot_ref, up_ref, bias_ref, out_ref, acc_ref):
    step = pl.program_id(0)
    tokens = second_ref.shape[0] * second_ref.shape[1]
    second = second_ref[...].reshape(tokens, -1)
    hidden, _ = gelu_and_slope(dot(second, up_ref[...], ((1,), (1,))) + bias_ref[...])
    term = dot(hidden.astype(BF16), cot_ref[...].reshape(tokens, -1), ((0,), (0,)))

    @pl.when(step == 0)
    def _():
        acc_ref[...] = term

    @pl.when(step > 0)
    def _():
        acc_ref[...] += term

    @pl.when(step == pl.num_programs(0) - 1)
    def _():
        out_ref[...] = acc_ref[...].T.astype(BF16)


def up_part_kernel(second_ref, cot_ref, up_ref, bias_ref, down_ref, out_ref):
    step = pl.program_id(0)
    tokens = second_ref.shape[0] * second_ref.shape[1]
    second = second_ref[...].reshape(tokens, -1)
    _, slope = gelu_and_slope(dot(second, up_ref[...], ((1,), (1,))) + bias_ref[...])
    grad_pre = (dot(cot_ref[...].reshape(tokens, -1), down_ref[...]) * slope).astype(BF16)
    term = dot(grad_pre, second, ((0,), (0,)))

    @pl.when(step == 0)
    def _():
        out_ref[...] = term

    @pl.when(step > 0)
    def _():
        out_ref[...] += term


def struct(shape, dtype):
    return jax.ShapeDtypeStruct(shape, dtype)


VMEM = pl.BlockSpec(memory_space=pltpu.VMEM)
HBM = pl.BlockSpec(memory_space=pl.ANY)


def call(kernel, out, scratch, in_specs, *args, limit=24):
    return pl.pallas_call(
        kernel, out_shape=out, scratch_shapes=scratch, in_specs=in_specs,
        compiler_params=pltpu.CompilerParams(vmem_limit_bytes=limit << 20))(*args)


def ring_order(devices):
    width = devices // 8
    chips = []
    for row in range(4):
        columns = list(range(1, width))
        chips += [row * width + c for c in (columns if row % 2 == 0 else columns[::-1])]
    chips += [row * width for row in (3, 2, 1, 0)]
    return [2 * chip + core for chip in chips for core in (0, 1)]


def complex_weight(weight, block):
    pad = ((0, LANES - block), (0, LANES - block))
    re, im = jnp.pad(weight[0], pad), jnp.pad(weight[1], pad)
    return jnp.concatenate((jnp.concatenate((re, im), 1), jnp.concatenate((-im, re), 1)), 0)


def shards(
    block_input,
    cotangent,
    first_gain,
    first_shift,
    inner_weight,
    inner_bias,
    outer_weight,
    outer_bias,
    second_gain,
    second_shift,
    up_weight,
    up_bias,
    down_weight,
    down_bias,
):
    bands, length, channels = block_input.shape
    assert bands == 1
    devices = lax.axis_size("lat")
    index = lax.axis_index("lat")
    block = inner_weight.shape[2]
    blocks = channels // block
    members = devices // blocks
    per_member = -(-(length // 2 + 1) // members)
    per_member = -(-per_member // 16) * 16
    rows = 2 * per_member
    units = up_weight.shape[0]
    tokens = -(-length // 64) * 64
    x = block_input[0]
    cot = jnp.pad(cotangent[0], ((0, tokens - length), (0, 0)))
    ring = [ring_order(devices)]
    all_gather = partial(lax.all_gather, axis_name="lat", axis=0, axis_index_groups=ring)
    a2a = partial(lax.all_to_all, axis_name="lat", split_axis=0, concat_axis=0, tiled=True)
    cot_all = all_gather(cot)

    fwd = np.pad(lon_table(length, members, per_member, False), ((0, 0), (0, tokens - length)))
    inv = np.pad(lon_table(length, members, per_member, True), ((0, 0), (0, tokens - length)))
    all_rows, wide = members * rows, blocks * LANES
    packed = struct((devices, rows * block // LANES, LANES), BF16)
    row_scratch = pltpu.VMEM((all_rows, wide), BF16)
    table_scratch = pltpu.VMEM((2, all_rows, tokens), BF16)
    back_scratch = pltpu.VMEM((2, tokens, all_rows), BF16)
    sems = pltpu.SemaphoreType.DMA((2,))

    start = (index // members) * block
    def own(array):
        return lax.dynamic_slice_in_dim(array, start, block, 1)
    w1 = split(complex_weight(own(inner_weight), block))
    w2 = split(complex_weight(own(outer_weight), block))
    b1 = jnp.pad(own(inner_bias), ((0, 0), (0, LANES - block))).reshape(1, 2 * LANES)
    b2 = jnp.pad(own(outer_bias), ((0, 0), (0, LANES - block))).reshape(1, 2 * LANES)
    grad_hidden = dot(cot, down_weight)

    outgoing = call(
        partial(first_kernel, members, block), packed,
        [pltpu.VMEM((length, channels), BF16), table_scratch, sems], [HBM, VMEM, VMEM, HBM],
        x, first_gain, first_shift, host_split(fwd))
    incoming = a2a(outgoing)
    spectral = struct((devices * per_member, 2 * LANES), BF16)
    spectral_scratch = [
        pltpu.VMEM((devices * per_member, 2 * LANES), F32), pltpu.VMEM((devices, rows, LANES), F32)]
    returning, spec, hid, slope, bend = call(
        partial(filter_kernel, block), (packed, spectral, spectral, spectral, spectral), spectral_scratch,
        [VMEM] * 7, incoming, *w1, b1, *w2, b2)
    back = a2a(returning)
    token = struct((tokens, channels), BF16)
    residual, second = call(
        partial(second_kernel, members, block, blocks), (token, token), [row_scratch, back_scratch, sems],
        [VMEM] * 6 + [HBM],
        back, x, first_gain, first_shift, second_gain, second_shift, host_split(inv.T))

    chunk = 512
    hidden, grad_resid, grad_out = call(
        partial(mlp_kernel, members, block, chunk),
        (struct((tokens, units), BF16), struct((tokens, channels), F32), packed),
        [pltpu.VMEM((tokens, channels), F32), table_scratch, sems], [VMEM] * 7 + [HBM],
        second, cot, residual, second_gain, up_weight, up_bias[None], grad_hidden, host_split(inv), limit=32)
    grad_in = a2a(grad_out)
    second_out, cot_all, _ = lax.optimization_barrier((second, cot_all, grad_out))
    second_all = all_gather(second_out)
    block_output = (
        residual.astype(F32) + dot(hidden, down_weight, ((1,), (1,))) + down_bias
    ).astype(BF16)[None, :length]

    grad_back, terms = call(
        partial(filter_grad_kernel, block), (packed, struct((2, 2, block, block), F32)), spectral_scratch,
        [VMEM] * 7, grad_in, w1[0], w2[0], spec, hid, slope, bend)
    grad_lon = a2a(grad_back)
    input_grad = call(
        partial(last_kernel, members, block, blocks), struct((length, channels), BF16),
        [row_scratch, back_scratch, sems], [VMEM] * 4 + [HBM],
        grad_lon, x, first_gain, grad_resid, host_split(fwd.T))[None]

    part = block // members
    terms = terms.reshape(2, 2, members, part, block)
    member = index % members
    def piece(which):
        return lax.dynamic_index_in_dim(terms, which, 2, keepdims=False)
    total = piece(member)
    for hop in range(1, members):
        pairs = [(d, d - d % members + (d % members + hop) % members) for d in range(devices)]
        total = total + lax.ppermute(piece((member + hop) % members), "lat", pairs)

    share = units // devices
    up_own = lax.dynamic_slice_in_dim(up_weight, index * share, share, 0)
    bias_own = lax.dynamic_slice_in_dim(up_bias, index * share, share, 0)[None]
    down_own = lax.dynamic_slice_in_dim(down_weight, index * share, share, 1)
    group = 4 if devices % 4 == 0 else 1
    whole = lambda shape: pl.BlockSpec(shape, lambda i: (0,) * len(shape))
    gathered = pl.BlockSpec((group, tokens, channels), lambda i: (i, 0, 0))
    params = pltpu.CompilerParams(vmem_limit_bytes=24 << 20)
    down_part = pl.pallas_call(
        down_part_kernel, grid=(devices // group,),
        in_specs=[gathered, gathered, whole((share, channels)), whole((1, share))],
        out_specs=whole((channels, share)), out_shape=struct((channels, share), BF16),
        scratch_shapes=[pltpu.VMEM((share, channels), F32)], compiler_params=params,
    )(second_all, cot_all, up_own, bias_own)
    down_rows = a2a(down_part.reshape(devices, channels // devices, share))
    down_grad = down_rows.transpose(1, 0, 2).reshape(channels // devices, units).astype(F32)
    up_grad = pl.pallas_call(
        up_part_kernel, grid=(devices // group,),
        in_specs=[gathered, gathered, whole((share, channels)), whole((1, share)), whole((channels, share))],
        out_specs=whole((share, channels)), out_shape=struct((share, channels), F32), compiler_params=params,
    )(second_all, cot_all, up_own, bias_own, down_own)
    return (block_output, input_grad, up_grad, down_grad, total[0], total[1])


def solution(mesh):
    tokens = P(("rep", "lat"), None, None)
    return jax.shard_map(
        shards,
        mesh=mesh,
        in_specs=(tokens, tokens) + (P(),) * 12,
        out_specs=(
            tokens,
            tokens,
            P(("rep", "lat"), None),
            P(("rep", "lat"), None),
            P("rep", "lat", None),
            P("rep", "lat", None),
        ),
        check_vma=False,
    )
```

time: 472 us -> 164 us (0.35)
  waiting for transfers between devices: 313 us -> 44.4 us
  matrix products: 78.1 us -> 9.06 us
  Pallas kernels: 0 us -> 33.9 us
  blocking collectives: 13.7 us -> 0 us
  local copies, waits for them, and re-layouts: 26 us -> 35.9 us
  starting transfers between devices: 15.9 us -> 22.4 us
    reduce_scatter x3 -> x0, waiting for transfers between devices: 171 us -> none  [the longest x1 115 us: shards(): lax.psum_scatter(jnp.einsum('tc,td->cd', grad_pre, flat_normed, preferred...]
    unnamed x5 -> x2, waiting for transfers between devices: 116 us -> 0.03 us
    dot_general x54 -> x2, matrix products: 78.1 us -> 9.06 us  [dot(): return lax.dot_general(a, b, (dims, ((), ())), preferred_element_type=F32)]
    pallas_call x0 -> x8, Pallas kernels: none -> 33.9 us  [the longest x6 18.5 us: call(): pl.pallas_call(kernel, out_shape=out, scratch_shapes=scratch, in_specs=in...]
    unnamed x85 -> x72, local copies, waits for them, and re-layouts: 11.5 us -> 27.7 us
    all_to_all x1 -> x0, blocking collectives: 13.7 us -> none  [to_modes(): lax.all_to_all(outgoing, 'lat', split_axis=1, concat_axis=0, tiled=True)]
    all_gather x0 -> x2, waiting for transfers between devices: none -> 11 us  [the longest x1 11 us: shards(): second_all = all_gather(second_out)]
    all_to_all x3 -> x5, waiting for transfers between devices: 26 us -> 33.4 us  [the longest x1 13.3 us: shards(): grad_in = a2a(grad_out)]
  transfers between devices with their start and end apart: 7 -> 8, of which waited for: 6 -> 4; matrix products, arithmetic and copies ran while one was open for 11% -> 10% of each run, Pallas kernels for 0% -> 21%
where the time goes in v1:
time: 164 us; the launch traced here: 162 us
  waiting for transfers between devices  44.4 us (27%)
  local copies, waits for them, and re-layouts  35.9 us (22%)
  Pallas kernels  33.9 us (21%)
  starting transfers between devices  22.4 us (14%)
  between operations  14.4 us (9%)
  matrix products  9.06 us (6%)
  other arithmetic  2.01 us (1%)
    unnamed x72, local copies, waits for them, and re-layouts  27.7 us
    pallas_call x6, Pallas kernels, call(): pl.pallas_call(kernel, out_shape=out, scratch_shapes=scratch, in_specs=in...  18.5 us
    all_to_all x1, waiting for transfers between devices, shards(): grad_in = a2a(grad_out)  13.3 us
    all_to_all x1, waiting for transfers between devices, shards(): incoming = a2a(outgoing)  12.8 us
    all_gather x1, waiting for transfers between devices, shards(): second_all = all_gather(second_out)  11 us
    dot_general x2, matrix products, dot(): return lax.dot_general(a, b, (dims, ((), ())), preferred_element_type=F32)  9.06 us
    pallas_call x1, Pallas kernels, shards(): pl.pallas_call(up_part_kernel, grid=(devices // group,), in_specs=[gather...  7.73 us
    pallas_call x1, Pallas kernels, shards(): pl.pallas_call(down_part_kernel, grid=(devices // group,), in_specs=[gath...  7.65 us
  transfers between devices with their start and end apart: 8, of which 4 were waited for; matrix products, arithmetic and copies ran while one was open for 10% of the time, Pallas kernels for 21%

profile of v1, /device:TPU:0, one launch (start us, length us, event | category | flops | bytes accessed | tf_op | source)
XLA Modules:
  0.0 162.2 jit_solution(15426400964278357679)
XLA Ops:
  7.2 1.7 %pad.30.cot_ref = bf16[192,768]{1,0:T(8,128)(2,1)} pad(bf16[180,768]{1,0:T(8,128)(2,1)} %bitcast.44, bf16[]{:T(256)} %constant.56.clone.1), padding=0_12x0_0 | pad | bytes 571394 | tf_op jit(solution)/shard_map/jit(_pad)/pad | solution.py:390
  9.0 0.9 copy-done.6
  9.9 0.9 copy-done.23
  10.8 0.7 copy-done.25
  12.2 2.1 %shard_map.217 = bf16[16,72,128]{2,1,0:T(8,128)(2,1)} custom-call(bf16[180,768]{1,0:T(8,128)(2,1)S(1)} %bitcast.34, f32[768]{0:T(1024)S(1)} %copy-done.25, f32[768]{0:T(1024)S(1)} %copy-done.27, bf16[2,192,192]{2,1,0:T(8,128)(2,1)S(1)} %copy-done.23), custom_call_target="tpu_custom_call" | custom-call | tf_op jit(solution)/shard_map/pallas_call | solution.py:340
  14.3 7.4 %all-to-all-start = ((bf16[16,72,128]{2,1,0:T(8,128)(2,1)}), bf16[16,72,128]{2,1,0:T(8,128)(2,1)S(1)}, u32[]{:S(2)}, u32[]{:S(2)}) async-start(bf16[16,72,128]{2,1,0:T(8,128)(2,1)} %shard_map.217), calls=%async_computation | async-start | bytes 589824 | tf_op jit(solution)/shard_map/all_to_all | solution.py:418
  21.7 1.2 constant_dynamic-slice_fusion.5
  23.1 0.8 constant_dynamic-slice_fusion.4
  24.2 12.8 %all-to-all-done.in_ref = bf16[16,72,128]{2,1,0:T(8,128)(2,1)S(1)} async-done(((bf16[16,72,128]{2,1,0:T(8,128)(2,1)}), bf16[16,72,128]{2,1,0:T(8,128)(2,1)S(1)}, u32[]{:S(2)}, u32[]{:S(2)}) %all-to-all-start) | async-done | bytes 294944 | tf_op jit(solution)/shard_map/all_to_all | solution.py:418
  37.0 3.1 %shard_map.218 = (bf16[16,72,128]{2,1,0:T(8,128)(2,1)}, bf16[768,256]{1,0:T(8,128)(2,1)S(1)}, bf16[768,256]{1,0:T(8,128)(2,1)S(1)}, bf16[768,256]{1,0:T(8,128)(2,1)S(1)}, bf16[768,256]{1,0:T(8,128)(2,1)S(1)}) custom-call(bf16[16,72,128]{2,1,0:T(8,128)(2,1)S(1)} %all-to-all-done.in_ref, bf16[256,256]{1,0:T(8,128)(2,1)S(1)} %fusion.4.w1h_ref.w1_ref, ...), custom_call_target="tpu_custom_call" | custom-call | tf_op jit(solution)/shard_map/pallas_call | solution.py:340
  40.1 0.7 copy-done.13
  40.9 0.8 copy-done.15
  41.6 0.7 copy-done.17
  42.4 0.7 copy-done.19
  43.1 3.5 %all-to-all-start.1 = ((bf16[16,72,128]{2,1,0:T(8,128)(2,1)}), bf16[16,72,128]{2,1,0:T(8,128)(2,1)S(1)}, u32[]{:S(2)}, u32[]{:S(2)}) async-start(bf16[16,72,128]{2,1,0:T(8,128)(2,1)} %get-tuple-element.20), calls=%async_computation.1 | async-start | bytes 589824 | tf_op jit(solution)/shard_map/all_to_all | solution.py:425
  46.8 3.7 %fusion.5.ghid_ref = f32[192,3072]{1,0:T(8,128)S(1)} fusion(bf16[768,3072]{1,0:T(8,128)(2,1)} %param.30, bf16[180,768]{1,0:T(8,128)(2,1)} %bitcast.45), kind=kOutput, calls=%fused_computation.25 | convolution fusion | flops 905969664 | bytes 7354368 | tf_op jit(solution)/shard_map/dot_general | solution.py:21
  50.6 7.2 %all-to-all-done.1.in_ref = bf16[16,72,128]{2,1,0:T(8,128)(2,1)S(1)} async-done(((bf16[16,72,128]{2,1,0:T(8,128)(2,1)}), bf16[16,72,128]{2,1,0:T(8,128)(2,1)S(1)}, u32[]{:S(2)}, u32[]{:S(2)}) %all-to-all-start.1) | async-done | bytes 294944 | tf_op jit(solution)/shard_map/all_to_all | solution.py:425
  57.8 0.9 copy-done.22
  58.7 2.1 %shard_map.219 = (bf16[192,768]{1,0:T(8,128)(2,1)S(1)}, bf16[192,768]{1,0:T(8,128)(2,1)}) custom-call(bf16[16,72,128]{2,1,0:T(8,128)(2,1)S(1)} %all-to-all-done.1.in_ref, bf16[180,768]{1,0:T(8,128)(2,1)S(1)} %bitcast.35, f32[768]{0:T(1024)S(1)} %copy-done.26, f32[768]{0:T(1024)S(1)} %copy-done.28, f32[768]{0:T(1024)S(1)} %copy-done.29, f32[768]{0:T(1024)S(1)} %copy-done.31, ...), custom_call_target="tpu_custom_call" | custom-call | tf_op jit(solution)/shard_map/pallas_call | solution.py:340
  60.8 0.7 copy-done.8
  61.5 2.3 %copy-done.4 = bf16[3072,768]{1,0:T(8,128)(2,1)S(1)} copy-done((bf16[3072,768]{1,0:T(8,128)(2,1)S(1)}, bf16[3072,768]{1,0:T(8,128)(2,1)}, u32[]{:S(2)}) %copy-start.4) | copy-done | bytes 4718616
  63.9 1.0 copy-done.9
  64.8 0.9 copy-done.24
  65.8 7.6 %shard_map.220 = (bf16[192,3072]{1,0:T(8,128)(2,1)S(1)}, f32[192,768]{1,0:T(8,128)S(1)}, bf16[16,72,128]{2,1,0:T(8,128)(2,1)}) custom-call(bf16[192,768]{1,0:T(8,128)(2,1)} %get-tuple-element.31.second_ref, bf16[192,768]{1,0:T(8,128)(2,1)S(1)} %copy-done.5, bf16[192,768]{1,0:T(8,128)(2,1)S(1)} %copy-done.9, f32[768]{0:T(1024)S(1)} %copy-done.29, ...), custom_call_target="tpu_custom_call" | custom-call | tf_op jit(solution)/shard_map/pallas_call | solution.py:340
  73.4 0.8 copy-done.11
  74.2 1.0 copy-done.32
  75.2 3.7 %all-to-all-start.2 = ((bf16[16,72,128]{2,1,0:T(8,128)(2,1)}), bf16[16,72,128]{2,1,0:T(8,128)(2,1)S(1)}, u32[]{:S(2)}, u32[]{:S(2)}) async-start(bf16[16,72,128]{2,1,0:T(8,128)(2,1)} %get-tuple-element.24), calls=%async_computation.2 | async-start | bytes 589824 | tf_op jit(solution)/shard_map/all_to_all | solution.py:438
  79.0 1.2 constant_dynamic-slice_fusion.2.down_ref
  80.2 13.3 %all-to-all-done.2.in_ref = bf16[16,72,128]{2,1,0:T(8,128)(2,1)S(1)} async-done(((bf16[16,72,128]{2,1,0:T(8,128)(2,1)}), bf16[16,72,128]{2,1,0:T(8,128)(2,1)S(1)}, u32[]{:S(2)}, u32[]{:S(2)}) %all-to-all-start.2) | async-done | bytes 294944 | tf_op jit(solution)/shard_map/all_to_all | solution.py:438
  93.6 1.0 copy-done.14
  94.5 1.0 copy-done.16
  95.6 1.0 copy-done.18
  96.6 1.0 copy-done.20
  97.6 1.7 %shard_map.221 = (bf16[16,72,128]{2,1,0:T(8,128)(2,1)}, f32[2,2,96,96]{3,2,1,0:T(8,128)S(1)}) custom-call(bf16[16,72,128]{2,1,0:T(8,128)(2,1)S(1)} %all-to-all-done.2.in_ref, bf16[256,256]{1,0:T(8,128)(2,1)S(1)} %fusion.4.w1h_ref.w1_ref, bf16[256,256]{1,0:T(8,128)(2,1)S(1)} %fusion.3.w2h_ref.w2_ref, bf16[768,256]{1,0:T(8,128)(2,1)S(1)} %copy-done.14, ...), custom_call_target="tpu_custom_call" | custom-call | tf_op jit(solution)/shard_map/pallas_call | solution.py:340
  99.3 3.5 %all-to-all-start.3 = ((bf16[16,72,128]{2,1,0:T(8,128)(2,1)}), bf16[16,72,128]{2,1,0:T(8,128)(2,1)S(1)}, u32[]{:S(2)}, u32[]{:S(2)}) async-start(bf16[16,72,128]{2,1,0:T(8,128)(2,1)} %get-tuple-element.29), calls=%async_computation.3 | async-start | bytes 589824 | tf_op jit(solution)/shard_map/all_to_all | solution.py:448
  102.8 1.0 constant_dynamic-slice_fusion.3.up_ref
  103.9 5.3 %fusion.10 = f32[192,768]{1,0:T(8,128)} fusion(bf16[192,3072]{1,0:T(8,128)(2,1)} %copy-done.32, bf16[768,3072]{1,0:T(8,128)(2,1)} %param.30), kind=kOutput, calls=%fused_computation.30 | convolution fusion | flops 905969664 | bytes 6488064 | tf_op jit(solution)/shard_map/dot_general | solution.py:21
  109.6 11.0 %all-gather.7.cloned.1.call-done = bf16[3072,768]{1,0:T(8,128)(2,1)} async-done(((bf16[192,768]{1,0:T(8,128)(2,1)}), bf16[3072,768]{1,0:T(8,128)(2,1)}) %all-gather.7.cloned.1.call-update) | async-done | bytes 4718608 | tf_op jit(solution)/shard_map/all_gather | solution.py:440
  120.6 2.3 %copy-done = bf16[3072,768]{1,0:T(8,128)(2,1)S(1)} copy-done((bf16[3072,768]{1,0:T(8,128)(2,1)S(1)}, bf16[3072,768]{1,0:T(8,128)(2,1)}, u32[]{:S(2)}) %copy-start) | copy-done | bytes 4718616
  123.0 2.3 %copy-done.2 = bf16[3072,768]{1,0:T(8,128)(2,1)S(1)} copy-done((bf16[3072,768]{1,0:T(8,128)(2,1)S(1)}, bf16[3072,768]{1,0:T(8,128)(2,1)}, u32[]{:S(2)}) %copy-start.2) | copy-done | bytes 4718616
  125.3 7.7 %shard_map.224 = bf16[768,192]{1,0:T(8,128)(2,1)} custom-call(bf16[16,192,768]{2,1,0:T(8,128)(2,1)S(1)} %bitcast.32, bf16[16,192,768]{2,1,0:T(8,128)(2,1)S(1)} %bitcast.30, bf16[192,768]{1,0:T(8,128)(2,1)S(1)} %constant_dynamic-slice_fusion.3.up_ref, f32[1,192]{1,0:T(1,128)S(1)} %bitcast.40), custom_call_target="tpu_custom_call" | custom-call | tf_op jit(solution)/shard_map/pallas_call | solution.py:472
  133.0 3.8 %all-to-all-start.4 = ((bf16[16,48,192]{2,1,0:T(8,128)(2,1)}), bf16[16,48,192]{2,1,0:T(8,128)(2,1)S(1)}, u32[]{:S(2)}, u32[]{:S(2)}) async-start(bf16[16,48,192]{2,1,0:T(8,128)(2,1)} %bitcast.14), calls=%async_computation.4 | async-start | bytes 786432 | tf_op jit(solution)/shard_map/all_to_all | solution.py:478
  136.7 1.8 %fusion.2 = bf16[1,180,768]{2,1,0:T(8,128)(2,1)} fusion(f32[192,768]{1,0:T(8,128)} %fusion.10, f32[768]{0:T(1024)S(1)} %copy-done.33, bf16[192,768]{1,0:T(8,128)(2,1)S(1)} %copy-done.10), kind=kLoop, calls=%fused_computation.4 | loop fusion | flops 552960 | bytes 1108992 | tf_op jit(solution)/shard_map/broadcast_in_dim | solution.py:441
  139.2 2.0 %shard_map.222 = bf16[180,768]{1,0:T(8,128)(2,1)} custom-call(bf16[16,72,128]{2,1,0:T(8,128)(2,1)S(1)} %all-to-all-done.3.in_ref, bf16[180,768]{1,0:T(8,128)(2,1)S(1)} %bitcast.36, f32[768]{0:T(1024)S(1)} %copy-done.26, f32[192,768]{1,0:T(8,128)S(1)} %copy-done.12, bf16[2,192,192]{2,1,0:T(8,128)(2,1)S(1)} %copy-done.21), custom_call_target="tpu_custom_call" | custom-call | tf_op jit(solution)/shard_map/pallas_call | solution.py:340
  141.3 2.3 %copy-done.1 = bf16[3072,768]{1,0:T(8,128)(2,1)S(1)} copy-done((bf16[3072,768]{1,0:T(8,128)(2,1)S(1)}, bf16[3072,768]{1,0:T(8,128)(2,1)}, u32[]{:S(2)}) %copy-start.1) | copy-done | bytes 4718616
  143.6 2.3 %copy-done.3 = bf16[3072,768]{1,0:T(8,128)(2,1)S(1)} copy-done((bf16[3072,768]{1,0:T(8,128)(2,1)S(1)}, bf16[3072,768]{1,0:T(8,128)(2,1)}, u32[]{:S(2)}) %copy-start.3) | copy-done | bytes 4718616
  145.9 7.7 %shard_map.223 = f32[192,768]{1,0:T(8,128)} custom-call(bf16[16,192,768]{2,1,0:T(8,128)(2,1)S(1)} %bitcast.33, bf16[16,192,768]{2,1,0:T(8,128)(2,1)S(1)} %bitcast.31, bf16[192,768]{1,0:T(8,128)(2,1)S(1)} %constant_dynamic-slice_fusion.3.up_ref, f32[1,192]{1,0:T(1,128)S(1)} %bitcast.41, bf16[768,192]{1,0:T(8,128)(2,1)S(1)} %constant_dynamic-slice_fusion.2.down_ref), custom_call_target="tpu_custom_call" | custom-call | tf_op jit(solution)/shard_map/pallas_call | solution.py:480
  154.2 1.1 reshape.32
  (75 shorter events, 3.0 us)
Async XLA Ops:
  7.2 68.0 %all-gather.5.cloned.1.call-start = ((), (), s32[]{:S(2)}) async-start(), calls=%async_computation.5 | async-start | bytes 5013504 | tf_op jit(solution)/shard_map/all_gather | solution.py:394
  8.9 1.0 copy-start.6
  9.9 0.9 copy-start.23
  10.8 0.7 copy-start.25
  11.5 0.7 copy-start.27
  14.3 22.7 %all-to-all-start = ((bf16[16,72,128]{2,1,0:T(8,128)(2,1)}), bf16[16,72,128]{2,1,0:T(8,128)(2,1)S(1)}, u32[]{:S(2)}, u32[]{:S(2)}) async-start(bf16[16,72,128]{2,1,0:T(8,128)(2,1)} %shard_map.217), calls=%async_computation | async-start | bytes 589824 | tf_op jit(solution)/shard_map/all_to_all | solution.py:418
  40.1 0.7 copy-start.13
  40.9 0.8 copy-start.15
  41.6 0.7 copy-start.17
  42.4 0.8 copy-start.19
  43.1 14.6 %all-to-all-start.1 = ((bf16[16,72,128]{2,1,0:T(8,128)(2,1)}), bf16[16,72,128]{2,1,0:T(8,128)(2,1)S(1)}, u32[]{:S(2)}, u32[]{:S(2)}) async-start(bf16[16,72,128]{2,1,0:T(8,128)(2,1)} %get-tuple-element.20), calls=%async_computation.1 | async-start | bytes 589824 | tf_op jit(solution)/shard_map/all_to_all | solution.py:425
  46.7 11.1 %copy-start.7 = (bf16[1,180,768]{2,1,0:T(8,128)(2,1)S(1)}, bf16[1,180,768]{2,1,0:T(8,128)(2,1)}, u32[]{:S(2)}) copy-start(bf16[1,180,768]{2,1,0:T(8,128)(2,1)} %param.18) | copy-start | bytes 829444
  46.7 11.1 %copy-start.26 = (f32[768]{0:T(1024)S(1)}, f32[768]{0:T(1024)}, u32[]{:S(2)}) copy-start(f32[768]{0:T(1024)} %gain_ref.5) | copy-start | bytes 9220
  46.7 11.1 %copy-start.28 = (f32[768]{0:T(1024)S(1)}, f32[768]{0:T(1024)}, u32[]{:S(2)}) copy-start(f32[768]{0:T(1024)} %shift1_ref.1) | copy-start | bytes 9220
  46.7 11.1 %copy-start.29 = (f32[768]{0:T(1024)S(1)}, f32[768]{0:T(1024)}, u32[]{:S(2)}) copy-start(f32[768]{0:T(1024)} %gain_ref.4) | copy-start | bytes 9220
  46.7 11.1 %copy-start.31 = (f32[768]{0:T(1024)S(1)}, f32[768]{0:T(1024)}, u32[]{:S(2)}) copy-start(f32[768]{0:T(1024)} %shift2_ref.1) | copy-start | bytes 9220
  46.7 14.8 %copy-start.5 = (bf16[192,768]{1,0:T(8,128)(2,1)S(1)}, bf16[192,768]{1,0:T(8,128)(2,1)}, u32[]{:S(2)}) copy-start(bf16[192,768]{1,0:T(8,128)(2,1)} %pad.30.cot_ref) | copy-start | bytes 884740
  46.7 14.8 %copy-start.30 = (f32[3072]{0:T(1024)S(1)}, f32[3072]{0:T(1024)}, u32[]{:S(2)}) copy-start(f32[3072]{0:T(1024)} %param.29) | copy-start | bytes 36868
  46.8 73.9 %all-gather.7.cloned.1.call-start = ((), (), s32[]{:S(2)}) async-start(), calls=%async_computation.6 | async-start | bytes 5013504 | tf_op jit(solution)/shard_map/all_gather | solution.py:440
  57.8 0.9 copy-start.22
  60.8 0.7 copy-start.8
  61.5 2.3 %copy-start.4 = (bf16[3072,768]{1,0:T(8,128)(2,1)S(1)}, bf16[3072,768]{1,0:T(8,128)(2,1)}, u32[]{:S(2)}) copy-start(bf16[3072,768]{1,0:T(8,128)(2,1)} %up_ref.1) | copy-start | bytes 14155780
  63.9 1.0 copy-start.9
  64.8 0.9 copy-start.24
  73.4 0.8 copy-start.11
  74.2 1.0 copy-start.32
  75.2 18.3 %all-to-all-start.2 = ((bf16[16,72,128]{2,1,0:T(8,128)(2,1)}), bf16[16,72,128]{2,1,0:T(8,128)(2,1)S(1)}, u32[]{:S(2)}, u32[]{:S(2)}) async-start(bf16[16,72,128]{2,1,0:T(8,128)(2,1)} %get-tuple-element.24), calls=%async_computation.2 | async-start | bytes 589824 | tf_op jit(solution)/shard_map/all_to_all | solution.py:438
  93.6 1.0 copy-start.14
  94.5 1.0 copy-start.16
  95.6 1.0 copy-start.18
  96.6 1.0 copy-start.20
  99.3 33.7 %all-to-all-start.3 = ((bf16[16,72,128]{2,1,0:T(8,128)(2,1)}), bf16[16,72,128]{2,1,0:T(8,128)(2,1)S(1)}, u32[]{:S(2)}, u32[]{:S(2)}) async-start(bf16[16,72,128]{2,1,0:T(8,128)(2,1)} %get-tuple-element.29), calls=%async_computation.3 | async-start | bytes 589824 | tf_op jit(solution)/shard_map/all_to_all | solution.py:448
  109.2 29.4 %collective-permute-start = (f32[2,2,48,96]{3,2,1,0:T(8,128)S(1)}, f32[2,2,48,96]{3,2,1,0:T(8,128)S(1)}, u32[]{:S(2)}, u32[]{:S(2)}) collective-permute-start(f32[2,2,48,96]{3,2,1,0:T(8,128)S(1)} %dynamic-slice_bitcast_fusion), channel_id=1, source_target_pairs={{0,1},{1,0},{2,3},{3,2},{4,5},{5,4},{6,7},{7,6},{8,9},{9,8},{10,11... | collective-permute-start | bytes 221192 | tf_op jit(solution)/shard_map/ppermute | solution.py:462
  120.6 2.3 %copy-start = (bf16[3072,768]{1,0:T(8,128)(2,1)S(1)}, bf16[3072,768]{1,0:T(8,128)(2,1)}, u32[]{:S(2)}) copy-start(bf16[3072,768]{1,0:T(8,128)(2,1)} %all-gather.5.cloned.1.call-done) | copy-start | bytes 14155780
  123.0 2.3 %copy-start.2 = (bf16[3072,768]{1,0:T(8,128)(2,1)S(1)}, bf16[3072,768]{1,0:T(8,128)(2,1)}, u32[]{:S(2)}) copy-start(bf16[3072,768]{1,0:T(8,128)(2,1)} %all-gather.7.cloned.1.call-done) | copy-start | bytes 14155780
  125.3 11.4 %copy-start.10 = (bf16[192,768]{1,0:T(8,128)(2,1)S(1)}, bf16[192,768]{1,0:T(8,128)(2,1)}, u32[]{:S(2)}) copy-start(bf16[192,768]{1,0:T(8,128)(2,1)} %copy-done.8) | copy-start | bytes 884740
  125.3 11.4 %copy-start.33 = (f32[768]{0:T(1024)S(1)}, f32[768]{0:T(1024)}, u32[]{:S(2)}) copy-start(f32[768]{0:T(1024)} %param.31) | copy-start | bytes 9220
  125.3 14.0 %copy-start.12 = (f32[192,768]{1,0:T(8,128)S(1)}, f32[192,768]{1,0:T(8,128)}, u32[]{:S(2)}) copy-start(f32[192,768]{1,0:T(8,128)} %copy-done.11) | copy-start | bytes 1769476
  125.3 14.0 %copy-start.21 = (bf16[2,192,192]{2,1,0:T(8,128)(2,1)S(1)}, bf16[2,192,192]{2,1,0:T(8,128)(2,1)}, u32[]{:S(2)}) copy-start(bf16[2,192,192]{2,1,0:T(8,128)(2,1)} %constant.63.clone.table_hbm) | copy-start | bytes 442372
  133.0 20.7 %all-to-all-start.4 = ((bf16[16,48,192]{2,1,0:T(8,128)(2,1)}), bf16[16,48,192]{2,1,0:T(8,128)(2,1)S(1)}, u32[]{:S(2)}, u32[]{:S(2)}) async-start(bf16[16,48,192]{2,1,0:T(8,128)(2,1)} %bitcast.14), calls=%async_computation.4 | async-start | bytes 786432 | tf_op jit(solution)/shard_map/all_to_all | solution.py:478
  141.2 2.3 %copy-start.1 = (bf16[3072,768]{1,0:T(8,128)(2,1)S(1)}, bf16[3072,768]{1,0:T(8,128)(2,1)}, u32[]{:S(2)}) copy-start(bf16[3072,768]{1,0:T(8,128)(2,1)} %all-gather.5.cloned.1.call-done) | copy-start | bytes 14155780
  143.6 2.3 %copy-start.3 = (bf16[3072,768]{1,0:T(8,128)(2,1)S(1)}, bf16[3072,768]{1,0:T(8,128)(2,1)}, u32[]{:S(2)}) copy-start(bf16[3072,768]{1,0:T(8,128)(2,1)} %all-gather.7.cloned.1.call-done) | copy-start | bytes 14155780
Sparse Core Ops, SparseCore 0:
  9.6 45.6 all-gather.4
  75.4 45.2 all-gather.6

commit v2 on v1

--- a/solution.py
+++ b/solution.py
@@ -164,14 +164,20 @@
     return copies
 
 
-def first_kernel(members, block, x_hbm, gain_ref, shift_ref, table_hbm, out_ref, x_ref, table_ref, sems):
-    x_copy, table_copy = fetch(((x_hbm, x_ref), (table_hbm, table_ref)), sems)
-    x_copy.wait()
+def first_kernel(members, block, x_hbm, cot_hbm, gain_hbm, shift_hbm, table_hbm, out_ref, pad_ref,
+                 x_ref, cot_ref, gain_ref, shift_ref, table_ref, sems):
+    copies = fetch(((x_hbm, x_ref), (gain_hbm, gain_ref), (shift_hbm, shift_ref), (table_hbm, table_ref),
+                    (cot_hbm, cot_ref)), sems)
+    copies[0].wait()
     unit, _ = moments(x_ref[...].astype(F32))
+    copies[1].wait()
+    copies[2].wait()
     first = unit * gain_ref[...][None] + shift_ref[...][None]
-    wide = split(spread(pad_rows(first, table_ref.shape[2]), block))
-    table_copy.wait()
+    wide = split(spread(pad_rows(first, pad_ref.shape[0]), block))
+    copies[3].wait()
     scatter_blocks(dot3((table_ref[0], table_ref[1]), wide), members, block, out_ref)
+    copies[4].wait()
+    pad_ref[...] = pad_rows(cot_ref[...].astype(F32), pad_ref.shape[0]).astype(BF16)
 
 
 def load_transform(ref, block, sign, wide_ref, rows_ref):
@@ -203,21 +209,32 @@
         ref[h] = (pack(rows_ref[h], block) * factor).astype(BF16)
 
 
-def filter_kernel(block, in_ref, w1h_ref, w1l_ref, b1_ref, w2h_ref, w2l_ref, b2_ref,
-                  out_ref, spec_ref, hid_ref, slope_ref, shrink_ref, wide_ref, rows_ref):
+def filter_kernel(block, in_ref, w1_ref, b1_ref, w2_ref, b2_ref,
+                  out_ref, spec_hbm, hid_hbm, slope_hbm, shrink_hbm, wide_ref, rows_ref,
+                  spec_ref, hid_ref, slope_ref, shrink_ref, sems):
+    def keep(which, ref, hbm):
+        copy = pltpu.make_async_copy(ref, hbm, sems.at[which])
+        copy.start()
+        return copy
+
     load_transform(in_ref, block, -1.0, wide_ref, rows_ref)
     spectrum = split(wide_ref[...])
     spec_ref[...] = spectrum[0]
-    pre = dot3(spectrum, (w1h_ref[...], w1l_ref[...])) + b1_ref[...]
+    copies = [keep(0, spec_ref, spec_hbm)]
+    pre = dot3(spectrum, split(w1_ref[...])) + b1_ref[...]
     inner, slope = gelu_and_slope(pre)
     slope_ref[...] = slope.astype(BF16)
     inner = split(inner)
     hid_ref[...] = inner[0]
-    outer = dot3(inner, (w2h_ref[...], w2l_ref[...])) + b2_ref[...]
+    copies += [keep(1, hid_ref, hid_hbm), keep(2, slope_ref, slope_hbm)]
+    outer = dot3(inner, split(w2_ref[...])) + b2_ref[...]
     bend = jnp.tanh(outer / SHRINK)
     shrink_ref[...] = (bend * bend).astype(BF16)
+    copies += [keep(3, shrink_ref, shrink_hbm)]
     wide_ref[...] = outer - SHRINK * bend
     store_transform(wide_ref, block, 1.0, out_ref, rows_ref)
+    for copy in copies:
+        copy.wait()
 
 
 def complex_grad(grad, block):
@@ -225,30 +242,40 @@
     return grad[a, a] + grad[b, b], grad[a, b] - grad[b, a]
 
 
-def filter_grad_kernel(block, in_ref, w1_ref, w2_ref, spec_ref, hid_ref, slope_ref, shrink_ref,
-                       out_ref, grads_ref, wide_ref, rows_ref):
+def filter_grad_kernel(block, in_ref, w1_ref, w2_ref, spec_hbm, hid_hbm, slope_hbm, shrink_hbm,
+                       out_ref, grads_ref, wide_ref, rows_ref, spec_ref, hid_ref, slope_ref, shrink_ref, sems):
+    copies = fetch(((shrink_hbm, shrink_ref), (slope_hbm, slope_ref), (spec_hbm, spec_ref), (hid_hbm, hid_ref)), sems)
     load_transform(in_ref, block, -1.0, wide_ref, rows_ref)
+    copies[0].wait()
     grad_outer = (wide_ref[...] * shrink_ref[...].astype(F32)).astype(BF16)
-    grad_inner = dot(grad_outer, w2_ref[...], ((1,), (1,)))
+    grad_inner = dot(grad_outer, w2_ref[...].astype(BF16), ((1,), (1,)))
+    copies[1].wait()
     grad_pre = (grad_inner * slope_ref[...].astype(F32)).astype(BF16)
-    wide_ref[...] = dot(grad_pre, w1_ref[...], ((1,), (1,)))
+    wide_ref[...] = dot(grad_pre, w1_ref[...].astype(BF16), ((1,), (1,)))
     store_transform(wide_ref, block, 1.0, out_ref, rows_ref)
+    copies[2].wait()
     re, im = complex_grad(dot(spec_ref[...], grad_pre, ((0,), (0,))), block)
     grads_ref[0, 0] = re
     grads_ref[0, 1] = im
+    copies[3].wait()
     re, im = complex_grad(dot(hid_ref[...], grad_outer, ((0,), (0,))), block)
     grads_ref[1, 0] = re
     grads_ref[1, 1] = im
 
 
-def second_kernel(members, block, blocks, in_ref, x_ref, gain1_ref, shift1_ref, gain2_ref, shift2_ref, table_hbm,
-                  resid_ref, second_ref, rows_ref, table_ref, sems):
-    (table_copy,) = fetch(((table_hbm, table_ref),), sems)
+def second_kernel(members, block, blocks, in_ref, x_hbm, gain1_hbm, shift1_hbm, gain2_hbm, shift2_hbm, table_hbm,
+                  resid_ref, second_ref, rows_ref, table_ref, x_ref, gain1_ref, shift1_ref, gain2_ref, shift2_ref,
+                  sems):
+    copies = fetch(((x_hbm, x_ref), (gain1_hbm, gain1_ref), (shift1_hbm, shift1_ref), (table_hbm, table_ref),
+                    (gain2_hbm, gain2_ref), (shift2_hbm, shift2_ref)), sems)
     back = gather_blocks(in_ref, members, block, rows_ref)
+    for copy in copies[:3]:
+        copy.wait()
     x = x_ref[...].astype(F32)
     unit, _ = moments(x)
     x = pad_rows(x + (unit * gain1_ref[...][None] + shift1_ref[...][None]), resid_ref.shape[0])
-    table_copy.wait()
+    for copy in copies[3:]:
+        copy.wait()
     filtered = compact(dot(table_ref[0], back) + dot(table_ref[1], back), block, blocks)
     residual = (x + filtered).astype(BF16)
     resid_ref[...] = residual
@@ -257,36 +284,48 @@
     second_ref[...] = pad_rows(second[:x_ref.shape[0]], resid_ref.shape[0]).astype(BF16)
 
 
-def mlp_kernel(members, block, chunk, second_ref, cot_ref, resid_ref, gain_ref, up_ref, upb_ref, ghid_ref, table_hbm,
-               hid_ref, gres_ref, out_ref, acc_ref, table_ref, sems):
-    (table_copy,) = fetch(((table_hbm, table_ref),), sems)
-    for start in range(0, up_ref.shape[0], chunk):
-        part = slice(start, start + chunk)
+def mlp_kernel(members, block, chunk, second_ref, resid_hbm, cot_hbm, gain_hbm, up_hbm, upb_hbm, ghid_hbm, table_hbm,
+               hid_ref, gres_ref, out_ref, acc_ref, resid_ref, cot_ref, gain_ref, up_ref, upb_ref, ghid_ref, table_ref,
+               sems):
+    units = up_ref.shape[0]
+    parts = [slice(start, start + chunk) for start in range(0, units, chunk)]
+    pairs = [(upb_hbm, upb_ref)]
+    for part in parts:
+        pairs += [(up_hbm.at[part], up_ref.at[part]), (ghid_hbm.at[:, part], ghid_ref.at[:, part])]
+    tail = len(pairs)
+    pairs += [(resid_hbm, resid_ref), (cot_hbm, cot_ref), (gain_hbm, gain_ref), (table_hbm, table_ref)]
+    copies = fetch(pairs, sems)
+    copies[0].wait()
+    for i, part in enumerate(parts):
+        copies[2 * i + 1].wait()
         pre = dot(second_ref[...], up_ref[part], ((1,), (1,))) + upb_ref[:, part]
         hidden, slope = gelu_and_slope(pre)
         hid_ref[:, part] = hidden.astype(BF16)
+        copies[2 * i + 2].wait()
         grad_pre = (ghid_ref[:, part] * slope).astype(BF16)
         term = dot(grad_pre, up_ref[part])
-        if start == 0:
+        if i == 0:
             acc_ref[...] = term
         else:
             acc_ref[...] += term
+    for copy in copies[tail:]:
+        copy.wait()
     unit, scale = moments(resid_ref[...].astype(F32))
     grad = cot_ref[...].astype(F32) + norm_grad(unit, scale, acc_ref[...] * gain_ref[...][None])
     gres_ref[...] = grad
     wide = split(spread(grad, block))
-    table_copy.wait()
     scatter_blocks(dot3((table_ref[0], table_ref[1]), wide), members, block, out_ref)
 
 
-def last_kernel(members, block, blocks, in_ref, x_ref, gain_ref, gres_ref, table_hbm, out_ref, rows_ref, table_ref,
-                sems):
-    (table_copy,) = fetch(((table_hbm, table_ref),), sems)
+def last_kernel(members, block, blocks, in_ref, x_hbm, gain_hbm, gres_hbm, table_hbm, out_ref, rows_ref, table_ref,
+                x_ref, gain_ref, gres_ref, sems):
+    copies = fetch(((x_hbm, x_ref), (gain_hbm, gain_ref), (gres_hbm, gres_ref), (table_hbm, table_ref)), sems)
     back = gather_blocks(in_ref, members, block, rows_ref)
+    for copy in copies:
+        copy.wait()
     unit, scale = moments(x_ref[...].astype(F32))
     length = unit.shape[0]
     gres = gres_ref[:length]
-    table_copy.wait()
     grad = compact(dot(table_ref[0], back) + dot(table_ref[1], back), block, blocks)[:length]
     out_ref[...] = (gres + norm_grad(unit, scale, (grad + gres) * gain_ref[...][None])).astype(BF16)
 
@@ -295,8 +334,8 @@
     step = pl.program_id(0)
     tokens = second_ref.shape[0] * second_ref.shape[1]
     second = second_ref[...].reshape(tokens, -1)
-    hidden, _ = gelu_and_slope(dot(second, up_ref[...], ((1,), (1,))) + bias_ref[...])
-    term = dot(hidden.astype(BF16), cot_ref[...].reshape(tokens, -1), ((0,), (0,)))
+    hidden, _ = gelu_and_slope(dot(up_ref[...], second, ((1,), (1,))) + bias_ref[...])
+    term = dot(hidden.astype(BF16), cot_ref[...].reshape(tokens, -1))
 
     @pl.when(step == 0)
     def _():
@@ -315,9 +354,9 @@
     step = pl.program_id(0)
     tokens = second_ref.shape[0] * second_ref.shape[1]
     second = second_ref[...].reshape(tokens, -1)
-    _, slope = gelu_and_slope(dot(second, up_ref[...], ((1,), (1,))) + bias_ref[...])
-    grad_pre = (dot(cot_ref[...].reshape(tokens, -1), down_ref[...]) * slope).astype(BF16)
-    term = dot(grad_pre, second, ((0,), (0,)))
+    _, slope = gelu_and_slope(dot(up_ref[...], second, ((1,), (1,))) + bias_ref[...])
+    grad_hidden = dot(down_ref[...], cot_ref[...].reshape(tokens, -1), ((1,), (1,)))
+    term = dot((grad_hidden * slope).astype(BF16), second)
 
     @pl.when(step == 0)
     def _():
@@ -333,12 +372,15 @@
 
 
 VMEM = pl.BlockSpec(memory_space=pltpu.VMEM)
-HBM = pl.BlockSpec(memory_space=pl.ANY)
-
-
-def call(kernel, out, scratch, in_specs, *args, limit=24):
+HBM = pl.BlockSpec(memory_space=pltpu.HBM)
+
+
+def call(kernel, out, scratch, in_specs, *args, out_specs=None, limit=24):
+    if out_specs is None:
+        out_specs = jax.tree.map(lambda _: VMEM, out)
+    args = [pltpu.with_memory_space_constraint(a, pltpu.HBM) if spec is HBM else a for a, spec in zip(args, in_specs)]
     return pl.pallas_call(
-        kernel, out_shape=out, scratch_shapes=scratch, in_specs=in_specs,
+        kernel, out_shape=out, scratch_shapes=scratch, in_specs=in_specs, out_specs=out_specs,
         compiler_params=pltpu.CompilerParams(vmem_limit_bytes=limit << 20))(*args)
 
 
@@ -387,11 +429,9 @@
     units = up_weight.shape[0]
     tokens = -(-length // 64) * 64
     x = block_input[0]
-    cot = jnp.pad(cotangent[0], ((0, tokens - length), (0, 0)))
     ring = [ring_order(devices)]
     all_gather = partial(lax.all_gather, axis_name="lat", axis=0, axis_index_groups=ring)
     a2a = partial(lax.all_to_all, axis_name="lat", split_axis=0, concat_axis=0, tiled=True)
-    cot_all = all_gather(cot)
 
     fwd = np.pad(lon_table(length, members, per_member, False), ((0, 0), (0, tokens - length)))
     inv = np.pad(lon_table(length, members, per_member, True), ((0, 0), (0, tokens - length)))
@@ -400,55 +440,61 @@
     row_scratch = pltpu.VMEM((all_rows, wide), BF16)
     table_scratch = pltpu.VMEM((2, all_rows, tokens), BF16)
     back_scratch = pltpu.VMEM((2, tokens, all_rows), BF16)
-    sems = pltpu.SemaphoreType.DMA((2,))
+    sems = lambda count: pltpu.SemaphoreType.DMA((count,))
+    row = pltpu.VMEM((channels,), F32)
+    short = pltpu.VMEM((length, channels), BF16)
 
     start = (index // members) * block
     def own(array):
         return lax.dynamic_slice_in_dim(array, start, block, 1)
-    w1 = split(complex_weight(own(inner_weight), block))
-    w2 = split(complex_weight(own(outer_weight), block))
+    w1 = complex_weight(own(inner_weight), block)
+    w2 = complex_weight(own(outer_weight), block)
     b1 = jnp.pad(own(inner_bias), ((0, 0), (0, LANES - block))).reshape(1, 2 * LANES)
     b2 = jnp.pad(own(outer_bias), ((0, 0), (0, LANES - block))).reshape(1, 2 * LANES)
+
+    token = struct((tokens, channels), BF16)
+    outgoing, cot = call(
+        partial(first_kernel, members, block), (packed, token), [short, short, row, row, table_scratch, sems(5)],
+        [HBM] * 5, x, cotangent[0], first_gain, first_shift, host_split(fwd))
+    cot_all = all_gather(cot)
+    incoming = a2a(outgoing)
     grad_hidden = dot(cot, down_weight)
-
-    outgoing = call(
-        partial(first_kernel, members, block), packed,
-        [pltpu.VMEM((length, channels), BF16), table_scratch, sems], [HBM, VMEM, VMEM, HBM],
-        x, first_gain, first_shift, host_split(fwd))
-    incoming = a2a(outgoing)
     spectral = struct((devices * per_member, 2 * LANES), BF16)
-    spectral_scratch = [
-        pltpu.VMEM((devices * per_member, 2 * LANES), F32), pltpu.VMEM((devices, rows, LANES), F32)]
-    returning, spec, hid, slope, bend = call(
+    kept_scratch = [pltpu.VMEM(spectral.shape, BF16)] * 4 + [sems(4)]
+    spectral_scratch = [pltpu.VMEM(spectral.shape, F32), pltpu.VMEM((devices, rows, LANES), F32)] + kept_scratch
+    returning, *kept = call(
         partial(filter_kernel, block), (packed, spectral, spectral, spectral, spectral), spectral_scratch,
-        [VMEM] * 7, incoming, *w1, b1, *w2, b2)
-    back = a2a(returning)
-    token = struct((tokens, channels), BF16)
+        [VMEM] * 5, incoming, w1, b1, w2, b2, out_specs=(VMEM, HBM, HBM, HBM, HBM))
+    back, grad_hidden = lax.optimization_barrier((a2a(returning), grad_hidden))
     residual, second = call(
-        partial(second_kernel, members, block, blocks), (token, token), [row_scratch, back_scratch, sems],
-        [VMEM] * 6 + [HBM],
+        partial(second_kernel, members, block, blocks), (token, token),
+        [row_scratch, back_scratch, short, row, row, row, row, sems(6)], [VMEM] + [HBM] * 6,
         back, x, first_gain, first_shift, second_gain, second_shift, host_split(inv.T))
+    second_out, cot_all = lax.optimization_barrier((second, cot_all))
+    second_all = all_gather(second_out)
 
     chunk = 512
+    full = pltpu.VMEM((tokens, channels), BF16)
     hidden, grad_resid, grad_out = call(
         partial(mlp_kernel, members, block, chunk),
         (struct((tokens, units), BF16), struct((tokens, channels), F32), packed),
-        [pltpu.VMEM((tokens, channels), F32), table_scratch, sems], [VMEM] * 7 + [HBM],
-        second, cot, residual, second_gain, up_weight, up_bias[None], grad_hidden, host_split(inv), limit=32)
+        [pltpu.VMEM((tokens, channels), F32), full, full, row, pltpu.VMEM((units, channels), BF16),
+         pltpu.VMEM((1, units), F32), pltpu.VMEM((tokens, units), F32), table_scratch,
+         sems(2 * (units // chunk) + 5)],
+        [VMEM] + [HBM] * 7,
+        second, residual, cot, second_gain, up_weight, up_bias[None], grad_hidden, host_split(inv), limit=32)
     grad_in = a2a(grad_out)
-    second_out, cot_all, _ = lax.optimization_barrier((second, cot_all, grad_out))
-    second_all = all_gather(second_out)
     block_output = (
         residual.astype(F32) + dot(hidden, down_weight, ((1,), (1,))) + down_bias
     ).astype(BF16)[None, :length]
 
     grad_back, terms = call(
         partial(filter_grad_kernel, block), (packed, struct((2, 2, block, block), F32)), spectral_scratch,
-        [VMEM] * 7, grad_in, w1[0], w2[0], spec, hid, slope, bend)
+        [VMEM] * 3 + [HBM] * 4, grad_in, w1, w2, *kept)
     grad_lon = a2a(grad_back)
     input_grad = call(
         partial(last_kernel, members, block, blocks), struct((length, channels), BF16),
-        [row_scratch, back_scratch, sems], [VMEM] * 4 + [HBM],
+        [row_scratch, back_scratch, short, row, pltpu.VMEM((tokens, channels), F32), sems(4)], [VMEM] + [HBM] * 4,
         grad_lon, x, first_gain, grad_resid, host_split(fwd.T))[None]
 
     part = block // members
@@ -463,25 +509,26 @@
 
     share = units // devices
     up_own = lax.dynamic_slice_in_dim(up_weight, index * share, share, 0)
-    bias_own = lax.dynamic_slice_in_dim(up_bias, index * share, share, 0)[None]
-    down_own = lax.dynamic_slice_in_dim(down_weight, index * share, share, 1)
+    bias_own = lax.dynamic_slice_in_dim(up_bias, index * share, share, 0)[:, None]
+    down_own = lax.dynamic_slice_in_dim(down_weight, index * share, share, 1).T
     group = 4 if devices % 4 == 0 else 1
     whole = lambda shape: pl.BlockSpec(shape, lambda i: (0,) * len(shape))
     gathered = pl.BlockSpec((group, tokens, channels), lambda i: (i, 0, 0))
     params = pltpu.CompilerParams(vmem_limit_bytes=24 << 20)
+    gathered_pair = [pltpu.with_memory_space_constraint(array, pltpu.HBM) for array in (second_all, cot_all)]
     down_part = pl.pallas_call(
         down_part_kernel, grid=(devices // group,),
-        in_specs=[gathered, gathered, whole((share, channels)), whole((1, share))],
+        in_specs=[gathered, gathered, whole((share, channels)), whole((share, 1))],
         out_specs=whole((channels, share)), out_shape=struct((channels, share), BF16),
         scratch_shapes=[pltpu.VMEM((share, channels), F32)], compiler_params=params,
-    )(second_all, cot_all, up_own, bias_own)
+    )(*gathered_pair, up_own, bias_own)
     down_rows = a2a(down_part.reshape(devices, channels // devices, share))
     down_grad = down_rows.transpose(1, 0, 2).reshape(channels // devices, units).astype(F32)
     up_grad = pl.pallas_call(
         up_part_kernel, grid=(devices // group,),
-        in_specs=[gathered, gathered, whole((share, channels)), whole((1, share)), whole((channels, share))],
+        in_specs=[gathered, gathered, whole((share, channels)), whole((share, 1)), whole((share, channels))],
         out_specs=whole((share, channels)), out_shape=struct((share, channels), F32), compiler_params=params,
-    )(second_all, cot_all, up_own, bias_own, down_own)
+    )(*gathered_pair, up_own, bias_own, down_own)
     return (block_output, input_grad, up_grad, down_grad, total[0], total[1])
 
 

time: 164 us -> 139 us (0.85)
  local copies, waits for them, and re-layouts: 35.9 us -> 12.4 us
  waiting for transfers between devices: 44.4 us -> 34.6 us
  Pallas kernels: 33.9 us -> 42.4 us
  starting transfers between devices: 22.4 us -> 24.4 us
    unnamed x72 -> x21, local copies, waits for them, and re-layouts: 27.7 us -> 5.05 us
    all_gather x1, waiting for transfers between devices: 11 us -> 0.01 us  [shards(): second_all = all_gather(second_out)]
    pallas_call x6, Pallas kernels: 18.5 us -> 26.3 us  [call(): pl.pallas_call(kernel, out_shape=out, scratch_shapes=scratch, in_specs=in...]
    all_to_all x1, starting transfers between devices: 3.76 us -> 5.82 us  [shards(): down_rows = a2a(down_part.reshape(devices, channels // devices, share))]
    pad x1 -> x0, local copies, waits for them, and re-layouts: 1.71 us -> none  [shards(): cot = jnp.pad(cotangent[0], ((0, tokens - length), (0, 0)))]
  transfers between devices with their start and end apart: 8 -> 8, of which waited for: 4 -> 3; matrix products, arithmetic and copies ran while one was open for 10% -> 12% of each run, Pallas kernels for 21% -> 29%
where the time goes in v2:
time: 139 us; the launch traced here: 138 us
  Pallas kernels  42.4 us (31%)
  waiting for transfers between devices  34.6 us (25%)
  starting transfers between devices  24.4 us (18%)
  between operations  14.4 us (10%)
  local copies, waits for them, and re-layouts  12.4 us (9%)
  matrix products  9.09 us (7%)
    pallas_call x6, Pallas kernels, call(): pl.pallas_call(kernel, out_shape=out, scratch_shapes=scratch, in_specs=in...  26.3 us
    all_to_all x1, waiting for transfers between devices, shards(): grad_in = a2a(grad_out)  14 us
    all_to_all x1, waiting for transfers between devices, shards(): incoming = a2a(outgoing)  12.4 us
    dot_general x2, matrix products, dot(): return lax.dot_general(a, b, (dims, ((), ())), preferred_element_type=F32)  9.09 us
    all_to_all x1, waiting for transfers between devices, shards(): back, grad_hidden = lax.optimization_barrier((a2a(returning), grad_hidden))  8.2 us
    pallas_call x1, Pallas kernels, shards(): pl.pallas_call(up_part_kernel, grid=(devices // group,), in_specs=[gather...  8.2 us
    pallas_call x1, Pallas kernels, shards(): pl.pallas_call(down_part_kernel, grid=(devices // group,), in_specs=[gath...  7.97 us
    all_to_all x1, starting transfers between devices, shards(): incoming = a2a(outgoing)  7.38 us
  transfers between devices with their start and end apart: 8, of which 3 were waited for; matrix products, arithmetic and copies ran while one was open for 12% of the time, Pallas kernels for 29%

profile of v2, /device:TPU:0, one launch (start us, length us, event | category | flops | bytes accessed | tf_op | source)
XLA Modules:
  0.0 138.2 jit_solution(774201608497869884)
XLA Ops:
  7.2 0.0 all-gather.5.cloned.1.call-start
  7.2 2.9 %shard_map.217 = (bf16[16,72,128]{2,1,0:T(8,128)(2,1)}, bf16[192,768]{1,0:T(8,128)(2,1)}) custom-call(bf16[180,768]{1,0:T(8,128)(2,1)} %bitcast.41, bf16[180,768]{1,0:T(8,128)(2,1)} %bitcast.45, f32[768]{0:T(1024)} %gain_hbm.5, f32[768]{0:T(1024)} %shift1_hbm.1, bf16[2,192,192]{2,1,0:T(8,128)(2,1)} %constant.58.clone.table_hbm), custom_call_target="tpu_custom_call" | custom-call | tf_op jit(solution)/shard_map/pallas_call | solution.py:382
  10.1 0.0 all-gather.5.cloned.1.call-update
  10.2 7.4 %all-to-all-start = ((bf16[16,72,128]{2,1,0:T(8,128)(2,1)}), bf16[16,72,128]{2,1,0:T(8,128)(2,1)S(1)}, u32[]{:S(2)}, u32[]{:S(2)}) async-start(bf16[16,72,128]{2,1,0:T(8,128)(2,1)} %get-tuple-element.24), calls=%async_computation | async-start | bytes 589824 | tf_op jit(solution)/shard_map/all_to_all | solution.py:460
  17.6 1.2 constant_dynamic-slice_fusion.5
  18.7 0.1 copy.35
  18.8 0.1 copy.36
  18.9 0.8 constant_dynamic-slice_fusion.4
  19.7 0.1 copy.38
  19.8 0.1 copy.39
  20.0 12.4 %all-to-all-done.in_ref = bf16[16,72,128]{2,1,0:T(8,128)(2,1)S(1)} async-done(((bf16[16,72,128]{2,1,0:T(8,128)(2,1)}), bf16[16,72,128]{2,1,0:T(8,128)(2,1)S(1)}, u32[]{:S(2)}, u32[]{:S(2)}) %all-to-all-start) | async-done | bytes 294944 | tf_op jit(solution)/shard_map/all_to_all | solution.py:460
  32.4 4.3 %shard_map.218 = (bf16[16,72,128]{2,1,0:T(8,128)(2,1)}, bf16[768,256]{1,0:T(8,128)(2,1)S(1)}, bf16[768,256]{1,0:T(8,128)(2,1)S(1)}, bf16[768,256]{1,0:T(8,128)(2,1)S(1)}, bf16[768,256]{1,0:T(8,128)(2,1)S(1)}) custom-call(bf16[16,72,128]{2,1,0:T(8,128)(2,1)S(1)} %all-to-all-done.in_ref, f32[256,256]{1,0:T(8,128)S(1)} %maximum_maximum_fusion.w1_ref, ...), custom_call_target="tpu_custom_call" | custom-call | tf_op jit(solution)/shard_map/pallas_call | solution.py:382
  36.7 0.0 copy-start.3
  36.7 0.7 copy-done.3
  37.5 0.8 copy-done.4
  38.2 0.8 copy-done.5
  39.0 0.8 copy-done.6
  39.8 3.5 %all-to-all-start.1 = ((bf16[16,72,128]{2,1,0:T(8,128)(2,1)}), bf16[16,72,128]{2,1,0:T(8,128)(2,1)S(1)}, u32[]{:S(2)}, u32[]{:S(2)}) async-start(bf16[16,72,128]{2,1,0:T(8,128)(2,1)} %get-tuple-element.25), calls=%async_computation.1 | async-start | bytes 589824 | tf_op jit(solution)/shard_map/all_to_all | solution.py:468
  43.3 0.0 all-gather.7.cloned.1.call-start
  43.4 5.0 %fusion.5.ghid_hbm = f32[192,3072]{1,0:T(8,128)} fusion(bf16[192,768]{1,0:T(8,128)(2,1)} %get-tuple-element.26.cot_hbm, bf16[768,3072]{1,0:T(8,128)(2,1)} %param.30), kind=kOutput, calls=%fused_computation.23 | convolution fusion | flops 905969664 | bytes 7372800 | tf_op jit(solution)/shard_map/dot_general | solution.py:21
  48.4 8.2 %all-to-all-done.1.in_ref = bf16[16,72,128]{2,1,0:T(8,128)(2,1)S(1)} async-done(((bf16[16,72,128]{2,1,0:T(8,128)(2,1)}), bf16[16,72,128]{2,1,0:T(8,128)(2,1)S(1)}, u32[]{:S(2)}, u32[]{:S(2)}) %all-to-all-start.1) | async-done | bytes 294944 | tf_op jit(solution)/shard_map/all_to_all | solution.py:468
  56.6 2.8 %shard_map.219 = (bf16[192,768]{1,0:T(8,128)(2,1)S(1)}, bf16[192,768]{1,0:T(8,128)(2,1)}) custom-call(bf16[16,72,128]{2,1,0:T(8,128)(2,1)S(1)} %all-to-all-done.1.in_ref, bf16[180,768]{1,0:T(8,128)(2,1)} %bitcast.42, f32[768]{0:T(1024)} %gain_hbm.5, f32[768]{0:T(1024)} %shift1_hbm.1, f32[768]{0:T(1024)} %gain_hbm.4, f32[768]{0:T(1024)} %shift2_hbm.1, ...), custom_call_target="tpu_custom_call" | custom-call | tf_op jit(solution)/shard_map/pallas_call | solution.py:382
  59.4 0.7 copy-done
  60.1 0.0 all-gather.7.cloned.1.call-update
  60.1 10.3 %shard_map.220 = (bf16[192,3072]{1,0:T(8,128)(2,1)S(1)}, f32[192,768]{1,0:T(8,128)S(1)}, bf16[16,72,128]{2,1,0:T(8,128)(2,1)}) custom-call(bf16[192,768]{1,0:T(8,128)(2,1)} %get-tuple-element.39.second_ref, bf16[192,768]{1,0:T(8,128)(2,1)} %copy-done, bf16[192,768]{1,0:T(8,128)(2,1)} %get-tuple-element.26.cot_hbm, f32[768]{0:T(1024)} %gain_hbm.4, ...), custom_call_target="tpu_custom_call" | custom-call | tf_op jit(solution)/shard_map/pallas_call | solution.py:382
  70.4 0.0 copy-start.2
  70.4 0.8 copy-done.2
  71.2 3.7 %all-to-all-start.2 = ((bf16[16,72,128]{2,1,0:T(8,128)(2,1)}), bf16[16,72,128]{2,1,0:T(8,128)(2,1)S(1)}, u32[]{:S(2)}, u32[]{:S(2)}) async-start(bf16[16,72,128]{2,1,0:T(8,128)(2,1)} %get-tuple-element.32), calls=%async_computation.2 | async-start | bytes 589824 | tf_op jit(solution)/shard_map/all_to_all | solution.py:486
  74.9 1.3 constant_dynamic-slice_fusion.2
  76.2 14.0 %all-to-all-done.2.in_ref = bf16[16,72,128]{2,1,0:T(8,128)(2,1)S(1)} async-done(((bf16[16,72,128]{2,1,0:T(8,128)(2,1)}), bf16[16,72,128]{2,1,0:T(8,128)(2,1)S(1)}, u32[]{:S(2)}, u32[]{:S(2)}) %all-to-all-start.2) | async-done | bytes 294944 | tf_op jit(solution)/shard_map/all_to_all | solution.py:486
  90.2 3.3 %shard_map.221 = (bf16[16,72,128]{2,1,0:T(8,128)(2,1)}, f32[2,2,96,96]{3,2,1,0:T(8,128)S(1)}) custom-call(bf16[16,72,128]{2,1,0:T(8,128)(2,1)S(1)} %all-to-all-done.2.in_ref, f32[256,256]{1,0:T(8,128)S(1)} %maximum_maximum_fusion.w1_ref, f32[256,256]{1,0:T(8,128)S(1)} %maximum_maximum_fusion.1.w2_ref, bf16[768,256]{1,0:T(8,128)(2,1)} %copy-done.3, ...), custom_call_target="tpu_custom_call" | custom-call | tf_op jit(solution)/shard_map/pallas_call | solution.py:382
  93.5 3.5 %all-to-all-start.3 = ((bf16[16,72,128]{2,1,0:T(8,128)(2,1)}), bf16[16,72,128]{2,1,0:T(8,128)(2,1)S(1)}, u32[]{:S(2)}, u32[]{:S(2)}) async-start(bf16[16,72,128]{2,1,0:T(8,128)(2,1)} %get-tuple-element.37), calls=%async_computation.3 | async-start | bytes 589824 | tf_op jit(solution)/shard_map/all_to_all | solution.py:494
  97.1 1.0 constant_dynamic-slice_fusion.3.up_ref
  98.0 0.8 dynamic_slice.33
  98.8 0.1 copy.31.bias_ref
  99.0 0.2 copy.40
  99.1 4.1 %fusion.6 = f32[192,768]{1,0:T(8,128)S(1)} fusion(bf16[192,3072]{1,0:T(8,128)(2,1)S(1)} %get-tuple-element.31, bf16[768,3072]{1,0:T(8,128)(2,1)} %param.30), kind=kOutput, calls=%fused_computation.24 | convolution fusion | flops 905969664 | bytes 6488064 | tf_op jit(solution)/shard_map/dot_general | solution.py:21
  103.2 0.3 collective-permute-start
  103.6 8.0 %shard_map.224 = bf16[768,192]{1,0:T(8,128)(2,1)} custom-call(bf16[16,192,768]{2,1,0:T(8,128)(2,1)} %bitcast.39, bf16[16,192,768]{2,1,0:T(8,128)(2,1)} %bitcast.37, bf16[192,768]{1,0:T(8,128)(2,1)S(1)} %constant_dynamic-slice_fusion.3.up_ref, f32[192,1]{1,0:T(8,128)S(1)} %copy.31.bias_ref), custom_call_target="tpu_custom_call" | custom-call | tf_op jit(solution)/shard_map/pallas_call | solution.py:519
  111.5 0.0 all-to-all-done.3.in_ref
  111.5 5.8 %all-to-all-start.4 = ((bf16[16,48,192]{2,1,0:T(8,128)(2,1)}), bf16[16,48,192]{2,1,0:T(8,128)(2,1)S(1)}, u32[]{:S(2)}, u32[]{:S(2)}) async-start(bf16[16,48,192]{2,1,0:T(8,128)(2,1)} %bitcast.15), calls=%async_computation.4 | async-start | bytes 786432 | tf_op jit(solution)/shard_map/all_to_all | solution.py:525
  117.4 0.8 fusion.2
  118.2 0.6 slice_bitcast_fusion
  118.8 2.7 %shard_map.222 = bf16[180,768]{1,0:T(8,128)(2,1)} custom-call(bf16[16,72,128]{2,1,0:T(8,128)(2,1)S(1)} %all-to-all-done.3.in_ref, bf16[180,768]{1,0:T(8,128)(2,1)} %bitcast.43, f32[768]{0:T(1024)} %gain_hbm.5, f32[192,768]{1,0:T(8,128)} %copy-done.2, bf16[2,192,192]{2,1,0:T(8,128)(2,1)} %constant.61.clone.table_hbm), custom_call_target="tpu_custom_call" | custom-call | tf_op jit(solution)/shard_map/pallas_call | solution.py:382
  121.5 8.2 %shard_map.223 = f32[192,768]{1,0:T(8,128)} custom-call(bf16[16,192,768]{2,1,0:T(8,128)(2,1)} %bitcast.40, bf16[16,192,768]{2,1,0:T(8,128)(2,1)} %bitcast.38, bf16[192,768]{1,0:T(8,128)(2,1)S(1)} %constant_dynamic-slice_fusion.3.up_ref, f32[192,1]{1,0:T(8,128)S(1)} %copy.31.bias_ref, bf16[192,768]{1,0:T(8,128)(2,1)S(1)} %bitcast.32), custom_call_target="tpu_custom_call" | custom-call | tf_op jit(solution)/shard_map/pallas_call | solution.py:527
  129.7 0.1 convert_bitcast_fusion
  129.8 0.5 copy.33
  130.3 1.1 reshape.32
  (22 shorter events, 0.1 us)
Async XLA Ops:
  7.2 52.9 %all-gather.5.cloned.1.call-start = ((), (), s32[]{:S(2)}) async-start(), calls=%async_computation.5 | async-start | bytes 5013504 | tf_op jit(solution)/shard_map/all_gather | solution.py:459
  10.2 22.3 %all-to-all-start = ((bf16[16,72,128]{2,1,0:T(8,128)(2,1)}), bf16[16,72,128]{2,1,0:T(8,128)(2,1)S(1)}, u32[]{:S(2)}, u32[]{:S(2)}) async-start(bf16[16,72,128]{2,1,0:T(8,128)(2,1)} %get-tuple-element.24), calls=%async_computation | async-start | bytes 589824 | tf_op jit(solution)/shard_map/all_to_all | solution.py:460
  36.7 0.7 copy-start.3
  37.5 0.8 copy-start.4
  38.2 0.8 copy-start.5
  39.0 0.8 copy-start.6
  39.8 16.8 %all-to-all-start.1 = ((bf16[16,72,128]{2,1,0:T(8,128)(2,1)}), bf16[16,72,128]{2,1,0:T(8,128)(2,1)S(1)}, u32[]{:S(2)}, u32[]{:S(2)}) async-start(bf16[16,72,128]{2,1,0:T(8,128)(2,1)} %get-tuple-element.25), calls=%async_computation.1 | async-start | bytes 589824 | tf_op jit(solution)/shard_map/all_to_all | solution.py:468
  43.3 60.2 %all-gather.7.cloned.1.call-start = ((), (), s32[]{:S(2)}) async-start(), calls=%async_computation.6 | async-start | bytes 5013504 | tf_op jit(solution)/shard_map/all_gather | solution.py:474
  59.4 0.7 copy-start
  70.4 0.8 copy-start.2
  71.2 19.0 %all-to-all-start.2 = ((bf16[16,72,128]{2,1,0:T(8,128)(2,1)}), bf16[16,72,128]{2,1,0:T(8,128)(2,1)S(1)}, u32[]{:S(2)}, u32[]{:S(2)}) async-start(bf16[16,72,128]{2,1,0:T(8,128)(2,1)} %get-tuple-element.32), calls=%async_computation.2 | async-start | bytes 589824 | tf_op jit(solution)/shard_map/all_to_all | solution.py:486
  93.5 18.0 %all-to-all-start.3 = ((bf16[16,72,128]{2,1,0:T(8,128)(2,1)}), bf16[16,72,128]{2,1,0:T(8,128)(2,1)S(1)}, u32[]{:S(2)}, u32[]{:S(2)}) async-start(bf16[16,72,128]{2,1,0:T(8,128)(2,1)} %get-tuple-element.37), calls=%async_computation.3 | async-start | bytes 589824 | tf_op jit(solution)/shard_map/all_to_all | solution.py:494
  103.2 14.9 %collective-permute-start = (f32[2,2,48,96]{3,2,1,0:T(8,128)S(1)}, f32[2,2,48,96]{3,2,1,0:T(8,128)S(1)}, u32[]{:S(2)}, u32[]{:S(2)}) collective-permute-start(f32[2,2,48,96]{3,2,1,0:T(8,128)S(1)} %dynamic-slice_bitcast_fusion), channel_id=1, source_target_pairs={{0,1},{1,0},{2,3},{3,2},{4,5},{5,4},{6,7},{7,6},{8,9},{9,8},{10,11... | collective-permute-start | bytes 221192 | tf_op jit(solution)/shard_map/ppermute | solution.py:508
  103.6 13.8 %copy-start.1 = (bf16[192,768]{1,0:T(8,128)(2,1)S(1)}, bf16[192,768]{1,0:T(8,128)(2,1)}, u32[]{:S(2)}) copy-start(bf16[192,768]{1,0:T(8,128)(2,1)} %copy-done) | copy-start | bytes 884740
  103.6 13.8 %copy-start.7 = (f32[768]{0:T(1024)S(1)}, f32[768]{0:T(1024)}, u32[]{:S(2)}) copy-start(f32[768]{0:T(1024)} %param.31) | copy-start | bytes 9220
  111.5 18.2 %all-to-all-start.4 = ((bf16[16,48,192]{2,1,0:T(8,128)(2,1)}), bf16[16,48,192]{2,1,0:T(8,128)(2,1)S(1)}, u32[]{:S(2)}, u32[]{:S(2)}) async-start(bf16[16,48,192]{2,1,0:T(8,128)(2,1)} %bitcast.15), calls=%async_computation.4 | async-start | bytes 786432 | tf_op jit(solution)/shard_map/all_to_all | solution.py:525
Sparse Core Ops, SparseCore 0:
  10.3 46.2 all-gather.4
  60.3 40.8 all-gather.6

commit v3 on v2

--- a/solution.py
+++ b/solution.py
@@ -263,18 +263,19 @@
     grads_ref[1, 1] = im
 
 
-def second_kernel(members, block, blocks, in_ref, x_hbm, gain1_hbm, shift1_hbm, gain2_hbm, shift2_hbm, table_hbm,
-                  resid_ref, second_ref, rows_ref, table_ref, x_ref, gain1_ref, shift1_ref, gain2_ref, shift2_ref,
+def second_kernel(members, block, blocks, in_hbm, x_hbm, gain1_hbm, shift1_hbm, gain2_hbm, shift2_hbm, table_hbm,
+                  up_hbm, resid_ref, second_ref, up_ref, in_ref, rows_ref, table_ref, x_ref, gain1_ref, shift1_ref, gain2_ref, shift2_ref,
                   sems):
     copies = fetch(((x_hbm, x_ref), (gain1_hbm, gain1_ref), (shift1_hbm, shift1_ref), (table_hbm, table_ref),
-                    (gain2_hbm, gain2_ref), (shift2_hbm, shift2_ref)), sems)
+                    (gain2_hbm, gain2_ref), (shift2_hbm, shift2_ref), (in_hbm, in_ref), (up_hbm, up_ref)), sems)
+    copies[6].wait()
     back = gather_blocks(in_ref, members, block, rows_ref)
     for copy in copies[:3]:
         copy.wait()
     x = x_ref[...].astype(F32)
     unit, _ = moments(x)
     x = pad_rows(x + (unit * gain1_ref[...][None] + shift1_ref[...][None]), resid_ref.shape[0])
-    for copy in copies[3:]:
+    for copy in copies[3:6]:
         copy.wait()
     filtered = compact(dot(table_ref[0], back) + dot(table_ref[1], back), block, blocks)
     residual = (x + filtered).astype(BF16)
@@ -282,39 +283,45 @@
     unit, _ = moments(residual.astype(F32))
     second = unit * gain2_ref[...][None] + shift2_ref[...][None]
     second_ref[...] = pad_rows(second[:x_ref.shape[0]], resid_ref.shape[0]).astype(BF16)
-
-
-def mlp_kernel(members, block, chunk, second_ref, resid_hbm, cot_hbm, gain_hbm, up_hbm, upb_hbm, ghid_hbm, table_hbm,
-               hid_ref, gres_ref, out_ref, acc_ref, resid_ref, cot_ref, gain_ref, up_ref, upb_ref, ghid_ref, table_ref,
+    copies[7].wait()
+
+
+def prepare_kernel(cot_hbm, down_hbm, ghid_ref, cot_ref, down_ref, sems):
+    for copy in fetch(((cot_hbm, cot_ref), (down_hbm, down_ref)), sems):
+        copy.wait()
+    ghid_ref[...] = dot(cot_ref[...], down_ref[...])
+
+
+def mlp_kernel(members, block, chunk, second_ref, up_ref, ghid_ref, resid_hbm, cot_hbm, gain_hbm, upb_hbm, table_hbm,
+               hid_hbm, gres_hbm, out_ref, acc_ref, hid_ref, gres_ref, resid_ref, cot_ref, gain_ref, upb_ref, table_ref,
                sems):
-    units = up_ref.shape[0]
-    parts = [slice(start, start + chunk) for start in range(0, units, chunk)]
-    pairs = [(upb_hbm, upb_ref)]
-    for part in parts:
-        pairs += [(up_hbm.at[part], up_ref.at[part]), (ghid_hbm.at[:, part], ghid_ref.at[:, part])]
-    tail = len(pairs)
-    pairs += [(resid_hbm, resid_ref), (cot_hbm, cot_ref), (gain_hbm, gain_ref), (table_hbm, table_ref)]
-    copies = fetch(pairs, sems)
+    copies = fetch(((upb_hbm, upb_ref), (resid_hbm, resid_ref), (cot_hbm, cot_ref), (gain_hbm, gain_ref),
+                    (table_hbm, table_ref)), sems)
     copies[0].wait()
-    for i, part in enumerate(parts):
-        copies[2 * i + 1].wait()
+    for start in range(0, up_ref.shape[0], chunk):
+        part = slice(start, start + chunk)
         pre = dot(second_ref[...], up_ref[part], ((1,), (1,))) + upb_ref[:, part]
         hidden, slope = gelu_and_slope(pre)
         hid_ref[:, part] = hidden.astype(BF16)
-        copies[2 * i + 2].wait()
         grad_pre = (ghid_ref[:, part] * slope).astype(BF16)
         term = dot(grad_pre, up_ref[part])
-        if i == 0:
+        if start == 0:
             acc_ref[...] = term
         else:
             acc_ref[...] += term
-    for copy in copies[tail:]:
+    hid_copy = pltpu.make_async_copy(hid_ref, hid_hbm, sems.at[5])
+    hid_copy.start()
+    for copy in copies[1:]:
         copy.wait()
     unit, scale = moments(resid_ref[...].astype(F32))
     grad = cot_ref[...].astype(F32) + norm_grad(unit, scale, acc_ref[...] * gain_ref[...][None])
     gres_ref[...] = grad
+    gres_copy = pltpu.make_async_copy(gres_ref, gres_hbm, sems.at[6])
+    gres_copy.start()
     wide = split(spread(grad, block))
     scatter_blocks(dot3((table_ref[0], table_ref[1]), wide), members, block, out_ref)
+    hid_copy.wait()
+    gres_copy.wait()
 
 
 def last_kernel(members, block, blocks, in_ref, x_hbm, gain_hbm, gres_hbm, table_hbm, out_ref, rows_ref, table_ref,
@@ -330,41 +337,74 @@
     out_ref[...] = (gres + norm_grad(unit, scale, (grad + gres) * gain_ref[...][None])).astype(BF16)
 
 
-def down_part_kernel(second_ref, cot_ref, up_ref, bias_ref, out_ref, acc_ref):
-    step = pl.program_id(0)
-    tokens = second_ref.shape[0] * second_ref.shape[1]
-    second = second_ref[...].reshape(tokens, -1)
-    hidden, _ = gelu_and_slope(dot(up_ref[...], second, ((1,), (1,))) + bias_ref[...])
-    term = dot(hidden.astype(BF16), cot_ref[...].reshape(tokens, -1))
-
-    @pl.when(step == 0)
-    def _():
-        acc_ref[...] = term
-
-    @pl.when(step > 0)
-    def _():
-        acc_ref[...] += term
-
-    @pl.when(step == pl.num_programs(0) - 1)
-    def _():
-        out_ref[...] = acc_ref[...].T.astype(BF16)
-
-
-def up_part_kernel(second_ref, cot_ref, up_ref, bias_ref, down_ref, out_ref):
-    step = pl.program_id(0)
-    tokens = second_ref.shape[0] * second_ref.shape[1]
-    second = second_ref[...].reshape(tokens, -1)
-    _, slope = gelu_and_slope(dot(up_ref[...], second, ((1,), (1,))) + bias_ref[...])
-    grad_hidden = dot(down_ref[...], cot_ref[...].reshape(tokens, -1), ((1,), (1,)))
-    term = dot((grad_hidden * slope).astype(BF16), second)
-
-    @pl.when(step == 0)
-    def _():
-        out_ref[...] = term
-
-    @pl.when(step > 0)
-    def _():
-        out_ref[...] += term
+def token_chunks(ref, width=384):
+    tokens = ref.shape[0]
+    return [slice(start, min(start + width, tokens)) for start in range(0, tokens, width)]
+
+
+def fetch_blocks(blocks, ref, sems, base):
+    size = ref.shape[0] // len(blocks)
+    copies = []
+    for i, block in enumerate(blocks):
+        copy = pltpu.make_async_copy(block, ref.at[i * size:(i + 1) * size], sems.at[base + i])
+        copy.start()
+        copies += [copy]
+    return copies
+
+
+def wait_blocks(copies, part, size):
+    for i in range(part.start // size, part.stop // size):
+        copies[i].wait()
+
+
+def grads_kernel(count, has_terms, spill, *refs):
+    refs = list(refs)
+    take = lambda n: [refs.pop(0) for _ in range(n)]
+    seconds, cots = take(count), take(count)
+    up_ref, bias_ref, down_ref, _ = take(4)
+    terms = take(2 * has_terms)
+    outs = take(2)
+    second_ref, cot_ref, sums_ref, sems = take(4)
+    size = second_ref.shape[0] // count
+    second_copies = fetch_blocks(seconds, second_ref, sems, 0)
+    cot_copies = fetch_blocks(cots, cot_ref, sems, count)
+    term_copies = [
+        pltpu.make_async_copy(term, sums_ref.at[i], sems.at[2 * count + i]) for i, term in enumerate(terms)]
+    for copy in term_copies:
+        copy.start()
+    sums = [0.0, 0.0]
+    for part in token_chunks(second_ref):
+        wait_blocks(second_copies, part, size)
+        hidden, slope = gelu_and_slope(dot(up_ref[...], second_ref[part], ((1,), (1,))) + bias_ref[...])
+        wait_blocks(cot_copies, part, size)
+        sums[0] = sums[0] + dot(hidden.astype(BF16), cot_ref[part])
+        grad_hidden = dot(down_ref[...], cot_ref[part], ((1,), (1,)))
+        sums[1] = sums[1] + dot((grad_hidden * slope).astype(BF16), second_ref[part])
+    for copy in term_copies:
+        copy.wait()
+    half = sums[0].shape[0] // 2
+    out_copies = []
+    for i, (out, total) in enumerate(zip(outs, sums)):
+        if has_terms:
+            total = total + jnp.concatenate((sums_ref[i, 0], sums_ref[i, 1]), axis=0)
+        target = sums_ref.at[i] if spill else out
+        target[0] = total[:half]
+        target[1] = total[half:]
+        if spill:
+            out_copies += [pltpu.make_async_copy(sums_ref.at[i], out, sems.at[2 * count + i])]
+            out_copies[-1].start()
+    for copy in out_copies:
+        copy.wait()
+
+
+def join_kernel(in_ref, out_ref):
+    width = in_ref.shape[2]
+    for d in range(in_ref.shape[0]):
+        out_ref[:, d * width:(d + 1) * width] = in_ref[d].astype(F32)
+
+
+def turn_kernel(own_ref, other_ref, out_ref):
+    out_ref[...] = (own_ref[...] + other_ref[...]).T.astype(BF16)
 
 
 def struct(shape, dtype):
@@ -372,15 +412,27 @@
 
 
 VMEM = pl.BlockSpec(memory_space=pltpu.VMEM)
+PINNED = pl.BlockSpec(memory_space=pltpu.VMEM)
 HBM = pl.BlockSpec(memory_space=pltpu.HBM)
-
-
-def call(kernel, out, scratch, in_specs, *args, out_specs=None, limit=24):
+EITHER = pl.BlockSpec(memory_space=pl.ANY)
+
+
+def call(kernel, out, scratch, in_specs, *args, out_specs=None, limit=12, cost=1):
     if out_specs is None:
         out_specs = jax.tree.map(lambda _: VMEM, out)
-    args = [pltpu.with_memory_space_constraint(a, pltpu.HBM) if spec is HBM else a for a, spec in zip(args, in_specs)]
+    flat = out_specs if isinstance(out_specs, tuple) else (out_specs,)
+    shapes = out if isinstance(out, tuple) else (out,)
+    shapes = tuple(
+        pltpu.HBM(o.shape, o.dtype) if spec is HBM else pltpu.VMEM(o.shape, o.dtype) if spec is PINNED else o
+        for o, spec in zip(shapes, flat))
+    out = shapes if isinstance(out, tuple) else shapes[0]
+    spaces = {id(HBM): pltpu.HBM, id(PINNED): pltpu.VMEM}
+    args = [
+        pltpu.with_memory_space_constraint(a, spaces[id(spec)]) if id(spec) in spaces else a
+        for a, spec in zip(args, in_specs)]
     return pl.pallas_call(
         kernel, out_shape=out, scratch_shapes=scratch, in_specs=in_specs, out_specs=out_specs,
+        cost_estimate=pl.CostEstimate(flops=cost, transcendentals=0, bytes_accessed=cost),
         compiler_params=pltpu.CompilerParams(vmem_limit_bytes=limit << 20))(*args)
 
 
@@ -390,8 +442,23 @@
     for row in range(4):
         columns = list(range(1, width))
         chips += [row * width + c for c in (columns if row % 2 == 0 else columns[::-1])]
-    chips += [row * width for row in (3, 2, 1, 0)]
-    return [2 * chip + core for chip in chips for core in (0, 1)]
+    return chips + [row * width for row in (3, 2, 1, 0)]
+
+
+class Ring:
+    def __init__(self, devices):
+        chips = ring_order(devices)
+        count = len(chips)
+        ahead = [(chips[i], chips[(i + 1) % count]) for i in range(count)]
+        forward = [(2 * a, 2 * b) for a, b in ahead] + [(2 * b + 1, 2 * a + 1) for a, b in ahead]
+        self.forward, self.backward = forward, [(b, a) for a, b in forward]
+        self.steps = count // 2
+
+    def step(self, blocks, number):
+        out = [lax.ppermute(blocks[0], "lat", self.forward)]
+        if number < self.steps:
+            out += [lax.ppermute(blocks[-1], "lat", self.backward)]
+        return out
 
 
 def complex_weight(weight, block):
@@ -429,8 +496,8 @@
     units = up_weight.shape[0]
     tokens = -(-length // 64) * 64
     x = block_input[0]
-    ring = [ring_order(devices)]
-    all_gather = partial(lax.all_gather, axis_name="lat", axis=0, axis_index_groups=ring)
+    ring = Ring(devices)
+    third = max(ring.steps - 1, 1)
     a2a = partial(lax.all_to_all, axis_name="lat", split_axis=0, concat_axis=0, tiled=True)
 
     fwd = np.pad(lon_table(length, members, per_member, False), ((0, 0), (0, tokens - length)))
@@ -456,79 +523,112 @@
     outgoing, cot = call(
         partial(first_kernel, members, block), (packed, token), [short, short, row, row, table_scratch, sems(5)],
         [HBM] * 5, x, cotangent[0], first_gain, first_shift, host_split(fwd))
-    cot_all = all_gather(cot)
-    incoming = a2a(outgoing)
-    grad_hidden = dot(cot, down_weight)
+    cots = [[cot], ring.step([cot], 1)]
+    share = units // devices
+    begin = (index // 2) * 2 * share
+    up_own = lax.dynamic_slice_in_dim(up_weight, begin, 2 * share, 0)
+    bias_own = lax.dynamic_slice_in_dim(up_bias, begin, 2 * share, 0)[:, None]
+    down_own = lax.dynamic_slice_in_dim(down_weight, begin, 2 * share, 1).T
+    incoming, cots[1], up_own, bias_own, down_own = lax.optimization_barrier(
+        (a2a(outgoing), cots[1], up_own, bias_own, down_own))
+    full = pltpu.VMEM((tokens, channels), BF16)
+    grad_hidden = call(
+        prepare_kernel, struct((tokens, units), F32),
+        [full, pltpu.VMEM(down_weight.shape, BF16), sems(2)], [HBM] * 2, cot, down_weight, out_specs=PINNED)
     spectral = struct((devices * per_member, 2 * LANES), BF16)
     kept_scratch = [pltpu.VMEM(spectral.shape, BF16)] * 4 + [sems(4)]
     spectral_scratch = [pltpu.VMEM(spectral.shape, F32), pltpu.VMEM((devices, rows, LANES), F32)] + kept_scratch
     returning, *kept = call(
         partial(filter_kernel, block), (packed, spectral, spectral, spectral, spectral), spectral_scratch,
         [VMEM] * 5, incoming, w1, b1, w2, b2, out_specs=(VMEM, HBM, HBM, HBM, HBM))
+    for number in range(2, third + 1):
+        cots += [ring.step(cots[-1], number)]
     back, grad_hidden = lax.optimization_barrier((a2a(returning), grad_hidden))
-    residual, second = call(
-        partial(second_kernel, members, block, blocks), (token, token),
-        [row_scratch, back_scratch, short, row, row, row, row, sems(6)], [VMEM] + [HBM] * 6,
-        back, x, first_gain, first_shift, second_gain, second_shift, host_split(inv.T))
-    second_out, cot_all = lax.optimization_barrier((second, cot_all))
-    second_all = all_gather(second_out)
-
-    chunk = 512
-    full = pltpu.VMEM((tokens, channels), BF16)
+    grad_hidden, cots[2:] = lax.optimization_barrier((grad_hidden, cots[2:]))
+    residual, second, up_near = call(
+        partial(second_kernel, members, block, blocks), (token, token, struct(up_weight.shape, BF16)),
+        [pltpu.VMEM(packed.shape, BF16), row_scratch, back_scratch, short, row, row, row, row, sems(8)],
+        [EITHER] + [HBM] * 7,
+        back, x, first_gain, first_shift, second_gain, second_shift, host_split(inv.T), up_weight,
+        out_specs=(VMEM, VMEM, PINNED))
+    seconds = [[second], ring.step([second], 1)]
+
+    chunk = 768
     hidden, grad_resid, grad_out = call(
         partial(mlp_kernel, members, block, chunk),
         (struct((tokens, units), BF16), struct((tokens, channels), F32), packed),
-        [pltpu.VMEM((tokens, channels), F32), full, full, row, pltpu.VMEM((units, channels), BF16),
-         pltpu.VMEM((1, units), F32), pltpu.VMEM((tokens, units), F32), table_scratch,
-         sems(2 * (units // chunk) + 5)],
-        [VMEM] + [HBM] * 7,
-        second, residual, cot, second_gain, up_weight, up_bias[None], grad_hidden, host_split(inv), limit=32)
-    grad_in = a2a(grad_out)
+        [pltpu.VMEM((tokens, channels), F32), pltpu.VMEM((tokens, units), BF16), pltpu.VMEM((tokens, channels), F32),
+         full, full, row, pltpu.VMEM((1, units), F32), table_scratch, sems(7)],
+        [VMEM, PINNED, PINNED] + [HBM] * 5,
+        second, up_near, grad_hidden, residual, cot, second_gain, up_bias[None], host_split(inv),
+        out_specs=(HBM, HBM, VMEM), limit=20)
     block_output = (
         residual.astype(F32) + dot(hidden, down_weight, ((1,), (1,))) + down_bias
     ).astype(BF16)[None, :length]
-
-    grad_back, terms = call(
+    seconds[1], _ = lax.optimization_barrier((seconds[1], grad_out))
+    for number in range(2, third):
+        seconds += [ring.step(seconds[-1], number)]
+    grad_in, cots[third] = lax.optimization_barrier((a2a(grad_out), cots[third]))
+    cots += [ring.step(cots[-1], ring.steps)]
+
+    grad_back, squares = call(
         partial(filter_grad_kernel, block), (packed, struct((2, 2, block, block), F32)), spectral_scratch,
         [VMEM] * 3 + [HBM] * 4, grad_in, w1, w2, *kept)
+    seconds[2:], _ = lax.optimization_barrier((seconds[2:], grad_back))
+    seconds += [ring.step(seconds[-1], third)]
     grad_lon = a2a(grad_back)
+    seconds += [ring.step(seconds[-1], ring.steps)]
+    part = block // members
+    squares = squares.reshape(2, 2, members, part, block)
+    member = index % members
+    def piece(which):
+        return lax.dynamic_index_in_dim(squares, which, 2, keepdims=False)
+    total = piece(member)
+    for hop in range(1, members):
+        pairs = [(d, d - d % members + (d % members + hop) % members) for d in range(devices)]
+        total = total + lax.ppermute(piece((member + hop) % members), "lat", pairs)
+
+    seconds = [block for step in seconds for block in step]
+    cots = [block for step in cots for block in step]
+    last = len(seconds) - 3
+    halves = struct((2, share, channels), F32)
+
+    def grads(low, high, terms, after, spill=False):
+        count = high - low
+        stack = pltpu.VMEM((count * tokens, channels), BF16)
+        sums = pltpu.VMEM((2,) + halves.shape, F32)
+        return call(
+            partial(grads_kernel, count, terms is not None, spill), (halves, halves),
+            [stack, stack, sums, sems(2 * count + 2)],
+            [HBM] * (2 * count) + [VMEM] * 3 + [EITHER] + [HBM] * len(terms or ()),
+            *seconds[low:high], *cots[low:high], up_own, bias_own, down_own, after, *(terms or ()),
+            out_specs=(HBM, HBM) if spill else None, limit=24)
+
+    terms = None
+    for low in range(0, last, 5):
+        terms = grads(low, min(low + 5, last), terms, grad_back, True)
+    grad_lon, seconds[-1], total = lax.optimization_barrier((grad_lon, seconds[-1], total))
+    down_term, up_term = grads(last, last + 3, terms, grad_lon)
+    core = index % 2
+    swap = [(d, d ^ 1) for d in range(devices)]
+
+    def halved(term):
+        mine = lax.dynamic_index_in_dim(term, core, 0, keepdims=False)
+        other = lax.dynamic_index_in_dim(term, 1 - core, 0, keepdims=False)
+        return mine, lax.ppermute(other, "lat", swap)
+
     input_grad = call(
         partial(last_kernel, members, block, blocks), struct((length, channels), BF16),
         [row_scratch, back_scratch, short, row, pltpu.VMEM((tokens, channels), F32), sems(4)], [VMEM] + [HBM] * 4,
         grad_lon, x, first_gain, grad_resid, host_split(fwd.T))[None]
-
-    part = block // members
-    terms = terms.reshape(2, 2, members, part, block)
-    member = index % members
-    def piece(which):
-        return lax.dynamic_index_in_dim(terms, which, 2, keepdims=False)
-    total = piece(member)
-    for hop in range(1, members):
-        pairs = [(d, d - d % members + (d % members + hop) % members) for d in range(devices)]
-        total = total + lax.ppermute(piece((member + hop) % members), "lat", pairs)
-
-    share = units // devices
-    up_own = lax.dynamic_slice_in_dim(up_weight, index * share, share, 0)
-    bias_own = lax.dynamic_slice_in_dim(up_bias, index * share, share, 0)[:, None]
-    down_own = lax.dynamic_slice_in_dim(down_weight, index * share, share, 1).T
-    group = 4 if devices % 4 == 0 else 1
-    whole = lambda shape: pl.BlockSpec(shape, lambda i: (0,) * len(shape))
-    gathered = pl.BlockSpec((group, tokens, channels), lambda i: (i, 0, 0))
-    params = pltpu.CompilerParams(vmem_limit_bytes=24 << 20)
-    gathered_pair = [pltpu.with_memory_space_constraint(array, pltpu.HBM) for array in (second_all, cot_all)]
-    down_part = pl.pallas_call(
-        down_part_kernel, grid=(devices // group,),
-        in_specs=[gathered, gathered, whole((share, channels)), whole((share, 1))],
-        out_specs=whole((channels, share)), out_shape=struct((channels, share), BF16),
-        scratch_shapes=[pltpu.VMEM((share, channels), F32)], compiler_params=params,
-    )(*gathered_pair, up_own, bias_own)
+    down_mine, down_other = halved(down_term)
+    down_mine, input_grad = lax.optimization_barrier((down_mine, input_grad))
+    down_part = call(turn_kernel, struct((channels, share), BF16), [], [VMEM] * 2, down_mine, down_other)
     down_rows = a2a(down_part.reshape(devices, channels // devices, share))
-    down_grad = down_rows.transpose(1, 0, 2).reshape(channels // devices, units).astype(F32)
-    up_grad = pl.pallas_call(
-        up_part_kernel, grid=(devices // group,),
-        in_specs=[gathered, gathered, whole((share, channels)), whole((share, 1)), whole((share, channels))],
-        out_specs=whole((share, channels)), out_shape=struct((share, channels), F32), compiler_params=params,
-    )(*gathered_pair, up_own, bias_own, down_own)
+    up_mine, up_other = halved(up_term)
+    down_rows, up_other = lax.optimization_barrier((down_rows, up_other))
+    down_grad = call(join_kernel, struct((channels // devices, units), F32), [], [VMEM], down_rows)
+    up_grad = up_mine + up_other
     return (block_output, input_grad, up_grad, down_grad, total[0], total[1])
 
 

time: 139 us -> 130 us (0.935)
  starting transfers between devices: 24.4 us -> 38.1 us
  between operations: 14.4 us -> 1.24 us
  matrix products: 9.09 us -> 4.08 us
  waiting for transfers between devices: 34.6 us -> 31.3 us
  local copies, waits for them, and re-layouts: 12.4 us -> 10.1 us
    pallas_call x2 -> x0, Pallas kernels: 16.2 us -> none  [the longest x1 8.2 us: shards(): pl.pallas_call(up_part_kernel, grid=(devices // group,), in_specs=[gather...]
    pallas_call x6 -> x11, Pallas kernels: 26.3 us -> 42.4 us  [call(): pl.pallas_call(kernel, out_shape=out, scratch_shapes=scratch, in_specs=in...]
    ppermute x0 -> x16, starting transfers between devices: none -> 14.6 us  [the longest x8 7.29 us: step(): out = [lax.ppermute(blocks[0], 'lat', self.forward)]]
    all_to_all x2, waiting for transfers between devices: 26.4 us -> 13.3 us  [the longest x1 8.73 us: shards(): a2a(grad_out)]
    all_to_all x1, waiting for transfers between devices: 0.01 us -> 6.63 us  [shards(): down_rows = a2a(down_part.reshape(devices, channels // devices, share))]
    ppermute x0 -> x16, waiting for transfers between devices: none -> 6.06 us  [the longest x8 5.72 us: step(): out = [lax.ppermute(blocks[0], 'lat', self.forward)]]
    dot_general x2 -> x1, matrix products: 9.09 us -> 4.08 us  [dot(): return lax.dot_general(a, b, (dims, ((), ())), preferred_element_type=F32)]
    all_to_all x1, waiting for transfers between devices: 8.2 us -> 5.34 us  [shards(): back, grad_hidden = lax.optimization_barrier((a2a(returning), grad_hidden))]
  transfers between devices with their start and end apart: 8 -> 22, of which waited for: 3 -> 8; matrix products, arithmetic and copies ran while one was open for 12% -> 9% of each run, Pallas kernels for 29% -> 26%
where the time goes in v3:
time: 130 us; the launch traced here: 129 us
  Pallas kernels  42.4 us (33%)
  starting transfers between devices  38.1 us (29%)
  waiting for transfers between devices  31.3 us (24%)
  local copies, waits for them, and re-layouts  10.1 us (8%)
  matrix products  4.08 us (3%)
  other arithmetic  1.74 us (1%)
    pallas_call x11, Pallas kernels, call(): pl.pallas_call(kernel, out_shape=out, scratch_shapes=scratch, in_specs=in...  42.4 us
    all_to_all x1, waiting for transfers between devices, shards(): a2a(grad_out)  8.73 us
    ppermute x8, starting transfers between devices, step(): out = [lax.ppermute(blocks[0], 'lat', self.forward)]  7.29 us
    ppermute x6, starting transfers between devices, step(): out += [lax.ppermute(blocks[-1], 'lat', self.backward)]  6.78 us
    all_to_all x1, waiting for transfers between devices, shards(): down_rows = a2a(down_part.reshape(devices, channels // devices, share))  6.63 us
    all_to_all x1, starting transfers between devices, shards(): a2a(outgoing)  6.29 us
    ppermute x8, waiting for transfers between devices, step(): out = [lax.ppermute(blocks[0], 'lat', self.forward)]  5.72 us
    all_to_all x1, waiting for transfers between devices, shards(): back, grad_hidden = lax.optimization_barrier((a2a(returning), grad_hidden))  5.34 us
  transfers between devices with their start and end apart: 22, of which 8 were waited for; matrix products, arithmetic and copies ran while one was open for 9% of the time, Pallas kernels for 26%

profile of v3, /device:TPU:0, one launch (start us, length us, event | category | flops | bytes accessed | tf_op | source)
XLA Modules:
  0.0 129.0 jit_solution(17157486089325874878)
XLA Ops:
  0.6 2.8 %shard_map.217 = (bf16[16,72,128]{2,1,0:T(8,128)(2,1)}, bf16[192,768]{1,0:T(8,128)(2,1)S(1)}) custom-call(bf16[180,768]{1,0:T(8,128)(2,1)} %bitcast.39, bf16[180,768]{1,0:T(8,128)(2,1)} %bitcast.43, f32[768]{0:T(1024)} %gain_hbm.5, f32[768]{0:T(1024)} %shift1_hbm.1, bf16[2,192,192]{2,1,0:T(8,128)(2,1)} %constant.75.clone.table_hbm), custom_call_target="tpu_custom_call" | custom-call | flops 1 | bytes 1 | tf_op jit(solution)/shard_map/pallas_call | solution.py:433
  3.5 3.0 %collective-permute-start = (bf16[192,768]{1,0:T(8,128)(2,1)S(1)}, bf16[192,768]{1,0:T(8,128)(2,1)S(1)}, u32[]{:S(2)}, u32[]{:S(2)}) collective-permute-start(bf16[192,768]{1,0:T(8,128)(2,1)S(1)} %get-tuple-element.53.cot_hbm.refs_5_), channel_id=1, source_target_pairs={{2,6},{6,10},{10,14},{14,12},{12,8},{8,4},{4,0},{0,2},{7,3},{11,7}... | collective-permute-start | bytes 884744 | tf_op jit(solution)/shard_map/ppermute | solution.py:458
  6.6 6.3 %all-to-all-start = ((bf16[16,72,128]{2,1,0:T(8,128)(2,1)}), bf16[16,72,128]{2,1,0:T(8,128)(2,1)S(1)}, u32[]{:S(2)}, u32[]{:S(2)}) async-start(bf16[16,72,128]{2,1,0:T(8,128)(2,1)} %get-tuple-element.52), calls=%async_computation | async-start | bytes 589824 | tf_op jit(solution)/shard_map/all_to_all | solution.py:533
  12.9 1.2 constant_dynamic-slice_fusion.3
  14.5 1.2 constant_dynamic-slice_fusion.6
  15.7 0.8 constant_dynamic-slice_fusion.2
  16.5 0.3 copy.32
  16.8 0.8 dynamic_slice.42
  17.7 1.2 constant_dynamic-slice_fusion.7.refs_10_.refs_6_
  18.9 4.6 %all-to-all-done.in_ref = bf16[16,72,128]{2,1,0:T(8,128)(2,1)S(1)} async-done(((bf16[16,72,128]{2,1,0:T(8,128)(2,1)}), bf16[16,72,128]{2,1,0:T(8,128)(2,1)S(1)}, u32[]{:S(2)}, u32[]{:S(2)}) %all-to-all-start) | async-done | bytes 294944 | tf_op jit(solution)/shard_map/all_to_all | solution.py:533
  23.5 2.0 %collective-permute-start.3 = (bf16[192,768]{1,0:T(8,128)(2,1)S(1)}, bf16[192,768]{1,0:T(8,128)(2,1)}, u32[]{:S(2)}, u32[]{:S(2)}) collective-permute-start(bf16[192,768]{1,0:T(8,128)(2,1)S(1)} %collective-permute-done.1.refs_7_), channel_id=1, source_target_pairs={{6,2},{10,6},{14,10},{12,14},{8,12},{4,8},{0,4},{2,0},{3,7},{7,11}... | collective-permute-start | bytes 884744 | tf_op jit(solution)/shard_map/ppermute | solution.py:460
  25.5 4.3 %shard_map.218 = (bf16[16,72,128]{2,1,0:T(8,128)(2,1)}, bf16[768,256]{1,0:T(8,128)(2,1)}, bf16[768,256]{1,0:T(8,128)(2,1)}, bf16[768,256]{1,0:T(8,128)(2,1)}, bf16[768,256]{1,0:T(8,128)(2,1)}) custom-call(bf16[16,72,128]{2,1,0:T(8,128)(2,1)S(1)} %all-to-all-done.in_ref, f32[256,256]{1,0:T(8,128)S(1)} %maximum_maximum_fusion.w1_ref, f32[1,256]{1,0:T(1,128)S(1)} %bitcast.37, ...), custom_call_target="tpu_custom_call" | custom-call | flops 1 | bytes 1 | tf_op jit(solution)/shard_map/pallas_call | solution.py:433
  29.8 4.2 %all-to-all-start.1 = ((bf16[16,72,128]{2,1,0:T(8,128)(2,1)}), bf16[16,72,128]{2,1,0:T(8,128)(2,1)}, u32[]{:S(2)}, u32[]{:S(2)}) async-start(bf16[16,72,128]{2,1,0:T(8,128)(2,1)} %get-tuple-element.55), calls=%async_computation.1 | async-start | bytes 589824 | tf_op jit(solution)/shard_map/all_to_all | solution.py:546
  34.0 1.8 %collective-permute-start.4 = (bf16[192,768]{1,0:T(8,128)(2,1)}, bf16[192,768]{1,0:T(8,128)(2,1)}, u32[]{:S(2)}, u32[]{:S(2)}) collective-permute-start(bf16[192,768]{1,0:T(8,128)(2,1)} %collective-permute-done.2.refs_8_), channel_id=1, source_target_pairs={{2,6},{6,10},{10,14},{14,12},{12,8},{8,4},{4,0},{0,2},{7,3},{11,7}... | collective-permute-start | bytes 884744 | tf_op jit(solution)/shard_map/ppermute | solution.py:458
  35.9 0.3 collective-permute-start.5
  36.2 3.6 %shard_map.219.ghid_ref = f32[192,3072]{1,0:T(8,128)S(1)} custom-call(bf16[192,768]{1,0:T(8,128)(2,1)} %copy-done, bf16[768,3072]{1,0:T(8,128)(2,1)} %down_hbm.1), custom_call_target="tpu_custom_call" | custom-call | flops 1 | bytes 1 | tf_op jit(solution)/shard_map/pallas_call | solution.py:433
  39.7 5.3 %all-to-all-done.1.in_hbm = bf16[16,72,128]{2,1,0:T(8,128)(2,1)} async-done(((bf16[16,72,128]{2,1,0:T(8,128)(2,1)}), bf16[16,72,128]{2,1,0:T(8,128)(2,1)}, u32[]{:S(2)}, u32[]{:S(2)}) %all-to-all-start.1) | async-done | bytes 294944 | tf_op jit(solution)/shard_map/all_to_all | solution.py:546
  45.1 3.5 %shard_map.220 = (bf16[192,768]{1,0:T(8,128)(2,1)S(1)}, bf16[192,768]{1,0:T(8,128)(2,1)}, bf16[3072,768]{1,0:T(8,128)(2,1)S(1)}) custom-call(bf16[16,72,128]{2,1,0:T(8,128)(2,1)} %all-to-all-done.1.in_hbm, bf16[180,768]{1,0:T(8,128)(2,1)} %bitcast.40, f32[768]{0:T(1024)} %gain_hbm.5, f32[768]{0:T(1024)} %shift1_hbm.1, f32[768]{0:T(1024)} %gain_hbm.4, ...), custom_call_target="tpu_custom_call" | custom-call | flops 1 | bytes 1 | tf_op jit(solution)/shard_map/pallas_call | solution.py:433
  48.6 0.7 copy-done.7
  49.3 2.0 %collective-permute-start.7 = (bf16[192,768]{1,0:T(8,128)(2,1)}, bf16[192,768]{1,0:T(8,128)(2,1)}, u32[]{:S(2)}, u32[]{:S(2)}) collective-permute-start(bf16[192,768]{1,0:T(8,128)(2,1)} %get-tuple-element.58.second_ref.refs_0_), channel_id=1, source_target_pairs={{6,2},{10,6},{14,10},{12,14},{8,12},{4,8},{0,4},{2,0},{3,7},{7,11}... | collective-permute-start | bytes 884744 | tf_op jit(solution)/shard_map/ppermute | solution.py:460
  51.3 7.1 %shard_map.221 = (bf16[192,3072]{1,0:T(8,128)(2,1)}, f32[192,768]{1,0:T(8,128)}, bf16[16,72,128]{2,1,0:T(8,128)(2,1)S(1)}) custom-call(bf16[192,768]{1,0:T(8,128)(2,1)} %get-tuple-element.58.second_ref.refs_0_, bf16[3072,768]{1,0:T(8,128)(2,1)S(1)} %get-tuple-element.59.up_ref, f32[192,3072]{1,0:T(8,128)S(1)} %shard_map.219.ghid_ref, ...), custom_call_target="tpu_custom_call" | custom-call | flops 1 | bytes 1 | tf_op jit(solution)/shard_map/pallas_call | solution.py:433
  58.4 0.7 copy-done.9
  59.2 3.5 %all-to-all-start.2 = ((bf16[16,72,128]{2,1,0:T(8,128)(2,1)}), bf16[16,72,128]{2,1,0:T(8,128)(2,1)S(1)}, u32[]{:S(2)}, u32[]{:S(2)}) async-start(bf16[16,72,128]{2,1,0:T(8,128)(2,1)} %copy-done.9), calls=%async_computation.2 | async-start | bytes 589824 | tf_op jit(solution)/shard_map/all_to_all | solution.py:571
  62.7 2.0 %collective-permute-start.8 = (bf16[192,768]{1,0:T(8,128)(2,1)}, bf16[192,768]{1,0:T(8,128)(2,1)S(1)}, u32[]{:S(2)}, u32[]{:S(2)}) collective-permute-start(bf16[192,768]{1,0:T(8,128)(2,1)} %collective-permute-done.6.refs_1_), channel_id=1, source_target_pairs={{2,6},{6,10},{10,14},{14,12},{12,8},{8,4},{4,0},{0,2},{7,3},{11,7}... | collective-permute-start | bytes 884744 | tf_op jit(solution)/shard_map/ppermute | solution.py:458
  65.0 8.7 %all-to-all-done.2.in_ref = bf16[16,72,128]{2,1,0:T(8,128)(2,1)S(1)} async-done(((bf16[16,72,128]{2,1,0:T(8,128)(2,1)}), bf16[16,72,128]{2,1,0:T(8,128)(2,1)S(1)}, u32[]{:S(2)}, u32[]{:S(2)}) %all-to-all-start.2) | async-done | bytes 294944 | tf_op jit(solution)/shard_map/all_to_all | solution.py:571
  73.7 0.9 copy-done.2
  74.7 0.9 copy-done.4
  75.6 3.3 %shard_map.222 = (bf16[16,72,128]{2,1,0:T(8,128)(2,1)}, f32[2,2,96,96]{3,2,1,0:T(8,128)S(1)}) custom-call(bf16[16,72,128]{2,1,0:T(8,128)(2,1)S(1)} %all-to-all-done.2.in_ref, f32[256,256]{1,0:T(8,128)S(1)} %copy-done.2, f32[256,256]{1,0:T(8,128)S(1)} %copy-done.4, bf16[768,256]{1,0:T(8,128)(2,1)} %get-tuple-element.71.spec_hbm, ...), custom_call_target="tpu_custom_call" | custom-call | flops 1 | bytes 1 | tf_op jit(solution)/shard_map/pallas_call | solution.py:433
  79.0 3.8 %all-to-all-start.3 = ((bf16[16,72,128]{2,1,0:T(8,128)(2,1)}), bf16[16,72,128]{2,1,0:T(8,128)(2,1)S(1)}, u32[]{:S(2)}, u32[]{:S(2)}) async-start(bf16[16,72,128]{2,1,0:T(8,128)(2,1)} %get-tuple-element.75.refs_13_), calls=%async_computation.3 | async-start | bytes 589824 | tf_op jit(solution)/shard_map/all_to_all | solution.py:579
  82.8 0.4 collective-permute-start.13
  83.3 2.4 %collective-permute-done.10.refs_0_ = bf16[192,768]{1,0:T(8,128)(2,1)S(1)} collective-permute-done((bf16[192,768]{1,0:T(8,128)(2,1)S(1)}, bf16[192,768]{1,0:T(8,128)(2,1)S(1)}, u32[]{:S(2)}, u32[]{:S(2)}) %collective-permute-start.10) | collective-permute-done | bytes 294944 | tf_op jit(solution)/shard_map/ppermute | solution.py:458
  85.7 2.0 %collective-permute-start.11 = (bf16[192,768]{1,0:T(8,128)(2,1)S(1)}, bf16[192,768]{1,0:T(8,128)(2,1)}, u32[]{:S(2)}, u32[]{:S(2)}) collective-permute-start(bf16[192,768]{1,0:T(8,128)(2,1)S(1)} %collective-permute-done.9.refs_4_), channel_id=1, source_target_pairs={{6,2},{10,6},{14,10},{12,14},{8,12},{4,8},{0,4},{2,0},{3,7},{7,11}... | collective-permute-start | bytes 884744 | tf_op jit(solution)/shard_map/ppermute | solution.py:460
  87.7 0.4 collective-permute-start.14
  88.3 8.3 %shard_map.223 = (f32[2,192,768]{2,1,0:T(8,128)}, f32[2,192,768]{2,1,0:T(8,128)}) custom-call(bf16[192,768]{1,0:T(8,128)(2,1)} %get-tuple-element.58.second_ref.refs_0_, bf16[192,768]{1,0:T(8,128)(2,1)} %collective-permute-done.6.refs_1_, bf16[192,768]{1,0:T(8,128)(2,1)} %collective-permute-done.7.refs_2_, bf16[192,768]{1,0:T(8,128)(2,1)} %copy-done.14, ...), custom_call_target="tpu_custom_call" | custom-call | flops 1 | bytes 1 | tf_op jit(solution)/shard_map/pallas_call | solution.py:433
  96.6 0.4 collective-permute-done.12.refs_2_
  97.0 0.3 collective-permute-done.11.refs_1_
  97.3 2.9 %collective-permute-done.14.refs_5_ = bf16[192,768]{1,0:T(8,128)(2,1)} collective-permute-done((bf16[192,768]{1,0:T(8,128)(2,1)}, bf16[192,768]{1,0:T(8,128)(2,1)}, u32[]{:S(2)}, u32[]{:S(2)}) %collective-permute-start.14) | collective-permute-done | bytes 294944 | tf_op jit(solution)/shard_map/ppermute | solution.py:458
  100.3 4.9 %shard_map.224 = (f32[2,192,768]{2,1,0:T(8,128)S(1)}, f32[2,192,768]{2,1,0:T(8,128)S(1)}) custom-call(bf16[192,768]{1,0:T(8,128)(2,1)} %copy-done.13, bf16[192,768]{1,0:T(8,128)(2,1)} %collective-permute-done.11.refs_1_, bf16[192,768]{1,0:T(8,128)(2,1)} %copy-done.15, bf16[192,768]{1,0:T(8,128)(2,1)} %collective-permute-done.4.refs_3_, ...), custom_call_target="tpu_custom_call" | custom-call | flops 1 | bytes 1 | tf_op jit(solution)/shard_map/pallas_call | solution.py:433
  105.3 2.8 %shard_map.225 = bf16[180,768]{1,0:T(8,128)(2,1)} custom-call(bf16[16,72,128]{2,1,0:T(8,128)(2,1)S(1)} %all-to-all-done.3.refs_9_.in_ref, bf16[180,768]{1,0:T(8,128)(2,1)} %bitcast.41, f32[768]{0:T(1024)} %gain_hbm.5, f32[192,768]{1,0:T(8,128)} %get-tuple-element.91.gres_hbm, bf16[2,192,192]{2,1,0:T(8,128)(2,1)} %constant.78.clone.table_hbm), custom_call_target="tpu_custom_call" | custom-call | flops 1 | bytes 1 | tf_op jit(solution)/shard_map/pallas_call | solution.py:433
  108.3 0.4 collective-permute-start.16
  108.7 0.9 shard_map.226
  109.6 5.3 %all-to-all-start.4 = ((bf16[16,48,192]{2,1,0:T(8,128)(2,1)}), bf16[16,48,192]{2,1,0:T(8,128)(2,1)S(1)}, u32[]{:S(2)}, u32[]{:S(2)}) async-start(bf16[16,48,192]{2,1,0:T(8,128)(2,1)} %bitcast.18), calls=%async_computation.4 | async-start | bytes 786432 | tf_op jit(solution)/shard_map/all_to_all | solution.py:627
  115.0 4.1 %fusion.5 = f32[192,768]{1,0:T(8,128)S(1)} fusion(bf16[192,3072]{1,0:T(8,128)(2,1)S(1)} %copy-done.17, bf16[768,3072]{1,0:T(8,128)(2,1)} %down_hbm.1), kind=kOutput, calls=%fused_computation.26 | convolution fusion | flops 905969664 | bytes 6488064 | tf_op jit(solution)/shard_map/dot_general | solution.py:21
  119.1 0.8 fusion.2
  119.9 0.6 slice_bitcast_fusion
  120.5 6.6 %all-to-all-done.4.in_ref = bf16[16,48,192]{2,1,0:T(8,128)(2,1)S(1)} async-done(((bf16[16,48,192]{2,1,0:T(8,128)(2,1)}), bf16[16,48,192]{2,1,0:T(8,128)(2,1)S(1)}, u32[]{:S(2)}, u32[]{:S(2)}) %all-to-all-start.4) | async-done | bytes 294944 | tf_op jit(solution)/shard_map/all_to_all | solution.py:627
  127.1 0.9 bitcast_add_fusion
  128.0 0.9 shard_map.227
  (71 shorter events, 1.3 us)
Async XLA Ops:
  3.5 12.2 %copy-start = (bf16[192,768]{1,0:T(8,128)(2,1)}, bf16[192,768]{1,0:T(8,128)(2,1)S(1)}, u32[]{:S(2)}) copy-start(bf16[192,768]{1,0:T(8,128)(2,1)S(1)} %get-tuple-element.53.cot_hbm.refs_5_) | copy-start | bytes 884740
  3.5 15.4 %collective-permute-start = (bf16[192,768]{1,0:T(8,128)(2,1)S(1)}, bf16[192,768]{1,0:T(8,128)(2,1)S(1)}, u32[]{:S(2)}, u32[]{:S(2)}) collective-permute-start(bf16[192,768]{1,0:T(8,128)(2,1)S(1)} %get-tuple-element.53.cot_hbm.refs_5_), channel_id=1, source_target_pairs={{2,6},{6,10},{10,14},{14,12},{12,8},{8,4},{4,0},{0,2},{7,3},{11,7}... | collective-permute-start | bytes 884744 | tf_op jit(solution)/shard_map/ppermute | solution.py:458
  6.5 12.4 %collective-permute-start.1 = (bf16[192,768]{1,0:T(8,128)(2,1)S(1)}, bf16[192,768]{1,0:T(8,128)(2,1)S(1)}, u32[]{:S(2)}, u32[]{:S(2)}) collective-permute-start(bf16[192,768]{1,0:T(8,128)(2,1)S(1)} %get-tuple-element.53.cot_hbm.refs_5_), channel_id=1, source_target_pairs={{6,2},{10,6},{14,10},{12,14},{8,12},{4,8},{0,4},{2,0},{3,7},{7,11}... | collective-permute-start | bytes 884744 | tf_op jit(solution)/shard_map/ppermute | solution.py:460
  6.6 16.9 %all-to-all-start = ((bf16[16,72,128]{2,1,0:T(8,128)(2,1)}), bf16[16,72,128]{2,1,0:T(8,128)(2,1)S(1)}, u32[]{:S(2)}, u32[]{:S(2)}) async-start(bf16[16,72,128]{2,1,0:T(8,128)(2,1)} %get-tuple-element.52), calls=%async_computation | async-start | bytes 589824 | tf_op jit(solution)/shard_map/all_to_all | solution.py:533
  14.5 11.1 %copy-start.1 = (f32[256,256]{1,0:T(8,128)}, f32[256,256]{1,0:T(8,128)S(1)}, u32[]{:S(2)}) copy-start(f32[256,256]{1,0:T(8,128)S(1)} %maximum_maximum_fusion.w1_ref) | copy-start | bytes 786436
  17.7 12.1 %copy-start.3 = (f32[256,256]{1,0:T(8,128)}, f32[256,256]{1,0:T(8,128)S(1)}, u32[]{:S(2)}) copy-start(f32[256,256]{1,0:T(8,128)S(1)} %maximum_maximum_fusion.1.w2_ref) | copy-start | bytes 786436
  18.9 17.0 %copy-start.10 = (bf16[192,768]{1,0:T(8,128)(2,1)}, bf16[192,768]{1,0:T(8,128)(2,1)S(1)}, u32[]{:S(2)}) copy-start(bf16[192,768]{1,0:T(8,128)(2,1)S(1)} %collective-permute-done.refs_6_) | copy-start | bytes 884740
  18.9 16.9 %copy-start.11 = (bf16[192,768]{1,0:T(8,128)(2,1)}, bf16[192,768]{1,0:T(8,128)(2,1)S(1)}, u32[]{:S(2)}) copy-start(bf16[192,768]{1,0:T(8,128)(2,1)S(1)} %collective-permute-done.1.refs_7_) | copy-start | bytes 884740
  23.5 10.5 %collective-permute-start.2 = (bf16[192,768]{1,0:T(8,128)(2,1)S(1)}, bf16[192,768]{1,0:T(8,128)(2,1)}, u32[]{:S(2)}, u32[]{:S(2)}) collective-permute-start(bf16[192,768]{1,0:T(8,128)(2,1)S(1)} %collective-permute-done.refs_6_), channel_id=1, source_target_pairs={{2,6},{6,10},{10,14},{14,12},{12,8},{8,4},{4,0},{0,2},{7,3},{11,7}... | collective-permute-start | bytes 884744 | tf_op jit(solution)/shard_map/ppermute | solution.py:458
  23.5 12.3 %collective-permute-start.3 = (bf16[192,768]{1,0:T(8,128)(2,1)S(1)}, bf16[192,768]{1,0:T(8,128)(2,1)}, u32[]{:S(2)}, u32[]{:S(2)}) collective-permute-start(bf16[192,768]{1,0:T(8,128)(2,1)S(1)} %collective-permute-done.1.refs_7_), channel_id=1, source_target_pairs={{6,2},{10,6},{14,10},{12,14},{8,12},{4,8},{0,4},{2,0},{3,7},{7,11}... | collective-permute-start | bytes 884744 | tf_op jit(solution)/shard_map/ppermute | solution.py:460
  29.8 15.3 %all-to-all-start.1 = ((bf16[16,72,128]{2,1,0:T(8,128)(2,1)}), bf16[16,72,128]{2,1,0:T(8,128)(2,1)}, u32[]{:S(2)}, u32[]{:S(2)}) async-start(bf16[16,72,128]{2,1,0:T(8,128)(2,1)} %get-tuple-element.55), calls=%async_computation.1 | async-start | bytes 589824 | tf_op jit(solution)/shard_map/all_to_all | solution.py:546
  34.0 17.3 %collective-permute-start.4 = (bf16[192,768]{1,0:T(8,128)(2,1)}, bf16[192,768]{1,0:T(8,128)(2,1)}, u32[]{:S(2)}, u32[]{:S(2)}) collective-permute-start(bf16[192,768]{1,0:T(8,128)(2,1)} %collective-permute-done.2.refs_8_), channel_id=1, source_target_pairs={{2,6},{6,10},{10,14},{14,12},{12,8},{8,4},{4,0},{0,2},{7,3},{11,7}... | collective-permute-start | bytes 884744 | tf_op jit(solution)/shard_map/ppermute | solution.py:458
  35.9 15.5 %collective-permute-start.5 = (bf16[192,768]{1,0:T(8,128)(2,1)}, bf16[192,768]{1,0:T(8,128)(2,1)}, u32[]{:S(2)}, u32[]{:S(2)}) collective-permute-start(bf16[192,768]{1,0:T(8,128)(2,1)} %collective-permute-done.3.refs_9_), channel_id=1, source_target_pairs={{6,2},{10,6},{14,10},{12,14},{8,12},{4,8},{0,4},{2,0},{3,7},{7,11}... | collective-permute-start | bytes 884744 | tf_op jit(solution)/shard_map/ppermute | solution.py:460
  48.6 0.7 copy-start.7
  49.3 13.4 %collective-permute-start.6 = (bf16[192,768]{1,0:T(8,128)(2,1)}, bf16[192,768]{1,0:T(8,128)(2,1)}, u32[]{:S(2)}, u32[]{:S(2)}) collective-permute-start(bf16[192,768]{1,0:T(8,128)(2,1)} %get-tuple-element.58.second_ref.refs_0_), channel_id=1, source_target_pairs={{2,6},{6,10},{10,14},{14,12},{12,8},{8,4},{4,0},{0,2},{7,3},{11,7}... | collective-permute-start | bytes 884744 | tf_op jit(solution)/shard_map/ppermute | solution.py:458
  49.3 13.4 %collective-permute-start.7 = (bf16[192,768]{1,0:T(8,128)(2,1)}, bf16[192,768]{1,0:T(8,128)(2,1)}, u32[]{:S(2)}, u32[]{:S(2)}) collective-permute-start(bf16[192,768]{1,0:T(8,128)(2,1)} %get-tuple-element.58.second_ref.refs_0_), channel_id=1, source_target_pairs={{6,2},{10,6},{14,10},{12,14},{8,12},{4,8},{0,4},{2,0},{3,7},{7,11}... | collective-permute-start | bytes 884744 | tf_op jit(solution)/shard_map/ppermute | solution.py:460
  58.4 0.7 copy-start.9
  59.2 14.6 %all-to-all-start.2 = ((bf16[16,72,128]{2,1,0:T(8,128)(2,1)}), bf16[16,72,128]{2,1,0:T(8,128)(2,1)S(1)}, u32[]{:S(2)}, u32[]{:S(2)}) async-start(bf16[16,72,128]{2,1,0:T(8,128)(2,1)} %copy-done.9), calls=%async_computation.2 | async-start | bytes 589824 | tf_op jit(solution)/shard_map/all_to_all | solution.py:571
  62.7 16.2 %collective-permute-start.8 = (bf16[192,768]{1,0:T(8,128)(2,1)}, bf16[192,768]{1,0:T(8,128)(2,1)S(1)}, u32[]{:S(2)}, u32[]{:S(2)}) collective-permute-start(bf16[192,768]{1,0:T(8,128)(2,1)} %collective-permute-done.6.refs_1_), channel_id=1, source_target_pairs={{2,6},{6,10},{10,14},{14,12},{12,8},{8,4},{4,0},{0,2},{7,3},{11,7}... | collective-permute-start | bytes 884744 | tf_op jit(solution)/shard_map/ppermute | solution.py:458
  64.8 14.1 %collective-permute-start.9 = (bf16[192,768]{1,0:T(8,128)(2,1)}, bf16[192,768]{1,0:T(8,128)(2,1)S(1)}, u32[]{:S(2)}, u32[]{:S(2)}) collective-permute-start(bf16[192,768]{1,0:T(8,128)(2,1)} %collective-permute-done.7.refs_2_), channel_id=1, source_target_pairs={{6,2},{10,6},{14,10},{12,14},{8,12},{4,8},{0,4},{2,0},{3,7},{7,11}... | collective-permute-start | bytes 884744 | tf_op jit(solution)/shard_map/ppermute | solution.py:460
  73.7 1.0 copy-start.2
  74.7 0.9 copy-start.4
  78.9 9.4 %copy-start.14 = (bf16[192,768]{1,0:T(8,128)(2,1)}, bf16[192,768]{1,0:T(8,128)(2,1)S(1)}, u32[]{:S(2)}) copy-start(bf16[192,768]{1,0:T(8,128)(2,1)S(1)} %collective-permute-done.8.refs_3_) | copy-start | bytes 884740
  78.9 9.4 %copy-start.12 = (bf16[192,768]{1,0:T(8,128)(2,1)}, bf16[192,768]{1,0:T(8,128)(2,1)S(1)}, u32[]{:S(2)}) copy-start(bf16[192,768]{1,0:T(8,128)(2,1)S(1)} %collective-permute-done.9.refs_4_) | copy-start | bytes 884740
  78.9 6.8 %collective-permute-start.10 = (bf16[192,768]{1,0:T(8,128)(2,1)S(1)}, bf16[192,768]{1,0:T(8,128)(2,1)S(1)}, u32[]{:S(2)}, u32[]{:S(2)}) collective-permute-start(bf16[192,768]{1,0:T(8,128)(2,1)S(1)} %collective-permute-done.8.refs_3_), channel_id=1, source_target_pairs={{2,6},{6,10},{10,14},{14,12},{12,8},{8,4},{4,0},{0,2},{7,3},{11,7}... | collective-permute-start | bytes 884744 | tf_op jit(solution)/shard_map/ppermute | solution.py:458
  79.0 17.6 %all-to-all-start.3 = ((bf16[16,72,128]{2,1,0:T(8,128)(2,1)}), bf16[16,72,128]{2,1,0:T(8,128)(2,1)S(1)}, u32[]{:S(2)}, u32[]{:S(2)}) async-start(bf16[16,72,128]{2,1,0:T(8,128)(2,1)} %get-tuple-element.75.refs_13_), calls=%async_computation.3 | async-start | bytes 589824 | tf_op jit(solution)/shard_map/all_to_all | solution.py:579
  82.8 13.7 %collective-permute-start.13 = (f32[2,2,48,96]{3,2,1,0:T(8,128)S(1)}, f32[2,2,48,96]{3,2,1,0:T(8,128)S(1)}, u32[]{:S(2)}, u32[]{:S(2)}) collective-permute-start(f32[2,2,48,96]{3,2,1,0:T(8,128)S(1)} %dynamic-slice_bitcast_fusion.3), channel_id=1, source_target_pairs={{0,1},{1,0},{2,3},{3,2},{4,5},{5,4},{6,7},{7,6},{8,9},{9,8},{10,11... | collective-permute-start | bytes 221192 | tf_op jit(solution)/shard_map/ppermute | solution.py:589
  85.7 10.9 %copy-start.13 = (bf16[192,768]{1,0:T(8,128)(2,1)}, bf16[192,768]{1,0:T(8,128)(2,1)S(1)}, u32[]{:S(2)}) copy-start(bf16[192,768]{1,0:T(8,128)(2,1)S(1)} %collective-permute-done.10.refs_0_) | copy-start | bytes 884740
  85.7 11.3 %collective-permute-start.12 = (bf16[192,768]{1,0:T(8,128)(2,1)S(1)}, bf16[192,768]{1,0:T(8,128)(2,1)S(1)}, u32[]{:S(2)}, u32[]{:S(2)}) collective-permute-start(bf16[192,768]{1,0:T(8,128)(2,1)S(1)} %collective-permute-done.10.refs_0_), channel_id=1, source_target_pairs={{2,6},{6,10},{10,14},{14,12},{12,8},{8,4},{4,0},{0,2},{7,3},{11,7}... | collective-permute-start | bytes 884744 | tf_op jit(solution)/shard_map/ppermute | solution.py:458
  85.7 11.6 %collective-permute-start.11 = (bf16[192,768]{1,0:T(8,128)(2,1)S(1)}, bf16[192,768]{1,0:T(8,128)(2,1)}, u32[]{:S(2)}, u32[]{:S(2)}) collective-permute-start(bf16[192,768]{1,0:T(8,128)(2,1)S(1)} %collective-permute-done.9.refs_4_), channel_id=1, source_target_pairs={{6,2},{10,6},{14,10},{12,14},{8,12},{4,8},{0,4},{2,0},{3,7},{7,11}... | collective-permute-start | bytes 884744 | tf_op jit(solution)/shard_map/ppermute | solution.py:460
  87.7 12.5 %collective-permute-start.14 = (bf16[192,768]{1,0:T(8,128)(2,1)}, bf16[192,768]{1,0:T(8,128)(2,1)}, u32[]{:S(2)}, u32[]{:S(2)}) collective-permute-start(bf16[192,768]{1,0:T(8,128)(2,1)} %collective-permute-done.4.refs_3_), channel_id=1, source_target_pairs={{2,6},{6,10},{10,14},{14,12},{12,8},{8,4},{4,0},{0,2},{7,3},{11,7}... | collective-permute-start | bytes 884744 | tf_op jit(solution)/shard_map/ppermute | solution.py:458
  97.0 3.3 %copy-start.15 = (bf16[192,768]{1,0:T(8,128)(2,1)}, bf16[192,768]{1,0:T(8,128)(2,1)S(1)}, u32[]{:S(2)}) copy-start(bf16[192,768]{1,0:T(8,128)(2,1)S(1)} %collective-permute-done.12.refs_2_) | copy-start | bytes 884740
  105.2 3.0 %copy-start.5 = (f32[2,192,768]{2,1,0:T(8,128)}, f32[2,192,768]{2,1,0:T(8,128)S(1)}, u32[]{:S(2)}) copy-start(f32[2,192,768]{2,1,0:T(8,128)S(1)} %get-tuple-element.93) | copy-start | bytes 3538948
  105.3 3.4 %collective-permute-start.15 = (f32[192,768]{1,0:T(8,128)S(1)}, f32[192,768]{1,0:T(8,128)S(1)}, u32[]{:S(2)}, u32[]{:S(2)}) collective-permute-start(f32[192,768]{1,0:T(8,128)S(1)} %get-tuple-element.98), channel_id=1, source_target_pairs={{0,1},{1,0},{2,3},{3,2},{4,5},{5,4},{6,7},{7,6},{8,9},{9,8},{10,11... | collective-permute-start | bytes 1769480 | tf_op jit(solution)/shard_map/ppermute | solution.py:618
  108.3 6.7 %copy-start.17 = (bf16[192,3072]{1,0:T(8,128)(2,1)S(1)}, bf16[192,3072]{1,0:T(8,128)(2,1)}, u32[]{:S(2)}) copy-start(bf16[192,3072]{1,0:T(8,128)(2,1)} %get-tuple-element.64) | copy-start | bytes 3538948
  108.3 12.2 %collective-permute-start.16 = (f32[192,768]{1,0:T(8,128)S(1)}, f32[192,768]{1,0:T(8,128)S(1)}, u32[]{:S(2)}, u32[]{:S(2)}) collective-permute-start(f32[192,768]{1,0:T(8,128)S(1)} %dynamic-slice_bitcast_fusion), channel_id=1, source_target_pairs={{0,1},{1,0},{2,3},{3,2},{4,5},{5,4},{6,7},{7,6},{8,9},{9,8},{10,11... | collective-permute-start | bytes 1769480 | tf_op jit(solution)/shard_map/ppermute | solution.py:618
  109.6 17.5 %all-to-all-start.4 = ((bf16[16,48,192]{2,1,0:T(8,128)(2,1)}), bf16[16,48,192]{2,1,0:T(8,128)(2,1)S(1)}, u32[]{:S(2)}, u32[]{:S(2)}) async-start(bf16[16,48,192]{2,1,0:T(8,128)(2,1)} %bitcast.18), calls=%async_computation.4 | async-start | bytes 786432 | tf_op jit(solution)/shard_map/all_to_all | solution.py:627
  115.0 4.1 %copy-start.8 = (bf16[192,768]{1,0:T(8,128)(2,1)S(1)}, bf16[192,768]{1,0:T(8,128)(2,1)}, u32[]{:S(2)}) copy-start(bf16[192,768]{1,0:T(8,128)(2,1)} %copy-done.7) | copy-start | bytes 884740
  115.0 4.1 %copy-start.16 = (f32[768]{0:T(1024)S(1)}, f32[768]{0:T(1024)}, u32[]{:S(2)}) copy-start(f32[768]{0:T(1024)} %param.31) | copy-start | bytes 9220
  119.1 8.1 %copy-start.6 = (f32[2,192,768]{2,1,0:T(8,128)S(1)}, f32[2,192,768]{2,1,0:T(8,128)}, u32[]{:S(2)}) copy-start(f32[2,192,768]{2,1,0:T(8,128)} %copy-done.5) | copy-start | bytes 3538948

commit v4 on v3

--- a/solution.py
+++ b/solution.py
@@ -242,11 +242,14 @@
     return grad[a, a] + grad[b, b], grad[a, b] - grad[b, a]
 
 
-def filter_grad_kernel(block, in_ref, w1_ref, w2_ref, spec_hbm, hid_hbm, slope_hbm, shrink_hbm,
-                       out_ref, grads_ref, wide_ref, rows_ref, spec_ref, hid_ref, slope_ref, shrink_ref, sems):
-    copies = fetch(((shrink_hbm, shrink_ref), (slope_hbm, slope_ref), (spec_hbm, spec_ref), (hid_hbm, hid_ref)), sems)
+def filter_grad_kernel(block, in_ref, w1_hbm, w2_hbm, spec_hbm, hid_hbm, slope_hbm, shrink_hbm, out_ref, grads_ref,
+                       wide_ref, rows_ref, spec_ref, hid_ref, slope_ref, shrink_ref, w1_ref, w2_ref, sems):
+    copies = fetch(((shrink_hbm, shrink_ref), (slope_hbm, slope_ref), (spec_hbm, spec_ref), (hid_hbm, hid_ref),
+                    (w2_hbm, w2_ref), (w1_hbm, w1_ref)), sems)
     load_transform(in_ref, block, -1.0, wide_ref, rows_ref)
     copies[0].wait()
+    copies[4].wait()
+    copies[5].wait()
     grad_outer = (wide_ref[...] * shrink_ref[...].astype(F32)).astype(BF16)
     grad_inner = dot(grad_outer, w2_ref[...].astype(BF16), ((1,), (1,)))
     copies[1].wait()
@@ -568,12 +571,13 @@
     seconds[1], _ = lax.optimization_barrier((seconds[1], grad_out))
     for number in range(2, third):
         seconds += [ring.step(seconds[-1], number)]
-    grad_in, cots[third] = lax.optimization_barrier((a2a(grad_out), cots[third]))
     cots += [ring.step(cots[-1], ring.steps)]
+    grad_out, cots[-1] = lax.optimization_barrier((grad_out, cots[-1]))
+    grad_in = a2a(grad_out)
 
     grad_back, squares = call(
-        partial(filter_grad_kernel, block), (packed, struct((2, 2, block, block), F32)), spectral_scratch,
-        [VMEM] * 3 + [HBM] * 4, grad_in, w1, w2, *kept)
+        partial(filter_grad_kernel, block), (packed, struct((2, 2, block, block), F32)), spectral_scratch[:-1] + [pltpu.VMEM(w1.shape, F32)] * 2 + [sems(6)],
+        [VMEM] + [HBM] * 6, grad_in, w1, w2, *kept)
     seconds[2:], _ = lax.optimization_barrier((seconds[2:], grad_back))
     seconds += [ring.step(seconds[-1], third)]
     grad_lon = a2a(grad_back)

time: 130 us -> 134 us (1.031)
  starting transfers between devices: 38.1 us -> 41.6 us
    ppermute x8, starting transfers between devices: 7.29 us -> 13 us  [step(): out = [lax.ppermute(blocks[0], 'lat', self.forward)]]
    ppermute x6, starting transfers between devices: 6.78 us -> 3.71 us  [step(): out += [lax.ppermute(blocks[-1], 'lat', self.backward)]]
    unnamed x41 -> x37, local copies, waits for them, and re-layouts: 3.97 us -> 2.76 us
  transfers between devices with their start and end apart: 22 -> 22, of which waited for: 8 -> 7; matrix products, arithmetic and copies ran while one was open for 9% -> 9% of each run, Pallas kernels for 26% -> 26%
where the time goes in v4:
time: 134 us; the launch traced here: 133 us
  Pallas kernels  42.9 us (32%)
  starting transfers between devices  41.6 us (31%)
  waiting for transfers between devices  32.3 us (24%)
  local copies, waits for them, and re-layouts  8.86 us (7%)
  matrix products  4.08 us (3%)
  other arithmetic  1.74 us (1%)
    pallas_call x11, Pallas kernels, call(): pl.pallas_call(kernel, out_shape=out, scratch_shapes=scratch, in_specs=in...  42.9 us
    ppermute x8, starting transfers between devices, step(): out = [lax.ppermute(blocks[0], 'lat', self.forward)]  13 us
    all_to_all x1, waiting for transfers between devices, shards(): grad_in = a2a(grad_out)  8.73 us
    all_to_all x1, waiting for transfers between devices, shards(): down_rows = a2a(down_part.reshape(devices, channels // devices, share))  6.63 us
    all_to_all x1, starting transfers between devices, shards(): a2a(outgoing)  6.29 us
    ppermute x8, waiting for transfers between devices, step(): out = [lax.ppermute(blocks[0], 'lat', self.forward)]  6.25 us
    all_to_all x1, waiting for transfers between devices, shards(): a2a(outgoing)  5.34 us
    all_to_all x1, waiting for transfers between devices, shards(): back, grad_hidden = lax.optimization_barrier((a2a(returning), grad_hidden))  5.34 us
  transfers between devices with their start and end apart: 22, of which 7 were waited for; matrix products, arithmetic and copies ran while one was open for 9% of the time, Pallas kernels for 26%

profile of v4, /device:TPU:0, one launch (start us, length us, event | category | flops | bytes accessed | tf_op | source)
XLA Modules:
  0.0 132.8 jit_solution(6123899019622421992)
XLA Ops:
  0.6 2.8 %shard_map.217 = (bf16[16,72,128]{2,1,0:T(8,128)(2,1)}, bf16[192,768]{1,0:T(8,128)(2,1)S(1)}) custom-call(bf16[180,768]{1,0:T(8,128)(2,1)} %bitcast.39, bf16[180,768]{1,0:T(8,128)(2,1)} %bitcast.43, f32[768]{0:T(1024)} %gain_hbm.5, f32[768]{0:T(1024)} %shift1_hbm.1, bf16[2,192,192]{2,1,0:T(8,128)(2,1)} %constant.75.clone.table_hbm), custom_call_target="tpu_custom_call" | custom-call | flops 1 | bytes 1 | tf_op jit(solution)/shard_map/pallas_call | solution.py:436
  3.5 3.0 %collective-permute-start = (bf16[192,768]{1,0:T(8,128)(2,1)S(1)}, bf16[192,768]{1,0:T(8,128)(2,1)S(1)}, u32[]{:S(2)}, u32[]{:S(2)}) collective-permute-start(bf16[192,768]{1,0:T(8,128)(2,1)S(1)} %get-tuple-element.52.cot_hbm.refs_5_), channel_id=1, source_target_pairs={{2,6},{6,10},{10,14},{14,12},{12,8},{8,4},{4,0},{0,2},{7,3},{11,7}... | collective-permute-start | bytes 884744 | tf_op jit(solution)/shard_map/ppermute | solution.py:461
  6.6 6.3 %all-to-all-start = ((bf16[16,72,128]{2,1,0:T(8,128)(2,1)}), bf16[16,72,128]{2,1,0:T(8,128)(2,1)S(1)}, u32[]{:S(2)}, u32[]{:S(2)}) async-start(bf16[16,72,128]{2,1,0:T(8,128)(2,1)} %get-tuple-element.51), calls=%async_computation | async-start | bytes 589824 | tf_op jit(solution)/shard_map/all_to_all | solution.py:536
  12.9 1.2 constant_dynamic-slice_fusion.3
  14.5 1.2 constant_dynamic-slice_fusion.6
  15.7 0.3 copy.32
  16.0 0.8 dynamic_slice.42
  16.9 1.2 constant_dynamic-slice_fusion.7.refs_10_.refs_6_
  18.2 5.3 %all-to-all-done.in_ref = bf16[16,72,128]{2,1,0:T(8,128)(2,1)S(1)} async-done(((bf16[16,72,128]{2,1,0:T(8,128)(2,1)}), bf16[16,72,128]{2,1,0:T(8,128)(2,1)S(1)}, u32[]{:S(2)}, u32[]{:S(2)}) %all-to-all-start) | async-done | bytes 294944 | tf_op jit(solution)/shard_map/all_to_all | solution.py:536
  23.5 2.0 %collective-permute-start.3 = (bf16[192,768]{1,0:T(8,128)(2,1)S(1)}, bf16[192,768]{1,0:T(8,128)(2,1)}, u32[]{:S(2)}, u32[]{:S(2)}) collective-permute-start(bf16[192,768]{1,0:T(8,128)(2,1)S(1)} %collective-permute-done.1.refs_7_), channel_id=1, source_target_pairs={{6,2},{10,6},{14,10},{12,14},{8,12},{4,8},{0,4},{2,0},{3,7},{7,11}... | collective-permute-start | bytes 884744 | tf_op jit(solution)/shard_map/ppermute | solution.py:463
  25.5 0.8 constant_dynamic-slice_fusion.2
  26.3 4.2 %shard_map.218 = (bf16[16,72,128]{2,1,0:T(8,128)(2,1)}, bf16[768,256]{1,0:T(8,128)(2,1)}, bf16[768,256]{1,0:T(8,128)(2,1)}, bf16[768,256]{1,0:T(8,128)(2,1)}, bf16[768,256]{1,0:T(8,128)(2,1)}) custom-call(bf16[16,72,128]{2,1,0:T(8,128)(2,1)S(1)} %all-to-all-done.in_ref, f32[256,256]{1,0:T(8,128)S(1)} %maximum_maximum_fusion.w1_ref.w1_hbm, ...), custom_call_target="tpu_custom_call" | custom-call | flops 1 | bytes 1 | tf_op jit(solution)/shard_map/pallas_call | solution.py:436
  30.6 4.2 %all-to-all-start.1 = ((bf16[16,72,128]{2,1,0:T(8,128)(2,1)}), bf16[16,72,128]{2,1,0:T(8,128)(2,1)}, u32[]{:S(2)}, u32[]{:S(2)}) async-start(bf16[16,72,128]{2,1,0:T(8,128)(2,1)} %get-tuple-element.54), calls=%async_computation.1 | async-start | bytes 589824 | tf_op jit(solution)/shard_map/all_to_all | solution.py:549
  34.8 1.8 %collective-permute-start.4 = (bf16[192,768]{1,0:T(8,128)(2,1)}, bf16[192,768]{1,0:T(8,128)(2,1)}, u32[]{:S(2)}, u32[]{:S(2)}) collective-permute-start(bf16[192,768]{1,0:T(8,128)(2,1)} %collective-permute-done.2.refs_8_), channel_id=1, source_target_pairs={{2,6},{6,10},{10,14},{14,12},{12,8},{8,4},{4,0},{0,2},{7,3},{11,7}... | collective-permute-start | bytes 884744 | tf_op jit(solution)/shard_map/ppermute | solution.py:461
  36.6 0.3 collective-permute-start.5
  37.0 3.6 %shard_map.219.ghid_ref = f32[192,3072]{1,0:T(8,128)S(1)} custom-call(bf16[192,768]{1,0:T(8,128)(2,1)} %copy-done, bf16[768,3072]{1,0:T(8,128)(2,1)} %down_hbm.1), custom_call_target="tpu_custom_call" | custom-call | flops 1 | bytes 1 | tf_op jit(solution)/shard_map/pallas_call | solution.py:436
  40.5 5.3 %all-to-all-done.1.in_hbm = bf16[16,72,128]{2,1,0:T(8,128)(2,1)} async-done(((bf16[16,72,128]{2,1,0:T(8,128)(2,1)}), bf16[16,72,128]{2,1,0:T(8,128)(2,1)}, u32[]{:S(2)}, u32[]{:S(2)}) %all-to-all-start.1) | async-done | bytes 294944 | tf_op jit(solution)/shard_map/all_to_all | solution.py:549
  45.9 3.1 %collective-permute-done.4.refs_3_ = bf16[192,768]{1,0:T(8,128)(2,1)} collective-permute-done((bf16[192,768]{1,0:T(8,128)(2,1)}, bf16[192,768]{1,0:T(8,128)(2,1)}, u32[]{:S(2)}, u32[]{:S(2)}) %collective-permute-start.4) | collective-permute-done | bytes 294944 | tf_op jit(solution)/shard_map/ppermute | solution.py:461
  48.9 1.5 %collective-permute-start.10 = (bf16[192,768]{1,0:T(8,128)(2,1)}, bf16[192,768]{1,0:T(8,128)(2,1)}, u32[]{:S(2)}, u32[]{:S(2)}) collective-permute-start(bf16[192,768]{1,0:T(8,128)(2,1)} %collective-permute-done.4.refs_3_), channel_id=1, source_target_pairs={{2,6},{6,10},{10,14},{14,12},{12,8},{8,4},{4,0},{0,2},{7,3},{11,7}... | collective-permute-start | bytes 884744 | tf_op jit(solution)/shard_map/ppermute | solution.py:461
  50.4 3.5 %shard_map.220 = (bf16[192,768]{1,0:T(8,128)(2,1)S(1)}, bf16[192,768]{1,0:T(8,128)(2,1)}, bf16[3072,768]{1,0:T(8,128)(2,1)S(1)}) custom-call(bf16[16,72,128]{2,1,0:T(8,128)(2,1)} %all-to-all-done.1.in_hbm, bf16[180,768]{1,0:T(8,128)(2,1)} %bitcast.40, f32[768]{0:T(1024)} %gain_hbm.5, f32[768]{0:T(1024)} %shift1_hbm.1, f32[768]{0:T(1024)} %gain_hbm.4, ...), custom_call_target="tpu_custom_call" | custom-call | flops 1 | bytes 1 | tf_op jit(solution)/shard_map/pallas_call | solution.py:436
  53.9 0.7 copy-done.5
  54.6 3.1 %collective-permute-start.6 = (bf16[192,768]{1,0:T(8,128)(2,1)}, bf16[192,768]{1,0:T(8,128)(2,1)}, u32[]{:S(2)}, u32[]{:S(2)}) collective-permute-start(bf16[192,768]{1,0:T(8,128)(2,1)} %get-tuple-element.57.second_ref.refs_0_), channel_id=1, source_target_pairs={{2,6},{6,10},{10,14},{14,12},{12,8},{8,4},{4,0},{0,2},{7,3},{11,7}... | collective-permute-start | bytes 884744 | tf_op jit(solution)/shard_map/ppermute | solution.py:461
  57.7 7.1 %shard_map.221 = (bf16[192,3072]{1,0:T(8,128)(2,1)}, f32[192,768]{1,0:T(8,128)}, bf16[16,72,128]{2,1,0:T(8,128)(2,1)S(1)}) custom-call(bf16[192,768]{1,0:T(8,128)(2,1)} %get-tuple-element.57.second_ref.refs_0_, bf16[3072,768]{1,0:T(8,128)(2,1)S(1)} %get-tuple-element.58.up_ref, f32[192,3072]{1,0:T(8,128)S(1)} %shard_map.219.ghid_ref, ...), custom_call_target="tpu_custom_call" | custom-call | flops 1 | bytes 1 | tf_op jit(solution)/shard_map/pallas_call | solution.py:436
  64.8 0.7 copy-done.7
  65.6 3.7 %all-to-all-start.2 = ((bf16[16,72,128]{2,1,0:T(8,128)(2,1)}), bf16[16,72,128]{2,1,0:T(8,128)(2,1)S(1)}, u32[]{:S(2)}, u32[]{:S(2)}) async-start(bf16[16,72,128]{2,1,0:T(8,128)(2,1)} %copy-done.7), calls=%async_computation.2 | async-start | bytes 589824 | tf_op jit(solution)/shard_map/all_to_all | solution.py:576
  69.3 1.9 %collective-permute-start.8 = (bf16[192,768]{1,0:T(8,128)(2,1)}, bf16[192,768]{1,0:T(8,128)(2,1)S(1)}, u32[]{:S(2)}, u32[]{:S(2)}) collective-permute-start(bf16[192,768]{1,0:T(8,128)(2,1)} %collective-permute-done.6.refs_1_), channel_id=1, source_target_pairs={{2,6},{6,10},{10,14},{14,12},{12,8},{8,4},{4,0},{0,2},{7,3},{11,7}... | collective-permute-start | bytes 884744 | tf_op jit(solution)/shard_map/ppermute | solution.py:461
  71.4 8.7 %all-to-all-done.2.in_ref = bf16[16,72,128]{2,1,0:T(8,128)(2,1)S(1)} async-done(((bf16[16,72,128]{2,1,0:T(8,128)(2,1)}), bf16[16,72,128]{2,1,0:T(8,128)(2,1)S(1)}, u32[]{:S(2)}, u32[]{:S(2)}) %all-to-all-start.2) | async-done | bytes 294944 | tf_op jit(solution)/shard_map/all_to_all | solution.py:576
  80.1 3.8 %shard_map.222 = (bf16[16,72,128]{2,1,0:T(8,128)(2,1)}, f32[2,2,96,96]{3,2,1,0:T(8,128)S(1)}) custom-call(bf16[16,72,128]{2,1,0:T(8,128)(2,1)S(1)} %all-to-all-done.2.in_ref, f32[256,256]{1,0:T(8,128)} %copy-done.1, f32[256,256]{1,0:T(8,128)} %copy-done.2, bf16[768,256]{1,0:T(8,128)(2,1)} %get-tuple-element.69.spec_hbm, ...), custom_call_target="tpu_custom_call" | custom-call | flops 1 | bytes 1 | tf_op jit(solution)/shard_map/pallas_call | solution.py:436
  83.9 0.7 collective-permute-start.11
  84.7 4.5 %all-to-all-start.3 = ((bf16[16,72,128]{2,1,0:T(8,128)(2,1)}), bf16[16,72,128]{2,1,0:T(8,128)(2,1)S(1)}, u32[]{:S(2)}, u32[]{:S(2)}) async-start(bf16[16,72,128]{2,1,0:T(8,128)(2,1)} %get-tuple-element.73.refs_13_), calls=%async_computation.3 | async-start | bytes 589824 | tf_op jit(solution)/shard_map/all_to_all | solution.py:583
  89.2 0.4 collective-permute-start.14
  89.6 1.4 %collective-permute-done.11.refs_0_ = bf16[192,768]{1,0:T(8,128)(2,1)S(1)} collective-permute-done((bf16[192,768]{1,0:T(8,128)(2,1)S(1)}, bf16[192,768]{1,0:T(8,128)(2,1)S(1)}, u32[]{:S(2)}, u32[]{:S(2)}) %collective-permute-start.11) | collective-permute-done | bytes 294944 | tf_op jit(solution)/shard_map/ppermute | solution.py:461
  91.0 1.0 collective-permute-start.13
  92.0 1.1 collective-permute-start.12
  93.2 8.3 %shard_map.223 = (f32[2,192,768]{2,1,0:T(8,128)}, f32[2,192,768]{2,1,0:T(8,128)}) custom-call(bf16[192,768]{1,0:T(8,128)(2,1)} %get-tuple-element.57.second_ref.refs_0_, bf16[192,768]{1,0:T(8,128)(2,1)} %collective-permute-done.6.refs_1_, bf16[192,768]{1,0:T(8,128)(2,1)} %collective-permute-done.7.refs_2_, bf16[192,768]{1,0:T(8,128)(2,1)} %copy-done.11, ...), custom_call_target="tpu_custom_call" | custom-call | flops 1 | bytes 1 | tf_op jit(solution)/shard_map/pallas_call | solution.py:436
  101.6 1.8 %collective-permute-done.13.refs_2_ = bf16[192,768]{1,0:T(8,128)(2,1)S(1)} collective-permute-done((bf16[192,768]{1,0:T(8,128)(2,1)S(1)}, bf16[192,768]{1,0:T(8,128)(2,1)S(1)}, u32[]{:S(2)}, u32[]{:S(2)}) %collective-permute-start.13) | collective-permute-done | bytes 294944 | tf_op jit(solution)/shard_map/ppermute | solution.py:461
  103.4 0.7 copy-done.13
  104.1 4.9 %shard_map.224 = (f32[2,192,768]{2,1,0:T(8,128)S(1)}, f32[2,192,768]{2,1,0:T(8,128)S(1)}) custom-call(bf16[192,768]{1,0:T(8,128)(2,1)} %copy-done.12, bf16[192,768]{1,0:T(8,128)(2,1)} %collective-permute-done.12.refs_1_, bf16[192,768]{1,0:T(8,128)(2,1)} %copy-done.13, bf16[192,768]{1,0:T(8,128)(2,1)} %collective-permute-done.4.refs_3_, ...), custom_call_target="tpu_custom_call" | custom-call | flops 1 | bytes 1 | tf_op jit(solution)/shard_map/pallas_call | solution.py:436
  109.1 2.8 %shard_map.225 = bf16[180,768]{1,0:T(8,128)(2,1)} custom-call(bf16[16,72,128]{2,1,0:T(8,128)(2,1)S(1)} %all-to-all-done.3.refs_9_.in_ref, bf16[180,768]{1,0:T(8,128)(2,1)} %bitcast.41, f32[768]{0:T(1024)} %gain_hbm.5, f32[192,768]{1,0:T(8,128)} %get-tuple-element.89.gres_hbm, bf16[2,192,192]{2,1,0:T(8,128)(2,1)} %constant.78.clone.table_hbm), custom_call_target="tpu_custom_call" | custom-call | flops 1 | bytes 1 | tf_op jit(solution)/shard_map/pallas_call | solution.py:436
  112.1 0.4 collective-permute-start.16
  112.5 0.9 shard_map.226
  113.4 5.3 %all-to-all-start.4 = ((bf16[16,48,192]{2,1,0:T(8,128)(2,1)}), bf16[16,48,192]{2,1,0:T(8,128)(2,1)S(1)}, u32[]{:S(2)}, u32[]{:S(2)}) async-start(bf16[16,48,192]{2,1,0:T(8,128)(2,1)} %bitcast.18), calls=%async_computation.4 | async-start | bytes 786432 | tf_op jit(solution)/shard_map/all_to_all | solution.py:631
  118.8 4.1 %fusion.5 = f32[192,768]{1,0:T(8,128)S(1)} fusion(bf16[192,3072]{1,0:T(8,128)(2,1)S(1)} %copy-done.15, bf16[768,3072]{1,0:T(8,128)(2,1)} %down_hbm.1), kind=kOutput, calls=%fused_computation.26 | convolution fusion | flops 905969664 | bytes 6488064 | tf_op jit(solution)/shard_map/dot_general | solution.py:21
  122.9 0.8 fusion.2
  123.7 0.6 slice_bitcast_fusion
  124.3 6.6 %all-to-all-done.4.in_ref = bf16[16,48,192]{2,1,0:T(8,128)(2,1)S(1)} async-done(((bf16[16,48,192]{2,1,0:T(8,128)(2,1)}), bf16[16,48,192]{2,1,0:T(8,128)(2,1)S(1)}, u32[]{:S(2)}, u32[]{:S(2)}) %all-to-all-start.4) | async-done | bytes 294944 | tf_op jit(solution)/shard_map/all_to_all | solution.py:631
  131.0 0.9 bitcast_add_fusion
  131.8 0.9 shard_map.227
  (67 shorter events, 1.2 us)
Async XLA Ops:
  3.5 12.2 %copy-start = (bf16[192,768]{1,0:T(8,128)(2,1)}, bf16[192,768]{1,0:T(8,128)(2,1)S(1)}, u32[]{:S(2)}) copy-start(bf16[192,768]{1,0:T(8,128)(2,1)S(1)} %get-tuple-element.52.cot_hbm.refs_5_) | copy-start | bytes 884740
  3.5 14.6 %collective-permute-start = (bf16[192,768]{1,0:T(8,128)(2,1)S(1)}, bf16[192,768]{1,0:T(8,128)(2,1)S(1)}, u32[]{:S(2)}, u32[]{:S(2)}) collective-permute-start(bf16[192,768]{1,0:T(8,128)(2,1)S(1)} %get-tuple-element.52.cot_hbm.refs_5_), channel_id=1, source_target_pairs={{2,6},{6,10},{10,14},{14,12},{12,8},{8,4},{4,0},{0,2},{7,3},{11,7}... | collective-permute-start | bytes 884744 | tf_op jit(solution)/shard_map/ppermute | solution.py:461
  6.5 11.7 %collective-permute-start.1 = (bf16[192,768]{1,0:T(8,128)(2,1)S(1)}, bf16[192,768]{1,0:T(8,128)(2,1)S(1)}, u32[]{:S(2)}, u32[]{:S(2)}) collective-permute-start(bf16[192,768]{1,0:T(8,128)(2,1)S(1)} %get-tuple-element.52.cot_hbm.refs_5_), channel_id=1, source_target_pairs={{6,2},{10,6},{14,10},{12,14},{8,12},{4,8},{0,4},{2,0},{3,7},{7,11}... | collective-permute-start | bytes 884744 | tf_op jit(solution)/shard_map/ppermute | solution.py:463
  6.6 16.9 %all-to-all-start = ((bf16[16,72,128]{2,1,0:T(8,128)(2,1)}), bf16[16,72,128]{2,1,0:T(8,128)(2,1)S(1)}, u32[]{:S(2)}, u32[]{:S(2)}) async-start(bf16[16,72,128]{2,1,0:T(8,128)(2,1)} %get-tuple-element.51), calls=%async_computation | async-start | bytes 589824 | tf_op jit(solution)/shard_map/all_to_all | solution.py:536
  14.5 11.9 %copy-start.1 = (f32[256,256]{1,0:T(8,128)}, f32[256,256]{1,0:T(8,128)S(1)}, u32[]{:S(2)}) copy-start(f32[256,256]{1,0:T(8,128)S(1)} %maximum_maximum_fusion.w1_ref.w1_hbm) | copy-start | bytes 786436
  16.9 13.7 %copy-start.2 = (f32[256,256]{1,0:T(8,128)}, f32[256,256]{1,0:T(8,128)S(1)}, u32[]{:S(2)}) copy-start(f32[256,256]{1,0:T(8,128)S(1)} %maximum_maximum_fusion.1.w2_ref.w2_hbm) | copy-start | bytes 786436
  18.1 18.5 %copy-start.8 = (bf16[192,768]{1,0:T(8,128)(2,1)}, bf16[192,768]{1,0:T(8,128)(2,1)S(1)}, u32[]{:S(2)}) copy-start(bf16[192,768]{1,0:T(8,128)(2,1)S(1)} %collective-permute-done.refs_6_) | copy-start | bytes 884740
  18.1 18.5 %copy-start.9 = (bf16[192,768]{1,0:T(8,128)(2,1)}, bf16[192,768]{1,0:T(8,128)(2,1)S(1)}, u32[]{:S(2)}) copy-start(bf16[192,768]{1,0:T(8,128)(2,1)S(1)} %collective-permute-done.1.refs_7_) | copy-start | bytes 884740
  23.5 11.3 %collective-permute-start.2 = (bf16[192,768]{1,0:T(8,128)(2,1)S(1)}, bf16[192,768]{1,0:T(8,128)(2,1)}, u32[]{:S(2)}, u32[]{:S(2)}) collective-permute-start(bf16[192,768]{1,0:T(8,128)(2,1)S(1)} %collective-permute-done.refs_6_), channel_id=1, source_target_pairs={{2,6},{6,10},{10,14},{14,12},{12,8},{8,4},{4,0},{0,2},{7,3},{11,7}... | collective-permute-start | bytes 884744 | tf_op jit(solution)/shard_map/ppermute | solution.py:461
  23.5 13.1 %collective-permute-start.3 = (bf16[192,768]{1,0:T(8,128)(2,1)S(1)}, bf16[192,768]{1,0:T(8,128)(2,1)}, u32[]{:S(2)}, u32[]{:S(2)}) collective-permute-start(bf16[192,768]{1,0:T(8,128)(2,1)S(1)} %collective-permute-done.1.refs_7_), channel_id=1, source_target_pairs={{6,2},{10,6},{14,10},{12,14},{8,12},{4,8},{0,4},{2,0},{3,7},{7,11}... | collective-permute-start | bytes 884744 | tf_op jit(solution)/shard_map/ppermute | solution.py:463
  30.6 15.3 %all-to-all-start.1 = ((bf16[16,72,128]{2,1,0:T(8,128)(2,1)}), bf16[16,72,128]{2,1,0:T(8,128)(2,1)}, u32[]{:S(2)}, u32[]{:S(2)}) async-start(bf16[16,72,128]{2,1,0:T(8,128)(2,1)} %get-tuple-element.54), calls=%async_computation.1 | async-start | bytes 589824 | tf_op jit(solution)/shard_map/all_to_all | solution.py:549
  34.8 14.1 %collective-permute-start.4 = (bf16[192,768]{1,0:T(8,128)(2,1)}, bf16[192,768]{1,0:T(8,128)(2,1)}, u32[]{:S(2)}, u32[]{:S(2)}) collective-permute-start(bf16[192,768]{1,0:T(8,128)(2,1)} %collective-permute-done.2.refs_8_), channel_id=1, source_target_pairs={{2,6},{6,10},{10,14},{14,12},{12,8},{8,4},{4,0},{0,2},{7,3},{11,7}... | collective-permute-start | bytes 884744 | tf_op jit(solution)/shard_map/ppermute | solution.py:461
  36.6 12.3 %collective-permute-start.5 = (bf16[192,768]{1,0:T(8,128)(2,1)}, bf16[192,768]{1,0:T(8,128)(2,1)}, u32[]{:S(2)}, u32[]{:S(2)}) collective-permute-start(bf16[192,768]{1,0:T(8,128)(2,1)} %collective-permute-done.3.refs_9_), channel_id=1, source_target_pairs={{6,2},{10,6},{14,10},{12,14},{8,12},{4,8},{0,4},{2,0},{3,7},{7,11}... | collective-permute-start | bytes 884744 | tf_op jit(solution)/shard_map/ppermute | solution.py:463
  48.9 16.6 %collective-permute-start.10 = (bf16[192,768]{1,0:T(8,128)(2,1)}, bf16[192,768]{1,0:T(8,128)(2,1)}, u32[]{:S(2)}, u32[]{:S(2)}) collective-permute-start(bf16[192,768]{1,0:T(8,128)(2,1)} %collective-permute-done.4.refs_3_), channel_id=1, source_target_pairs={{2,6},{6,10},{10,14},{14,12},{12,8},{8,4},{4,0},{0,2},{7,3},{11,7}... | collective-permute-start | bytes 884744 | tf_op jit(solution)/shard_map/ppermute | solution.py:461
  53.9 0.7 copy-start.5
  54.6 14.6 %collective-permute-start.6 = (bf16[192,768]{1,0:T(8,128)(2,1)}, bf16[192,768]{1,0:T(8,128)(2,1)}, u32[]{:S(2)}, u32[]{:S(2)}) collective-permute-start(bf16[192,768]{1,0:T(8,128)(2,1)} %get-tuple-element.57.second_ref.refs_0_), channel_id=1, source_target_pairs={{2,6},{6,10},{10,14},{14,12},{12,8},{8,4},{4,0},{0,2},{7,3},{11,7}... | collective-permute-start | bytes 884744 | tf_op jit(solution)/shard_map/ppermute | solution.py:461
  57.7 11.6 %collective-permute-start.7 = (bf16[192,768]{1,0:T(8,128)(2,1)}, bf16[192,768]{1,0:T(8,128)(2,1)}, u32[]{:S(2)}, u32[]{:S(2)}) collective-permute-start(bf16[192,768]{1,0:T(8,128)(2,1)} %get-tuple-element.57.second_ref.refs_0_), channel_id=1, source_target_pairs={{6,2},{10,6},{14,10},{12,14},{8,12},{4,8},{0,4},{2,0},{3,7},{7,11}... | collective-permute-start | bytes 884744 | tf_op jit(solution)/shard_map/ppermute | solution.py:463
  64.8 0.7 copy-start.7
  65.6 14.6 %all-to-all-start.2 = ((bf16[16,72,128]{2,1,0:T(8,128)(2,1)}), bf16[16,72,128]{2,1,0:T(8,128)(2,1)S(1)}, u32[]{:S(2)}, u32[]{:S(2)}) async-start(bf16[16,72,128]{2,1,0:T(8,128)(2,1)} %copy-done.7), calls=%async_computation.2 | async-start | bytes 589824 | tf_op jit(solution)/shard_map/all_to_all | solution.py:576
  69.3 14.6 %collective-permute-start.8 = (bf16[192,768]{1,0:T(8,128)(2,1)}, bf16[192,768]{1,0:T(8,128)(2,1)S(1)}, u32[]{:S(2)}, u32[]{:S(2)}) collective-permute-start(bf16[192,768]{1,0:T(8,128)(2,1)} %collective-permute-done.6.refs_1_), channel_id=1, source_target_pairs={{2,6},{6,10},{10,14},{14,12},{12,8},{8,4},{4,0},{0,2},{7,3},{11,7}... | collective-permute-start | bytes 884744 | tf_op jit(solution)/shard_map/ppermute | solution.py:461
  71.2 12.7 %collective-permute-start.9 = (bf16[192,768]{1,0:T(8,128)(2,1)}, bf16[192,768]{1,0:T(8,128)(2,1)S(1)}, u32[]{:S(2)}, u32[]{:S(2)}) collective-permute-start(bf16[192,768]{1,0:T(8,128)(2,1)} %collective-permute-done.7.refs_2_), channel_id=1, source_target_pairs={{6,2},{10,6},{14,10},{12,14},{8,12},{4,8},{0,4},{2,0},{3,7},{7,11}... | collective-permute-start | bytes 884744 | tf_op jit(solution)/shard_map/ppermute | solution.py:463
  83.9 9.3 %copy-start.11 = (bf16[192,768]{1,0:T(8,128)(2,1)}, bf16[192,768]{1,0:T(8,128)(2,1)S(1)}, u32[]{:S(2)}) copy-start(bf16[192,768]{1,0:T(8,128)(2,1)S(1)} %collective-permute-done.8.refs_3_) | copy-start | bytes 884740
  83.9 9.3 %copy-start.10 = (bf16[192,768]{1,0:T(8,128)(2,1)}, bf16[192,768]{1,0:T(8,128)(2,1)S(1)}, u32[]{:S(2)}) copy-start(bf16[192,768]{1,0:T(8,128)(2,1)S(1)} %collective-permute-done.9.refs_4_) | copy-start | bytes 884740
  83.9 7.1 %collective-permute-start.11 = (bf16[192,768]{1,0:T(8,128)(2,1)S(1)}, bf16[192,768]{1,0:T(8,128)(2,1)S(1)}, u32[]{:S(2)}, u32[]{:S(2)}) collective-permute-start(bf16[192,768]{1,0:T(8,128)(2,1)S(1)} %collective-permute-done.8.refs_3_), channel_id=1, source_target_pairs={{2,6},{6,10},{10,14},{14,12},{12,8},{8,4},{4,0},{0,2},{7,3},{11,7}... | collective-permute-start | bytes 884744 | tf_op jit(solution)/shard_map/ppermute | solution.py:461
  84.7 16.9 %all-to-all-start.3 = ((bf16[16,72,128]{2,1,0:T(8,128)(2,1)}), bf16[16,72,128]{2,1,0:T(8,128)(2,1)S(1)}, u32[]{:S(2)}, u32[]{:S(2)}) async-start(bf16[16,72,128]{2,1,0:T(8,128)(2,1)} %get-tuple-element.73.refs_13_), calls=%async_computation.3 | async-start | bytes 589824 | tf_op jit(solution)/shard_map/all_to_all | solution.py:583
  89.2 12.3 %collective-permute-start.14 = (f32[2,2,48,96]{3,2,1,0:T(8,128)S(1)}, f32[2,2,48,96]{3,2,1,0:T(8,128)S(1)}, u32[]{:S(2)}, u32[]{:S(2)}) collective-permute-start(f32[2,2,48,96]{3,2,1,0:T(8,128)S(1)} %dynamic-slice_bitcast_fusion.3), channel_id=1, source_target_pairs={{0,1},{1,0},{2,3},{3,2},{4,5},{5,4},{6,7},{7,6},{8,9},{9,8},{10,11... | collective-permute-start | bytes 221192 | tf_op jit(solution)/shard_map/ppermute | solution.py:593
  91.0 10.5 %copy-start.12 = (bf16[192,768]{1,0:T(8,128)(2,1)}, bf16[192,768]{1,0:T(8,128)(2,1)S(1)}, u32[]{:S(2)}) copy-start(bf16[192,768]{1,0:T(8,128)(2,1)S(1)} %collective-permute-done.11.refs_0_) | copy-start | bytes 884740
  91.0 12.3 %collective-permute-start.13 = (bf16[192,768]{1,0:T(8,128)(2,1)S(1)}, bf16[192,768]{1,0:T(8,128)(2,1)S(1)}, u32[]{:S(2)}, u32[]{:S(2)}) collective-permute-start(bf16[192,768]{1,0:T(8,128)(2,1)S(1)} %collective-permute-done.11.refs_0_), channel_id=1, source_target_pairs={{2,6},{6,10},{10,14},{14,12},{12,8},{8,4},{4,0},{0,2},{7,3},{11,7}... | collective-permute-start | bytes 884744 | tf_op jit(solution)/shard_map/ppermute | solution.py:461
  92.0 11.4 %collective-permute-start.12 = (bf16[192,768]{1,0:T(8,128)(2,1)S(1)}, bf16[192,768]{1,0:T(8,128)(2,1)}, u32[]{:S(2)}, u32[]{:S(2)}) collective-permute-start(bf16[192,768]{1,0:T(8,128)(2,1)S(1)} %collective-permute-done.9.refs_4_), channel_id=1, source_target_pairs={{6,2},{10,6},{14,10},{12,14},{8,12},{4,8},{0,4},{2,0},{3,7},{7,11}... | collective-permute-start | bytes 884744 | tf_op jit(solution)/shard_map/ppermute | solution.py:463
  103.4 0.7 copy-start.13
  109.0 3.0 %copy-start.3 = (f32[2,192,768]{2,1,0:T(8,128)}, f32[2,192,768]{2,1,0:T(8,128)S(1)}, u32[]{:S(2)}) copy-start(f32[2,192,768]{2,1,0:T(8,128)S(1)} %get-tuple-element.91) | copy-start | bytes 3538948
  109.1 3.4 %collective-permute-start.15 = (f32[192,768]{1,0:T(8,128)S(1)}, f32[192,768]{1,0:T(8,128)S(1)}, u32[]{:S(2)}, u32[]{:S(2)}) collective-permute-start(f32[192,768]{1,0:T(8,128)S(1)} %get-tuple-element.96), channel_id=1, source_target_pairs={{0,1},{1,0},{2,3},{3,2},{4,5},{5,4},{6,7},{7,6},{8,9},{9,8},{10,11... | collective-permute-start | bytes 1769480 | tf_op jit(solution)/shard_map/ppermute | solution.py:622
  112.1 6.7 %copy-start.15 = (bf16[192,3072]{1,0:T(8,128)(2,1)S(1)}, bf16[192,3072]{1,0:T(8,128)(2,1)}, u32[]{:S(2)}) copy-start(bf16[192,3072]{1,0:T(8,128)(2,1)} %get-tuple-element.63) | copy-start | bytes 3538948
  112.1 12.3 %collective-permute-start.16 = (f32[192,768]{1,0:T(8,128)S(1)}, f32[192,768]{1,0:T(8,128)S(1)}, u32[]{:S(2)}, u32[]{:S(2)}) collective-permute-start(f32[192,768]{1,0:T(8,128)S(1)} %dynamic-slice_bitcast_fusion), channel_id=1, source_target_pairs={{0,1},{1,0},{2,3},{3,2},{4,5},{5,4},{6,7},{7,6},{8,9},{9,8},{10,11... | collective-permute-start | bytes 1769480 | tf_op jit(solution)/shard_map/ppermute | solution.py:622
  113.4 17.5 %all-to-all-start.4 = ((bf16[16,48,192]{2,1,0:T(8,128)(2,1)}), bf16[16,48,192]{2,1,0:T(8,128)(2,1)S(1)}, u32[]{:S(2)}, u32[]{:S(2)}) async-start(bf16[16,48,192]{2,1,0:T(8,128)(2,1)} %bitcast.18), calls=%async_computation.4 | async-start | bytes 786432 | tf_op jit(solution)/shard_map/all_to_all | solution.py:631
  118.8 4.1 %copy-start.6 = (bf16[192,768]{1,0:T(8,128)(2,1)S(1)}, bf16[192,768]{1,0:T(8,128)(2,1)}, u32[]{:S(2)}) copy-start(bf16[192,768]{1,0:T(8,128)(2,1)} %copy-done.5) | copy-start | bytes 884740
  118.8 4.1 %copy-start.14 = (f32[768]{0:T(1024)S(1)}, f32[768]{0:T(1024)}, u32[]{:S(2)}) copy-start(f32[768]{0:T(1024)} %param.31) | copy-start | bytes 9220
  122.9 8.1 %copy-start.4 = (f32[2,192,768]{2,1,0:T(8,128)S(1)}, f32[2,192,768]{2,1,0:T(8,128)}, u32[]{:S(2)}) copy-start(f32[2,192,768]{2,1,0:T(8,128)} %copy-done.3) | copy-start | bytes 3538948
